TPU v7x, 512 devices: a whole 4x4x16 slice. The times are simulated.
512 devices in a mesh: worker: 16 (over x, y_hi, core), fsdp: 32 (over y_lo, z).
Axes of the slice: x: 4, y: 4 (y_hi: 2, y_lo: 2; y = y_hi * 2 + y_lo), z: 16, core: 2. Of those that a mesh axis runs over, the one named last changes fastest.
Arguments:
- inputs: bfloat16 [16, 2, 4096, 8192], P('worker', None, 'fsdp'), may hold values from -6 to 6
- targets: bfloat16 [16, 2, 4096, 512], P('worker', None, 'fsdp'), may hold values from -6 to 6
- base: float32 [8192, 512], P('fsdp', 'worker'), may hold values from -6 to 6
- adapter_a: float32 [16, 64, 8192], P('worker', None, 'fsdp'), may hold values from -6 to 6
- adapter_b: float32 [16, 512, 64], P('worker'), may hold values from -3 to 3
Outputs:
- new_base: float32 [8192, 512], P('fsdp', 'worker')
- final_a: float32 [16, 64, 8192], P('worker', None, 'fsdp')
- final_b: float32 [16, 512, 64], P('worker')
All inputs are finite; a program needn't handle non-finite values.
Results may differ from a plain program's by a relative error of at most 0.0048.
Values may be sent and summed in bfloat16 or wider, within the bound.
No kernel may reach another device: no remote copies, remote signals or barrier semaphores. Data moves between devices by JAX's collectives and lax.ppermute only.
A program may use at most 64 MiB of HBM per device.

v0:
```python
import jax
import jax.numpy as jnp
from jax import lax
from jax.sharding import Mesh
from jax.sharding import PartitionSpec as P

FSDP = ("fsdp_0", "fsdp_1")


branch_scale = 0.25
rate_down = 200.0
rate_up = 20.0


def joined_along(parts, dim):
    parts = jnp.moveaxis(parts, 0, dim)
    dims = parts.shape
    return parts.reshape(*dims[:dim], dims[dim] * dims[dim + 1], *dims[dim + 2 :])


def copy_for_each(value, axis):
    copies = jnp.broadcast_to(value, (lax.axis_size(axis), *value.shape))
    return lax.all_to_all(copies, axis, split_axis=0, concat_axis=0, tiled=True)


def gather_directly(value, axis, dim):
    return joined_along(copy_for_each(value, axis), dim)


def cut_along(value, dim, count):
    before, after = (value.shape[:dim], value.shape[dim + 1 :])
    return jnp.moveaxis(value.reshape(*before, count, -1, *after), dim, 0)


def sent_and_summed(value, axis, dim):
    count = lax.axis_size(axis)
    parts = lax.all_to_all(cut_along(value, dim, count), axis, 0, 0, tiled=True)
    return jnp.sum(parts, axis=0)


def padded_to(lines, count):
    spare = -len(lines) % count
    return jnp.pad(lines, [(0, spare)] + [(0, 0)] * (lines.ndim - 1))


def sum_by_parts(value, axes):
    own = sent_and_summed(padded_to(value, lax.axis_size(axes)), axes, 0)
    whole = gather_directly(own, axes, 0)
    return whole[: len(value)].reshape(value.shape)


def in_one(arrays, axis):
    ravelled, at, done = (jnp.concatenate([a.reshape(-1) for a in arrays]), 0, [])
    total = sum_by_parts(ravelled, axis)
    for a in arrays:
        done.append(total[at : at + a.size].reshape(a.shape))
        at += a.size
    return tuple(done)


def total_of(value, axes):
    lines = value.reshape(-1, value.shape[-1])
    padded = padded_to(lines, lax.axis_size(axes))
    whole = gather_directly(sent_and_summed(padded, axes, 0), axes, 0)
    return lax.slice_in_dim(whole, 0, len(lines)).reshape(value.shape)


def sum_in_order(parts, axes, order):
    inside = parts.shape[1:]
    parts = parts.reshape(*(lax.axis_size(a) for a in axes), *inside)
    parts = jnp.moveaxis(parts, order, range(len(axes))).reshape(-1, *inside)
    for k in order:
        parts = lax.psum_scatter(parts, axes[k], scatter_dimension=0, tiled=True)
    return parts[0]


def scatter_axes(value, axes, order, dim):
    count = lax.axis_size(axes)
    return sum_in_order(cut_along(value, dim, count), axes, order)


def local(inputs, targets, base, adapter_a, adapter_b):
    high = lax.Precision.HIGHEST
    tokens = inputs[0]
    wanted = targets[0].astype(jnp.float32)
    a_start = adapter_a[0]
    b_start = adapter_b[0]
    steps, rows, width = tokens.shape
    features = b_start.shape[0]
    scale = width ** (-0.5)
    total_rows = float(rows * lax.axis_size(FSDP))
    flat = tokens.reshape(steps * rows, width)
    base_half = base.astype(jnp.bfloat16)
    column = gather_directly(base_half, FSDP, 0)
    keys_flat = jnp.dot(
        flat,
        lax.all_gather(column, "worker", axis=1, tiled=True),
        preferred_element_type=jnp.float32,
    )
    keys_base = (keys_flat * scale).reshape(steps, rows, features)
    shard = a_start.shape[1]
    offset = lax.axis_index(FSDP) * shard
    adapter = a_start
    upper = b_start
    exact = lax.all_gather(a_start, FSDP, axis=1, tiled=True)
    a_half = exact.astype(jnp.bfloat16)
    for step in range(steps):
        current = tokens[step]
        low = jnp.einsum("td,rd->tr", current, a_half, preferred_element_type=jnp.float32) * scale
        output = keys_base[step] + branch_scale * jnp.dot(low, upper.T, precision=high)
        error = (output - wanted[step]) / total_rows
        b_part = branch_scale * jnp.dot(error.T, low, precision=high)
        back = (branch_scale * jnp.dot(error, upper, precision=high)).astype(jnp.bfloat16)
        a_part = jnp.dot(back.T, current, preferred_element_type=jnp.float32) * scale
        if step + 1 < steps:
            grad_b, grad_whole = in_one((b_part, a_part), FSDP)
            exact = exact - rate_down * grad_whole
            adapter = lax.dynamic_slice_in_dim(exact, offset, shard, 1)
            a_half = exact.astype(jnp.bfloat16)
        else:
            grad_b = total_of(b_part, FSDP)
            adapter = adapter - rate_down * scatter_axes(a_part, FSDP, (1, 0), 1)
        upper = upper - rate_up * grad_b
    change = branch_scale * (
        jnp.dot(adapter.T, upper.T, precision=high) - jnp.dot(a_start.T, b_start.T, precision=high)
    )
    merged = total_of(change, "worker")
    columns = base.shape[1]
    own_part = lax.dynamic_slice_in_dim(merged, lax.axis_index("worker") * columns, columns, 1)
    new_base = base + own_part / lax.axis_size("worker")
    return (new_base, adapter[None], upper[None])


def solution(mesh):
    finer = Mesh(mesh.devices.reshape(mesh.shape["worker"], 2, 16), ("worker", "fsdp_0", "fsdp_1"))
    return jax.shard_map(
        local,
        mesh=finer,
        in_specs=(
            P("worker", None, FSDP, None),
            P("worker", None, FSDP, None),
            P(FSDP, "worker"),
            P("worker", None, FSDP),
            P("worker", None, None),
        ),
        out_specs=(P(FSDP, "worker"), P("worker", None, FSDP), P("worker", None, None)),
        check_vma=False,
    )
```

profile of v0, /device:TPU:1, one launch (start us, length us, event | category | flops | bytes accessed | tf_op | source)
XLA Modules:
  0.0 637.4 jit_solution(12427288971075808958)
XLA Ops:
  7.2 0.7 all-gather.6.cloned.1.call-update
  8.0 0.8 convert_element_type.19
  8.7 0.1 broadcast_in_dim.18
  8.8 51.1 %all_to_all.40 = bf16[32,256,32]{1,2,0:T(8,128)(2,1)S(1)} all-to-all(bf16[32,256,32]{1,2,0:T(8,128)(2,1)S(1)} %broadcast_in_dim.18), channel_id=1, replica_groups=mesh['worker'=16,'fsdp_0'=2,'fsdp_1'=16] {'fsdp_0','fsdp_1'}, dimensions={0} | all-to-all | bytes 1048576 | tf_op jit(solution)/shard_map/all_to_all | solution.py:23
  59.9 0.8 copy.51
  60.8 0.1 convert_element_type.21
  60.8 72.5 %all-gather.6.cloned.1.call-done = f32[1,64,8192]{2,1,0:T(8,128)} async-done(((f32[1,64,256]{2,1,0:T(8,128)}), f32[1,64,8192]{2,1,0:T(8,128)}) %all-gather.6.cloned.1.call-update) | async-done | bytes 2097168 | tf_op jit(solution)/shard_map/all_gather | solution.py:105
  133.3 3.1 fusion.21
  136.4 101.3 %all-gather.4.cloned.1.call-done = bf16[8192,512]{0,1:T(8,128)(2,1)} async-done(((bf16[8192,32]{0,1:T(8,128)(2,1)}), bf16[8192,512]{0,1:T(8,128)(2,1)}) %all-gather.4.cloned.1.call-update) | async-done | bytes 8388624 | tf_op jit(solution)/shard_map/all_gather | solution.py:97
  237.7 7.0 %convolution_multiply_fusion.2 = f32[256,512]{1,0:T(8,128)S(1)} fusion(bf16[256,8192]{1,0:T(8,128)(2,1)} %bitcast.97, bf16[8192,512]{0,1:T(8,128)(2,1)} %all-gather.4.cloned.1.call-done), kind=kOutput, calls=%fused_computation.19 | convolution fusion | flops 2147614720 | bytes 13107200 | tf_op jit(solution)/shard_map/dot_general | solution.py:95
  244.8 0.4 fusion.19
  245.2 0.3 convolution_multiply_fusion.6
  245.5 0.0 copy-done.2
  245.6 0.4 fusion.27
  246.0 0.1 copy.43
  246.1 0.1 reshape.69
  246.2 2.1 fusion.11
  248.3 0.4 copy.52
  248.7 0.1 pad_maximum_fusion
  248.8 117.5 %all_to_all.41 = f32[32,1,17408]{2,1,0:T(1,128)S(1)} all-to-all(f32[32,1,17408]{2,1,0:T(1,128)S(1)} %bitcast.98), channel_id=1, replica_groups=mesh['worker'=16,'fsdp_0'=2,'fsdp_1'=16] {'fsdp_0','fsdp_1'}, dimensions={0} | all-to-all | bytes 4456448 | tf_op jit(solution)/shard_map/all_to_all | solution.py:37
  366.3 1.3 reduce_sum.27
  367.6 2.5 broadcast_in_dim.19
  370.1 4.8 all-to-all-start.2
  374.9 0.2 reduce-scatter.3.cloned.1.call-start
  375.1 0.1 copy.42
  375.3 96.7 %all-to-all-done.2 = f32[32,1,17408]{2,1,0:T(1,128)} async-done(((f32[32,1,17408]{2,1,0:T(1,128)}), f32[32,1,17408]{2,1,0:T(1,128)}, u32[]{:S(2)}, u32[]{:S(2)}) %all-to-all-start.2) | async-done | bytes 2228256 | tf_op jit(solution)/shard_map/all_to_all | solution.py:23
  471.9 6.9 %reduce.1 = f32[32,17408]{1,0:T(8,128)S(1)} reduce(f32[32,1,17408]{2,1,0:T(1,128)} %all-to-all-done.2, f32[]{:T(128)} %constant.52), dimensions={1}, to_apply=%all_to_all.28.reduce_sub_computation | reduce | bytes 4456452 | tf_op jit(solution)/shard_map/all_to_all | solution.py:23
  478.8 1.9 slice.39
  480.8 2.6 slice.43
  483.4 2.7 fusion
  486.1 0.8 copy-done
  486.9 0.9 fusion.24
  487.8 0.2 copy-done.3
  488.0 1.4 fusion.20
  489.4 1.5 fusion.28
  490.9 0.5 convolution_multiply_fusion
  491.4 0.6 copy.53
  492.1 2.6 copy.45
  494.7 0.3 convolution_multiply_fusion.5
  495.0 0.1 copy.46
  495.1 0.2 reshape.80
  495.3 26.9 %all_to_all.42 = f32[32,1,1024]{2,1,0:T(1,128)S(1)} all-to-all(f32[32,1,1024]{2,1,0:T(1,128)S(1)} %reshape.80), channel_id=1, replica_groups=mesh['worker'=16,'fsdp_0'=2,'fsdp_1'=16] {'fsdp_0','fsdp_1'}, dimensions={0} | all-to-all | bytes 262144 | tf_op jit(solution)/shard_map/all_to_all | solution.py:37
  522.2 0.5 broadcast.66
  522.7 1.0 reduce.3
  523.6 0.1 reshape.81
  523.8 0.8 reshape.82
  524.7 4.5 all-to-all-start.4
  529.2 15.5 %all-to-all-done.4 = f32[32,1,1024]{2,1,0:T(1,128)S(1)} async-done(((f32[32,1,1024]{2,1,0:T(1,128)}), f32[32,1,1024]{2,1,0:T(1,128)S(1)}, u32[]{:S(2)}, u32[]{:S(2)}) %all-to-all-start.4) | async-done | bytes 131104 | tf_op jit(solution)/shard_map/all_to_all | solution.py:23
  544.7 1.0 reduce.4
  545.7 0.1 reshape.83
  545.8 16.8 %reduce-scatter.3.cloned.1.call-done = f32[2,64,256]{2,1,0:T(8,128)} async-done(((f32[32,64,256]{2,1,0:T(8,128)}), f32[2,64,256]{2,1,0:T(8,128)}) %reduce-scatter.3.cloned.1.call-update) | async-done | bytes 131088 | tf_op jit(solution)/shard_map/reduce_scatter | solution.py:73
  562.7 1.0 bitcast_subtract_fusion
  563.7 29.1 %reduce-scatter.5.cloned.1.call-done = f32[1,64,256]{2,1,0:T(8,128)} async-done(((f32[2,64,256]{2,1,0:T(8,128)}), f32[1,64,256]{2,1,0:T(8,128)}) %reduce-scatter.5.cloned.1.call-update) | async-done | bytes 65552 | tf_op jit(solution)/shard_map/reduce_scatter | solution.py:73
  592.7 1.5 fusion.36
  594.2 0.6 fusion.14
  594.9 18.4 %all_to_all.43 = f32[16,16,512]{2,1,0:T(8,128)S(1)} all-to-all(f32[16,16,512]{2,1,0:T(8,128)S(1)} %bitcast.106), channel_id=1, replica_groups=mesh['worker'=16,'fsdp_0'=2,'fsdp_1'=16] {'worker'}, dimensions={0} | all-to-all | bytes 1048576 | tf_op jit(solution)/shard_map/all_to_all | solution.py:37
  613.4 0.9 broadcast_in_dim.21
  614.2 4.6 all-to-all-start.6
  618.8 0.1 copy.47
  618.9 0.8 copy.49
  619.7 0.6 fusion.35
  620.3 9.7 %all-to-all-done.6 = f32[16,16,512]{2,1,0:T(8,128)S(1)} async-done(((f32[16,16,512]{2,1,0:T(8,128)}), f32[16,16,512]{2,1,0:T(8,128)S(1)}, u32[]{:S(2)}, u32[]{:S(2)}) %all-to-all-start.6) | async-done | bytes 524320 | tf_op jit(solution)/shard_map/all_to_all | solution.py:23
  630.1 0.1 multiply_add_fusion
  630.2 0.7 copy.48
  (23 shorter events, 0.3 us)
Async XLA Ops:
  7.2 53.6 %copy-start.4 = (bf16[1,2,128,512]{3,2,1,0:T(8,128)(2,1)S(1)}, bf16[1,2,128,512]{3,2,1,0:T(8,128)(2,1)}, u32[]{:S(2)}) copy-start(bf16[1,2,128,512]{3,2,1,0:T(8,128)(2,1)} %param.6) | copy-start | bytes 786436
  7.2 126.1 %all-gather.6.cloned.1.call-start = ((), (), s32[]{:S(2)}) async-start(), calls=%async_computation.12 | async-start | bytes 2162688 | tf_op jit(solution)/shard_map/all_gather | solution.py:105
  7.9 229.8 %all-gather.4.cloned.1.call-start = ((), (), s32[]{:S(2)}) async-start(), calls=%async_computation.9 | async-start | bytes 8912896 | tf_op jit(solution)/shard_map/all_gather | solution.py:97
  237.7 7.1 %copy-start.1 = (f32[1,512,64]{1,2,0:T(8,128)S(1)}, f32[1,512,64]{1,2,0:T(8,128)}, u32[]{:S(2)}) copy-start(f32[1,512,64]{1,2,0:T(8,128)} %param.9) | copy-start | bytes 393220
  244.7 0.8 copy-start.2
  370.1 101.8 %all-to-all-start.2 = ((f32[32,1,17408]{2,1,0:T(1,128)}), f32[32,1,17408]{2,1,0:T(1,128)}, u32[]{:S(2)}, u32[]{:S(2)}) async-start(f32[32,1,17408]{2,1,0:T(1,128)} %broadcast_in_dim.19), calls=%async_computation.2 | async-start | bytes 4456448 | tf_op jit(solution)/shard_map/all_to_all | solution.py:23
  374.9 187.7 %reduce-scatter.3.cloned.1.call-start = ((), (), s32[]{:S(2)}) async-start(), calls=%async_computation.10 | async-start | bytes 2228224 | tf_op jit(solution)/shard_map/reduce_scatter | solution.py:73
  483.4 3.5 copy-start
  486.9 1.0 copy-start.3
  523.8 70.4 %copy-start.6 = (f32[1,64,256]{2,1,0:T(8,128)S(1)}, f32[1,64,256]{2,1,0:T(8,128)}, u32[]{:S(2)}) copy-start(f32[1,64,256]{2,1,0:T(8,128)} %param.8) | copy-start | bytes 196612
  524.7 20.1 %all-to-all-start.4 = ((f32[32,1,1024]{2,1,0:T(1,128)}), f32[32,1,1024]{2,1,0:T(1,128)S(1)}, u32[]{:S(2)}, u32[]{:S(2)}) async-start(f32[32,1,1024]{2,1,0:T(1,128)} %reshape.82), calls=%async_computation.6 | async-start | bytes 262144 | tf_op jit(solution)/shard_map/all_to_all | solution.py:23
  529.2 63.6 %reduce-scatter.5.cloned.1.call-start = ((), (), s32[]{:S(2)}) async-start(), calls=%async_computation.11 | async-start | bytes 196608 | tf_op jit(solution)/shard_map/reduce_scatter | solution.py:73
  594.2 24.6 %copy-start.7 = (f32[256,32]{0,1:T(8,128)S(1)}, f32[256,32]{0,1:T(8,128)}, u32[]{:S(2)}) copy-start(f32[256,32]{0,1:T(8,128)} %param.7) | copy-start | bytes 98308
  594.9 24.8 %copy-start.5 = (f32[1,64,256]{2,1,0:T(8,128)S(1)}, f32[1,64,256]{2,1,0:T(8,128)}, u32[]{:S(2)}) copy-start(f32[1,64,256]{2,1,0:T(8,128)} %reduce-scatter.5.cloned.1.call-done) | copy-start | bytes 196612
  614.2 15.8 %all-to-all-start.6 = ((f32[16,16,512]{2,1,0:T(8,128)}), f32[16,16,512]{2,1,0:T(8,128)S(1)}, u32[]{:S(2)}, u32[]{:S(2)}) async-start(f32[16,16,512]{2,1,0:T(8,128)} %broadcast_in_dim.21), calls=%async_computation.8 | async-start | bytes 1048576 | tf_op jit(solution)/shard_map/all_to_all | solution.py:23
Sparse Core Ops, SparseCore 0:
  10.1 123.1 all-gather.5
  136.6 101.0 all-gather.3
  494.8 67.7 reduce-scatter.2
  565.2 27.4 reduce-scatter.4
where the time goes:
time: 638 us; the launch traced here: 637 us
  waiting for transfers between devices  342 us (54%)
  blocking collectives  214 us (34%)
  matrix products  20 us (3%)
  local copies, waits for them, and re-layouts  17.3 us (3%)
  other arithmetic  15.6 us (2%)
  starting transfers between devices  14.2 us (2%)
  between operations  14.1 us (2%)
    all_to_all x3, blocking collectives, sent_and_summed(): parts = lax.all_to_all(cut_along(value, dim, count), axis, 0, 0, tiled=True)  163 us
    all_to_all x3, waiting for transfers between devices, copy_for_each(): return lax.all_to_all(copies, axis, split_axis=0, concat_axis=0, tiled=True)  122 us
    all_gather x1, waiting for transfers between devices, local(): lax.all_gather(column, 'worker', axis=1, tiled=True)  101 us
    all_gather x1, waiting for transfers between devices, local(): exact = lax.all_gather(a_start, FSDP, axis=1, tiled=True)  72.5 us
    all_to_all x1, blocking collectives, copy_for_each(): return lax.all_to_all(copies, axis, split_axis=0, concat_axis=0, tiled=True)  51.1 us
    reduce_scatter x2, waiting for transfers between devices, sum_in_order(): parts = lax.psum_scatter(parts, axes[k], scatter_dimension=0, tiled=True)  45.9 us
    all_to_all x3, starting transfers between devices, copy_for_each(): return lax.all_to_all(copies, axis, split_axis=0, concat_axis=0, tiled=True)  13.9 us
  transfers between devices with their start and end apart: 7, of which 7 were waited for; matrix products, arithmetic and copies ran while one was open for 2% of the time, Pallas kernels for 0%

commit v1 on v0

v1 whole, which is shorter than its diff:
```python
import jax
import jax.numpy as jnp
from jax import lax
from jax.experimental import pallas as pl
from jax.experimental.pallas import tpu as pltpu
from jax.sharding import Mesh
from jax.sharding import PartitionSpec as P

W = ("x", "yh", "c")
F = ("yl", "z")
NZ = 16

branch_scale = 0.25
rate_down = 200.0
rate_up = 20.0

bf16 = jnp.bfloat16
f32 = jnp.float32
HIGH = lax.Precision.HIGHEST
VMEM = pltpu.CompilerParams(vmem_limit_bytes=60 * 1024 * 1024)


def dot(a, b, ca, cb, precision=None):
    return lax.dot_general(a, b, (((ca,), (cb,)), ((), ())), precision=precision, preferred_element_type=f32)


def split(value):
    hi = value.astype(bf16)
    return hi, (value - hi.astype(f32)).astype(bf16)


def vmem(n):
    return [pl.BlockSpec(memory_space=pltpu.VMEM)] * n


def hbm(n):
    return [pl.BlockSpec(memory_space=pl.ANY)] * n


def smem():
    return pl.BlockSpec(memory_space=pltpu.SMEM)


def keys_kernel(idx, x_ref, xr0, xr1, y_ref, a_ref, *rest):
    pieces = rest[:8]
    sent_ref, later_ref, xs, bs, xsem, bsem = rest[8:]
    half = xs.shape[-1]
    scale = (2 * half) ** (-0.5)
    px, pyh, pc, pyl = idx[0], idx[1], idx[2], idx[3]
    rows = xs.shape[2]
    copies = []
    for j in range(2):
        copies.append(pltpu.make_async_copy(x_ref.at[j, :, pl.ds(pyl * half, half)], xs.at[j, pyl], xsem.at[j]))
    for j, got in enumerate((xr0, xr1)):
        copies.append(pltpu.make_async_copy(got, xs.at[j, 1 - pyl], xsem.at[2 + j]))
    for k, piece in enumerate(pieces):
        dc, dx = divmod(k, 4)
        for dy in range(2):
            w = lax.rem(px + 4 - dx, 4) * 4 + lax.rem(pyh + dy, 2) * 2 + lax.rem(pc + dc, 2)
            copies.append(pltpu.make_async_copy(piece.at[dy], bs.at[w], bsem.at[k * 2 + dy]))
    for copy in copies:
        copy.start()
    for copy in copies:
        copy.wait()
    cols = bs.shape[0] * bs.shape[1]
    tokens = xs[...].reshape(4 * rows, half)

    low = jnp.zeros((a_ref.shape[1], 2 * rows), f32)
    for z in range(NZ):
        n = a_ref.shape[2]
        low = low + dot(a_ref[z], tokens[: 2 * rows, z * n : (z + 1) * n], 1, 1)
    hi, lo = split(low * scale)
    sent_ref[2 * rows :, : 2 * rows] = hi
    sent_ref[2 * rows :, 2 * rows :] = lo

    def some(n, carry):
        block = bs[pl.ds(n * 4, 4)].reshape(128, half)
        part = dot(tokens, block, 1, 1) * scale
        for q in range(4):
            mine = (q % 2) == pyl
            wanted = jnp.where(mine, y_ref[q // 2, :, pl.ds(n * 128, 128)].astype(f32), 0.0)
            value = part[q * rows : (q + 1) * rows] - wanted
            if q < 2:
                sent_ref[q * rows : (q + 1) * rows, pl.ds(n * 128, 128)] = value.astype(bf16)
            else:
                later_ref[(q - 2) * rows : (q - 1) * rows, pl.ds(n * 128, 128)] = value
        return carry

    lax.fori_loop(0, cols // 128, some, 0)


def joined(blocks):
    return jnp.concatenate(
        [jnp.concatenate([blocks[2 * g], blocks[2 * g + 1]], axis=1) for g in range(NZ // 2)], axis=0
    )


def gradients(pyl, low, keys, up, xo, xr, out, total_rows):
    rows = xo.shape[0]
    output = keys + branch_scale * dot(low, up, 0, 0, HIGH)
    error = output / total_rows
    up_grad = branch_scale * dot(low, error, 1, 0, HIGH)
    back = (branch_scale * dot(up, error, 1, 1, HIGH)).astype(bf16)
    first, second = back[:, :rows], back[:, rows:]
    own = jnp.where(pyl == 0, first, second)
    other = jnp.where(pyl == 0, second, first)
    hi, lo = split(up_grad)
    n = xo.shape[1] // NZ
    for z in range(NZ):
        at = slice(z * n, (z + 1) * n)
        out[z, :64] = (dot(own, xo[:, at], 1, 0) + dot(other, xr[:, at], 1, 0)).astype(bf16)
        g, h = z // 2, z % 2
        out[z, 64:72] = hi[8 * g : 8 * g + 8, 256 * h : 256 * h + 256]
        out[z, 72:80] = lo[8 * g : 8 * g + 8, 256 * h : 256 * h + 256]


def first_kernel(total_rows, idx, own, got, blocks, xo, xr, out):
    rows = 2 * xo.shape[1]
    keys = own[:rows].astype(f32) + got[:rows].astype(f32)
    a, b = own[rows:].astype(f32), got[rows:].astype(f32)
    low = (a[:, :rows] + a[:, rows:]) + (b[:, :rows] + b[:, rows:])
    gradients(idx[3], low, keys, joined(blocks[...]), xo[0], xr[...], out, total_rows)


def low_kernel(idx, whole, xo, xr, out):
    n = whole.shape[2]
    rows = xo.shape[1]
    scale = (2 * xo.shape[2]) ** (-0.5)
    own = jnp.zeros((64, rows), f32)
    other = jnp.zeros((64, rows), f32)
    for z in range(NZ):
        own = own + dot(whole[z, :64], xo[0, :, z * n : (z + 1) * n], 1, 1)
        other = other + dot(whole[z, :64], xr[:, z * n : (z + 1) * n], 1, 1)
    first = idx[3] == 0
    out[:, :rows] = jnp.where(first, own, other) * scale
    out[:, rows:] = jnp.where(first, other, own) * scale


def second_kernel(total_rows, idx, own, got, low_own, low_got, whole, xo, xr, out):
    blocks = whole[:, 64:72].astype(f32) + whole[:, 72:80].astype(f32)
    gradients(
        idx[3], low_own[...] + low_got[...], own[...] + got[...], joined(blocks), xo[0], xr[...], out, total_rows
    )


def summed(parts):
    down = jnp.zeros((64, 256), f32)
    up = jnp.zeros((8, 256), f32)
    for z in range(NZ):
        down = down + parts[z, :64].astype(f32)
        up = up + (parts[z, 64:72].astype(f32) + parts[z, 72:80].astype(f32))
    return down, up


def update_kernel(scale, idx, parts, a_ref, blocks, a_out, b_out, copies):
    down, up = summed(parts)
    a = a_ref[...] - (rate_down * scale) * down
    b = blocks[idx[4]] - rate_up * up
    a_out[...] = a
    a_half = a.astype(bf16)
    hi, lo = split(b)
    b_out[...] = hi.astype(f32) + lo.astype(f32)
    for z in range(NZ):
        copies[z, :64] = a_half
        copies[z, 64:72] = hi
        copies[z, 72:80] = lo


def last_update_kernel(scale, parts, a_ref, b_ref, a_out, copies):
    down, up = summed(parts)
    a_out[...] = a_ref[...] - (rate_down * scale) * down
    b = b_ref[...] - rate_up * up
    for z in range(NZ):
        copies[z] = b


def change_kernel(a_ref, blocks, a_start, blocks_start, out, b_out):
    up = joined(blocks[...])
    left = jnp.concatenate([up, -joined(blocks_start[...])], axis=0)
    right = jnp.concatenate([a_ref[...], a_start[...]], axis=0)
    out[...] = branch_scale * dot(left, right, 0, 0, HIGH)
    b_out[...] = up.T


def merge_kernel(parts, base, out):
    total = parts[0]
    for w in range(1, parts.shape[0]):
        total = total + parts[w]
    out[...] = base[...] + (total * (1.0 / parts.shape[0])).T


def call(kernel, shapes, specs, *args, scratch=()):
    return pl.pallas_call(
        kernel,
        out_shape=shapes,
        in_specs=specs,
        scratch_shapes=scratch,
        compiler_params=VMEM,
    )(*args)


def shaped(dims, kind):
    return jax.ShapeDtypeStruct(dims, kind)


def own_half_spec(step, rows, half):
    return pl.BlockSpec((1, rows, half), lambda idx: (step, 0, idx[3]))


def with_tokens(kernel, step, idx, shape, inputs, args):
    tokens, got = inputs
    rows, half = got.shape
    return pl.pallas_call(
        kernel,
        out_shape=shape,
        grid_spec=pltpu.PrefetchScalarGridSpec(
            num_scalar_prefetch=1,
            grid=(1,),
            in_specs=[pl.BlockSpec(a.shape, lambda i, s, n=a.ndim: (0,) * n) for a in args]
            + [
                pl.BlockSpec((1, rows, half), lambda i, s: (step, 0, s[3])),
                pl.BlockSpec((rows, half), lambda i, s: (0, 0)),
            ],
            out_specs=pl.BlockSpec(shape.shape, lambda i, s, n=len(shape.shape): (0,) * n),
        ),
        compiler_params=VMEM,
    )(idx, *args, tokens, got)


def swap(value, axis):
    return lax.ppermute(value, axis, [(0, 1), (1, 0)])


def shift(value, axis, by, count):
    return lax.ppermute(value, axis, [(i, (i + by) % count) for i in range(count)])


def gather_z(value):
    copies = jnp.broadcast_to(value, (NZ, *value.shape))
    return lax.all_to_all(copies, "z", 0, 0, tiled=True)


def exchange_z(parts):
    return lax.all_to_all(parts, "z", 0, 0, tiled=True)


def local(inputs, targets, base, adapter_a, adapter_b):
    tokens = inputs[0]
    a_start = adapter_a[0]
    steps, rows, width = tokens.shape
    half = width // 2
    scale = width ** (-0.5)
    total_rows = float(rows * 2 * NZ)
    idx = jnp.stack([lax.axis_index(n) for n in ("x", "yh", "c", "yl", "z")]).astype(jnp.int32)
    away = (1 - lax.axis_index("yl")) * half

    blocks = adapter_b[0].T.reshape(8, 8, 2, 256).transpose(0, 2, 1, 3).reshape(NZ, 8, 256)

    send0 = lax.dynamic_slice(tokens, (0, 0, away), (1, rows, half))[0]
    got0 = swap(send0, "yl")
    cols = gather_z(base.T.astype(bf16))
    cols = cols.transpose(1, 0, 2).reshape(cols.shape[1], half)
    pair = jnp.stack([cols, swap(cols, "yh")])
    near = [pair, shift(pair, "x", 1, 4), shift(pair, "x", 2, 4), shift(pair, "x", 3, 4)]
    send1 = lax.dynamic_slice(tokens, (1, 0, away), (1, rows, half))[0]
    got1 = swap(send1, "yl")
    a_whole = gather_z(a_start.astype(bf16))
    pieces = near + [swap(piece, "c") for piece in near]

    sent, later = pl.pallas_call(
        keys_kernel,
        out_shape=(shaped((2 * rows + 64, 512), bf16), shaped((2 * rows, 512), f32)),
        in_specs=[smem()] + hbm(3) + vmem(2) + hbm(8),
        scratch_shapes=[
            pltpu.VMEM((2, 2, rows, half), bf16),
            pltpu.VMEM((16, 32, half), bf16),
            pltpu.SemaphoreType.DMA((4,)),
            pltpu.SemaphoreType.DMA((16,)),
        ],
        compiler_params=VMEM,
    )(idx, tokens, got0, got1, targets[0], a_whole, *pieces)

    got_sent = swap(sent, "yl")
    got_later = swap(later, "yl")
    payload = shaped((NZ, 80, 256), bf16)

    def first(idx_ref, *refs):
        first_kernel(total_rows, idx_ref, *refs)

    parts = exchange_z(with_tokens(first, 0, idx, payload, (tokens, got0), (sent, got_sent, blocks)))

    def update(*refs):
        update_kernel(scale, *refs)

    a_next, b_next, copies = call(
        update,
        (shaped((64, 256), f32), shaped((8, 256), f32), payload),
        [smem()] + vmem(3),
        idx,
        parts,
        a_start,
        blocks,
    )
    whole = exchange_z(copies)
    low = with_tokens(low_kernel, 1, idx, shaped((64, 2 * rows), f32), (tokens, got1), (whole,))
    got_low = swap(low, "yl")

    def second(idx_ref, *refs):
        second_kernel(total_rows, idx_ref, *refs)

    parts = exchange_z(
        with_tokens(second, 1, idx, payload, (tokens, got1), (later, got_later, low, got_low, whole))
    )

    def last_update(*refs):
        last_update_kernel(scale, *refs)

    a_last, copies = call(
        last_update, (shaped((64, 256), f32), shaped((NZ, 8, 256), f32)), vmem(3), parts, a_next, b_next
    )
    blocks_last = exchange_z(copies)
    change, b_last = call(
        change_kernel,
        (shaped((512, 256), f32), shaped((512, 64), f32)),
        vmem(4),
        a_last,
        blocks_last,
        a_start,
        blocks,
    )
    merged = lax.all_to_all(change.reshape(16, 32, 256), W, 0, 0, tiled=True)
    new_base = call(merge_kernel, shaped(base.shape, f32), vmem(2), merged, base)
    return (new_base, a_last[None], b_last[None])


def solution(mesh):
    finer = Mesh(mesh.devices.reshape(4, 2, 2, 2, NZ), (*W, *F))
    return jax.shard_map(
        local,
        mesh=finer,
        in_specs=(
            P(W, None, F, None),
            P(W, None, F, None),
            P(F, W),
            P(W, None, F),
            P(W, None, None),
        ),
        out_specs=(P(F, W), P(W, None, F), P(W, None, None)),
        check_vma=False,
    )
```

time: 638 us -> 322 us (0.50)
  waiting for transfers between devices: 342 us -> 75.5 us
  blocking collectives: 214 us -> 107 us
  starting transfers between devices: 14.2 us -> 86.2 us
  Pallas kernels: 0 us -> 35.1 us
  matrix products: 20 us -> 0 us
  other arithmetic: 15.6 us -> 1.66 us
  between operations: 14.1 us -> 0.95 us
    all_gather x2 -> x0, waiting for transfers between devices: 174 us -> none  [the longest x1 101 us: local(): lax.all_gather(column, 'worker', axis=1, tiled=True)]
    all_to_all x4 -> x3, blocking collectives: 214 us -> 107 us  [exchange_z(): return lax.all_to_all(parts, 'z', 0, 0, tiled=True)]
    all_to_all x3 -> x4, waiting for transfers between devices: 122 us -> 47.9 us  [the longest x1 26.2 us: exchange_z(): return lax.all_to_all(parts, 'z', 0, 0, tiled=True)]
    reduce_scatter x2 -> x0, waiting for transfers between devices: 45.9 us -> none  [sum_in_order(): parts = lax.psum_scatter(parts, axes[k], scatter_dimension=0, tiled=True)]
    ppermute x0 -> x13, starting transfers between devices: none -> 40.9 us  [the longest x10 30.3 us: swap(): return lax.ppermute(value, axis, [(0, 1), (1, 0)])]
    pallas_call x0 -> x8, Pallas kernels: none -> 35.1 us  [the longest x3 15.5 us: with_tokens(): pl.pallas_call(kernel, out_shape=shape, grid_spec=pltpu.PrefetchScalarGri...]
    all_to_all x3 -> x4, starting transfers between devices: 13.9 us -> 45.3 us  [the longest x2 26 us: gather_z(): return lax.all_to_all(copies, 'z', 0, 0, tiled=True)]
    ppermute x0 -> x13, waiting for transfers between devices: none -> 27.6 us  [the longest x10 27.6 us: swap(): return lax.ppermute(value, axis, [(0, 1), (1, 0)])]
  transfers between devices with their start and end apart: 7 -> 17, of which waited for: 7 -> 7; matrix products, arithmetic and copies ran while one was open for 2% -> 2% of each run, Pallas kernels for 0% -> 1%
where the time goes in v1:
time: 322 us; the launch traced here: 320 us
  blocking collectives  107 us (33%)
  starting transfers between devices  86.2 us (27%)
  waiting for transfers between devices  75.5 us (23%)
  Pallas kernels  35.1 us (11%)
  local copies, waits for them, and re-layouts  13.9 us (4%)
    all_to_all x3, blocking collectives, exchange_z(): return lax.all_to_all(parts, 'z', 0, 0, tiled=True)  107 us
    ppermute x10, starting transfers between devices, swap(): return lax.ppermute(value, axis, [(0, 1), (1, 0)])  30.3 us
    ppermute x10, waiting for transfers between devices, swap(): return lax.ppermute(value, axis, [(0, 1), (1, 0)])  27.6 us
    all_to_all x1, waiting for transfers between devices, exchange_z(): return lax.all_to_all(parts, 'z', 0, 0, tiled=True)  26.2 us
    all_to_all x2, starting transfers between devices, gather_z(): return lax.all_to_all(copies, 'z', 0, 0, tiled=True)  26 us
    pallas_call x3, Pallas kernels, with_tokens(): pl.pallas_call(kernel, out_shape=shape, grid_spec=pltpu.PrefetchScalarGri...  15.5 us
    all_to_all x2, waiting for transfers between devices, gather_z(): return lax.all_to_all(copies, 'z', 0, 0, tiled=True)  12.9 us
    pallas_call x1, Pallas kernels, local(): pl.pallas_call(keys_kernel, out_shape=(shaped((2 * rows + 64, 512), bf16)...  11.3 us
  transfers between devices with their start and end apart: 17, of which 7 were waited for; matrix products, arithmetic and copies ran while one was open for 2% of the time, Pallas kernels for 1%

profile of v1, /device:TPU:1, one launch (start us, length us, event | category | flops | bytes accessed | tf_op | source)
XLA Modules:
  0.0 320.3 jit_solution(5346062667800875747)
XLA Ops:
  0.6 0.8 convert_bitcast_fusion
  1.4 0.7 broadcast_in_dim.13
  2.1 15.7 %all-to-all-start.1 = ((bf16[16,32,256]{2,1,0:T(8,128)(2,1)}), bf16[16,32,256]{2,1,0:T(8,128)(2,1)S(1)}, u32[]{:S(2)}, u32[]{:S(2)}) async-start(bf16[16,32,256]{2,1,0:T(8,128)(2,1)} %broadcast_in_dim.13), calls=%async_computation.1 | async-start | bytes 524288 | tf_op jit(solution)/shard_map/all_to_all | solution.py:240
  17.9 0.8 bitcast_convert_fusion
  18.7 12.9 %all-to-all-done.1 = bf16[16,32,256]{2,1,0:T(8,128)(2,1)S(1)} async-done(((bf16[16,32,256]{2,1,0:T(8,128)(2,1)}), bf16[16,32,256]{2,1,0:T(8,128)(2,1)S(1)}, u32[]{:S(2)}, u32[]{:S(2)}) %all-to-all-start.1) | async-done | bytes 262176 | tf_op jit(solution)/shard_map/all_to_all | solution.py:240
  31.6 0.8 broadcast_in_dim.12
  32.5 10.3 %all-to-all-start = ((bf16[16,64,256]{2,1,0:T(8,128)(2,1)}), bf16[16,64,256]{2,1,0:T(8,128)(2,1)S(1)}, u32[]{:S(2)}, u32[]{:S(2)}) async-start(bf16[16,64,256]{2,1,0:T(8,128)(2,1)} %broadcast_in_dim.12), calls=%async_computation | async-start | bytes 1048576 | tf_op jit(solution)/shard_map/all_to_all | solution.py:240
  42.8 4.8 %collective-permute-start.2 = (bf16[32,4096]{1,0:T(8,128)(2,1)S(1)}, bf16[32,4096]{1,0:T(8,128)(2,1)S(1)}, u32[]{:S(2)}, u32[]{:S(2)}) collective-permute-start(bf16[32,4096]{1,0:T(8,128)(2,1)S(1)} %bitcast.45), channel_id=1, source_target_pairs={{0,64},{64,0},{1,65},{65,1},{2,66},{66,2},{3,67},{67,3},{4,68},{68... | collective-permute-start | bytes 786440 | tf_op jit(solution)/shard_map/ppermute | solution.py:231
  47.6 3.1 dynamic-slice_bitcast_fusion
  50.8 2.3 collective-permute-start.1
  53.1 0.2 copy.11
  53.2 0.1 stack_reshape.3
  53.3 0.0 collective-permute-done.2
  53.4 0.1 pad_maximum_fusion.rest_0_
  53.4 3.1 collective-permute-start.3
  56.6 3.0 collective-permute-start
  59.5 4.4 %collective-permute-start.4 = (bf16[2,32,4096]{2,1,0:T(8,128)(2,1)S(1)}, bf16[2,32,4096]{2,1,0:T(8,128)(2,1)}, u32[]{:S(2)}, u32[]{:S(2)}) collective-permute-start(bf16[2,32,4096]{2,1,0:T(8,128)(2,1)S(1)} %pad_maximum_fusion.rest_0_), channel_id=1, source_target_pairs={{0,256},{128,384},{256,0},{384,128},{1,257},{129,385},{257,1},{385... | collective-permute-start | bytes 1572872 | tf_op jit(solution)/shard_map/ppermute | solution.py:235
  63.9 3.1 collective-permute-start.5
  67.0 9.4 %collective-permute-done.1.xr1.xr.refs_6_ = bf16[128,4096]{1,0:T(8,128)(2,1)S(1)} collective-permute-done((bf16[128,4096]{1,0:T(8,128)(2,1)}, bf16[128,4096]{1,0:T(8,128)(2,1)S(1)}, u32[]{:S(2)}, u32[]{:S(2)}) %collective-permute-start.1) | collective-permute-done | bytes 1048608 | tf_op jit(solution)/shard_map/ppermute | solution.py:231
  76.4 5.7 %collective-permute-start.6 = (bf16[2,32,4096]{2,1,0:T(8,128)(2,1)S(1)}, bf16[2,32,4096]{2,1,0:T(8,128)(2,1)}, u32[]{:S(2)}, u32[]{:S(2)}) collective-permute-start(bf16[2,32,4096]{2,1,0:T(8,128)(2,1)S(1)} %pad_maximum_fusion.rest_0_), channel_id=1, source_target_pairs={{0,32},{32,0},{1,33},{33,1},{2,34},{34,2},{3,35},{35,3},{4,36},{36... | collective-permute-start | bytes 1572872 | tf_op jit(solution)/shard_map/ppermute | solution.py:231
  82.1 0.0 collective-permute-done.3.rest_1_
  82.1 1.9 collective-permute-start.7
  84.0 0.0 collective-permute-done.4.rest_2_
  84.0 2.4 collective-permute-start.8
  86.4 0.0 collective-permute-done.5.rest_3_
  86.5 3.2 collective-permute-start.9
  89.6 0.7 stack.29.idx.idx_ref.refs_0_
  90.3 8.4 %collective-permute-done.xr0.refs_4_ = bf16[128,4096]{1,0:T(8,128)(2,1)S(1)} collective-permute-done((bf16[128,4096]{1,0:T(8,128)(2,1)}, bf16[128,4096]{1,0:T(8,128)(2,1)S(1)}, u32[]{:S(2)}, u32[]{:S(2)}) %collective-permute-start) | collective-permute-done | bytes 1048608 | tf_op jit(solution)/shard_map/ppermute | solution.py:231
  98.7 0.0 collective-permute-done.6.rest_4_
  98.7 0.0 all-to-all-done.a_ref
  98.8 0.0 collective-permute-done.7.rest_5_
  98.8 0.0 collective-permute-done.8.rest_6_
  98.8 0.0 collective-permute-done.9.rest_7_
  98.8 0.9 copy-done.2
  99.7 0.2 copy-done.3
  99.9 11.3 %shard_map.76 = (bf16[320,512]{1,0:T(8,128)(2,1)}, f32[256,512]{1,0:T(8,128)}) custom-call(s32[5]{0:T(128)} %stack.29.idx.idx_ref.refs_0_, bf16[2,128,8192]{2,1,0:T(8,128)(2,1)} %bitcast.31, bf16[128,4096]{1,0:T(8,128)(2,1)} %copy-done.2, bf16[128,4096]{1,0:T(8,128)(2,1)} %copy-done, bf16[2,128,512]{2,1,0:T(8,128)(2,1)} %bitcast.43, ...), custom_call_target="tpu_custom_call" | custom-call | tf_op jit(solution)/shard_map/pallas_call | solution.py:270
  111.2 2.3 collective-permute-start.11
  113.5 6.9 %collective-permute-done.11.refs_1_ = bf16[320,512]{1,0:T(8,128)(2,1)S(1)} collective-permute-done((bf16[320,512]{1,0:T(8,128)(2,1)}, bf16[320,512]{1,0:T(8,128)(2,1)S(1)}, u32[]{:S(2)}, u32[]{:S(2)}) %collective-permute-start.11) | collective-permute-done | bytes 327712 | tf_op jit(solution)/shard_map/ppermute | solution.py:231
  120.4 0.7 copy-done.8
  121.2 5.7 %shard_map.77 = bf16[16,80,256]{2,1,0:T(8,128)(2,1)} custom-call(s32[5]{0:T(128)} %stack.29.idx.idx_ref.refs_0_, bf16[320,512]{1,0:T(8,128)(2,1)} %get-tuple-element.13.refs_0_, bf16[320,512]{1,0:T(8,128)(2,1)} %copy-done.8, f32[16,8,256]{2,1,0:T(8,128)} %bitcast.37, bf16[2,128,8192]{2,1,0:T(8,128)(2,1)} %bitcast.32, bf16[128,4096]{1,0:T(8,128)(2,1)} %copy-done.2), custom_call_target="tpu_custom_call" | custom-call | tf_op jit(solution)/shard_map/pallas_call | solution.py:213
  126.9 42.1 %all_to_all.35.refs_1_ = bf16[16,80,256]{2,1,0:T(8,128)(2,1)} all-to-all(bf16[16,80,256]{2,1,0:T(8,128)(2,1)} %shard_map.77), channel_id=1, replica_groups=mesh['x'=4,'yh'=2,'c'=2,'yl'=2,'z'=16] {'z'}, dimensions={0} | all-to-all | bytes 1310720 | tf_op jit(solution)/shard_map/all_to_all | solution.py:244
  169.1 2.1 shard_map.78
  171.2 8.9 %all-to-all-start.3 = ((bf16[16,80,256]{2,1,0:T(8,128)(2,1)}), bf16[16,80,256]{2,1,0:T(8,128)(2,1)S(1)}, u32[]{:S(2)}, u32[]{:S(2)}) async-start(bf16[16,80,256]{2,1,0:T(8,128)(2,1)} %get-tuple-element.14), calls=%async_computation.3 | async-start | bytes 1310720 | tf_op jit(solution)/shard_map/all_to_all | solution.py:244
  180.1 2.3 collective-permute-start.10
  182.4 26.2 %all-to-all-done.3.whole.refs_4_ = bf16[16,80,256]{2,1,0:T(8,128)(2,1)S(1)} async-done(((bf16[16,80,256]{2,1,0:T(8,128)(2,1)}), bf16[16,80,256]{2,1,0:T(8,128)(2,1)S(1)}, u32[]{:S(2)}, u32[]{:S(2)}) %all-to-all-start.3) | async-done | bytes 655392 | tf_op jit(solution)/shard_map/all_to_all | solution.py:244
  208.6 0.8 copy-done.1
  209.5 3.9 %shard_map.79.refs_2_ = f32[64,256]{1,0:T(8,128)} custom-call(s32[5]{0:T(128)} %stack.29.idx.idx_ref.refs_0_, bf16[16,80,256]{2,1,0:T(8,128)(2,1)} %copy-done.1, bf16[2,128,8192]{2,1,0:T(8,128)(2,1)} %bitcast.33, bf16[128,4096]{1,0:T(8,128)(2,1)} %copy-done), custom_call_target="tpu_custom_call" | custom-call | tf_op jit(solution)/shard_map/pallas_call | solution.py:213
  213.4 2.4 collective-permute-start.12
  215.8 0.0 collective-permute-done.10.refs_1_
  215.8 0.0 copy-start.7
  215.8 2.9 collective-permute-done.12.refs_3_
  218.7 0.6 copy-done.10
  219.3 5.9 %shard_map.80 = bf16[16,80,256]{2,1,0:T(8,128)(2,1)} custom-call(s32[5]{0:T(128)} %stack.29.idx.idx_ref.refs_0_, f32[256,512]{1,0:T(8,128)} %get-tuple-element.12.refs_0_, f32[256,512]{1,0:T(8,128)} %copy-done.7, f32[64,256]{1,0:T(8,128)} %shard_map.79.refs_2_, f32[64,256]{1,0:T(8,128)} %copy-done.10, bf16[16,80,256]{2,1,0:T(8,128)(2,1)} %copy-done.1, ...), custom_call_target="tpu_custom_call" | custom-call | tf_op jit(solution)/shard_map/pallas_call | solution.py:213
  225.3 46.2 %all_to_all.36.refs_0_ = bf16[16,80,256]{2,1,0:T(8,128)(2,1)} all-to-all(bf16[16,80,256]{2,1,0:T(8,128)(2,1)} %shard_map.80), channel_id=1, replica_groups=mesh['x'=4,'yh'=2,'c'=2,'yl'=2,'z'=16] {'z'}, dimensions={0} | all-to-all | bytes 1310720 | tf_op jit(solution)/shard_map/all_to_all | solution.py:244
  271.4 1.9 shard_map.81
  273.3 18.7 %all_to_all.37.blocks = f32[16,8,256]{2,1,0:T(8,128)} all-to-all(f32[16,8,256]{2,1,0:T(8,128)} %get-tuple-element.18), channel_id=1, replica_groups=mesh['x'=4,'yh'=2,'c'=2,'yl'=2,'z'=16] {'z'}, dimensions={0} | all-to-all | bytes 262144 | tf_op jit(solution)/shard_map/all_to_all | solution.py:244
  292.0 2.5 shard_map.82
  294.5 10.4 %all-to-all-start.6 = ((f32[16,32,256]{2,1,0:T(8,128)}), f32[16,32,256]{2,1,0:T(8,128)S(1)}, u32[]{:S(2)}, u32[]{:S(2)}) async-start(f32[16,32,256]{2,1,0:T(8,128)} %bitcast.42), calls=%async_computation.6 | async-start | bytes 1048576 | tf_op jit(solution)/shard_map/all_to_all | solution.py:331
  304.9 0.7 copy.13.base
  305.6 1.7 copy.15
  307.4 8.7 %all-to-all-done.6.parts = f32[16,32,256]{2,1,0:T(8,128)S(1)} async-done(((f32[16,32,256]{2,1,0:T(8,128)}), f32[16,32,256]{2,1,0:T(8,128)S(1)}, u32[]{:S(2)}, u32[]{:S(2)}) %all-to-all-start.6) | async-done | bytes 524320 | tf_op jit(solution)/shard_map/all_to_all | solution.py:331
  316.1 0.8 copy-done.5
  316.9 1.8 shard_map.83
  318.7 1.6 copy.14
  (16 shorter events, 0.0 us)
Async XLA Ops:
  2.1 29.5 %all-to-all-start.1 = ((bf16[16,32,256]{2,1,0:T(8,128)(2,1)}), bf16[16,32,256]{2,1,0:T(8,128)(2,1)S(1)}, u32[]{:S(2)}, u32[]{:S(2)}) async-start(bf16[16,32,256]{2,1,0:T(8,128)(2,1)} %broadcast_in_dim.13), calls=%async_computation.1 | async-start | bytes 524288 | tf_op jit(solution)/shard_map/all_to_all | solution.py:240
  32.5 66.3 %all-to-all-start = ((bf16[16,64,256]{2,1,0:T(8,128)(2,1)}), bf16[16,64,256]{2,1,0:T(8,128)(2,1)S(1)}, u32[]{:S(2)}, u32[]{:S(2)}) async-start(bf16[16,64,256]{2,1,0:T(8,128)(2,1)} %broadcast_in_dim.12), calls=%async_computation | async-start | bytes 1048576 | tf_op jit(solution)/shard_map/all_to_all | solution.py:240
  42.8 10.5 %collective-permute-start.2 = (bf16[32,4096]{1,0:T(8,128)(2,1)S(1)}, bf16[32,4096]{1,0:T(8,128)(2,1)S(1)}, u32[]{:S(2)}, u32[]{:S(2)}) collective-permute-start(bf16[32,4096]{1,0:T(8,128)(2,1)S(1)} %bitcast.45), channel_id=1, source_target_pairs={{0,64},{64,0},{1,65},{65,1},{2,66},{66,2},{3,67},{67,3},{4,68},{68... | collective-permute-start | bytes 786440 | tf_op jit(solution)/shard_map/ppermute | solution.py:231
  50.8 25.6 %collective-permute-start.1 = (bf16[128,4096]{1,0:T(8,128)(2,1)}, bf16[128,4096]{1,0:T(8,128)(2,1)S(1)}, u32[]{:S(2)}, u32[]{:S(2)}) collective-permute-start(bf16[128,4096]{1,0:T(8,128)(2,1)} %get-tuple-element.27), channel_id=1, source_target_pairs={{0,16},{16,0},{1,17},{17,1},{2,18},{18,2},{3,19},{19,3},{4,20},{20... | collective-permute-start | bytes 3145736 | tf_op jit(solution)/shard_map/ppermute | solution.py:231
  53.4 45.4 %copy-start.4 = (bf16[2,32,4096]{2,1,0:T(8,128)(2,1)}, bf16[2,32,4096]{2,1,0:T(8,128)(2,1)S(1)}, u32[]{:S(2)}) copy-start(bf16[2,32,4096]{2,1,0:T(8,128)(2,1)S(1)} %pad_maximum_fusion.rest_0_) | copy-start | bytes 1572868
  53.4 28.7 %collective-permute-start.3 = (bf16[2,32,4096]{2,1,0:T(8,128)(2,1)S(1)}, bf16[2,32,4096]{2,1,0:T(8,128)(2,1)}, u32[]{:S(2)}, u32[]{:S(2)}) collective-permute-start(bf16[2,32,4096]{2,1,0:T(8,128)(2,1)S(1)} %pad_maximum_fusion.rest_0_), channel_id=1, source_target_pairs={{0,128},{128,256},{256,384},{384,0},{1,129},{129,257},{257,385},{3... | collective-permute-start | bytes 1572872 | tf_op jit(solution)/shard_map/ppermute | solution.py:235
  56.6 42.2 %collective-permute-start = (bf16[128,4096]{1,0:T(8,128)(2,1)}, bf16[128,4096]{1,0:T(8,128)(2,1)S(1)}, u32[]{:S(2)}, u32[]{:S(2)}) collective-permute-start(bf16[128,4096]{1,0:T(8,128)(2,1)} %get-tuple-element.28), channel_id=1, source_target_pairs={{0,16},{16,0},{1,17},{17,1},{2,18},{18,2},{3,19},{19,3},{4,20},{20... | collective-permute-start | bytes 3145736 | tf_op jit(solution)/shard_map/ppermute | solution.py:231
  59.5 24.5 %collective-permute-start.4 = (bf16[2,32,4096]{2,1,0:T(8,128)(2,1)S(1)}, bf16[2,32,4096]{2,1,0:T(8,128)(2,1)}, u32[]{:S(2)}, u32[]{:S(2)}) collective-permute-start(bf16[2,32,4096]{2,1,0:T(8,128)(2,1)S(1)} %pad_maximum_fusion.rest_0_), channel_id=1, source_target_pairs={{0,256},{128,384},{256,0},{384,128},{1,257},{129,385},{257,1},{385... | collective-permute-start | bytes 1572872 | tf_op jit(solution)/shard_map/ppermute | solution.py:235
  63.9 22.5 %collective-permute-start.5 = (bf16[2,32,4096]{2,1,0:T(8,128)(2,1)S(1)}, bf16[2,32,4096]{2,1,0:T(8,128)(2,1)}, u32[]{:S(2)}, u32[]{:S(2)}) collective-permute-start(bf16[2,32,4096]{2,1,0:T(8,128)(2,1)S(1)} %pad_maximum_fusion.rest_0_), channel_id=1, source_target_pairs={{0,384},{128,0},{256,128},{384,256},{1,385},{129,1},{257,129},{385... | collective-permute-start | bytes 1572872 | tf_op jit(solution)/shard_map/ppermute | solution.py:235
  76.4 22.4 %copy-start = (bf16[128,4096]{1,0:T(8,128)(2,1)}, bf16[128,4096]{1,0:T(8,128)(2,1)S(1)}, u32[]{:S(2)}) copy-start(bf16[128,4096]{1,0:T(8,128)(2,1)S(1)} %collective-permute-done.1.xr1.xr.refs_6_) | copy-start | bytes 3145732
  76.4 22.4 %collective-permute-start.6 = (bf16[2,32,4096]{2,1,0:T(8,128)(2,1)S(1)}, bf16[2,32,4096]{2,1,0:T(8,128)(2,1)}, u32[]{:S(2)}, u32[]{:S(2)}) collective-permute-start(bf16[2,32,4096]{2,1,0:T(8,128)(2,1)S(1)} %pad_maximum_fusion.rest_0_), channel_id=1, source_target_pairs={{0,32},{32,0},{1,33},{33,1},{2,34},{34,2},{3,35},{35,3},{4,36},{36... | collective-permute-start | bytes 1572872 | tf_op jit(solution)/shard_map/ppermute | solution.py:231
  82.1 16.7 %collective-permute-start.7 = (bf16[2,32,4096]{2,1,0:T(8,128)(2,1)}, bf16[2,32,4096]{2,1,0:T(8,128)(2,1)}, u32[]{:S(2)}, u32[]{:S(2)}) collective-permute-start(bf16[2,32,4096]{2,1,0:T(8,128)(2,1)} %collective-permute-done.3.rest_1_), channel_id=1, source_target_pairs={{0,32},{32,0},{1,33},{33,1},{2,34},{34,2},{3,35},{35,3},{4,36},{36... | collective-permute-start | bytes 1572872 | tf_op jit(solution)/shard_map/ppermute | solution.py:231
  84.0 14.7 %collective-permute-start.8 = (bf16[2,32,4096]{2,1,0:T(8,128)(2,1)}, bf16[2,32,4096]{2,1,0:T(8,128)(2,1)}, u32[]{:S(2)}, u32[]{:S(2)}) collective-permute-start(bf16[2,32,4096]{2,1,0:T(8,128)(2,1)} %collective-permute-done.4.rest_2_), channel_id=1, source_target_pairs={{0,32},{32,0},{1,33},{33,1},{2,34},{34,2},{3,35},{35,3},{4,36},{36... | collective-permute-start | bytes 1572872 | tf_op jit(solution)/shard_map/ppermute | solution.py:231
  86.5 12.3 %collective-permute-start.9 = (bf16[2,32,4096]{2,1,0:T(8,128)(2,1)}, bf16[2,32,4096]{2,1,0:T(8,128)(2,1)}, u32[]{:S(2)}, u32[]{:S(2)}) collective-permute-start(bf16[2,32,4096]{2,1,0:T(8,128)(2,1)} %collective-permute-done.5.rest_3_), channel_id=1, source_target_pairs={{0,32},{32,0},{1,33},{33,1},{2,34},{34,2},{3,35},{35,3},{4,36},{36... | collective-permute-start | bytes 1572872 | tf_op jit(solution)/shard_map/ppermute | solution.py:231
  98.7 1.0 copy-start.2
  98.7 1.2 copy-start.3
  111.2 9.2 %collective-permute-start.11 = (bf16[320,512]{1,0:T(8,128)(2,1)}, bf16[320,512]{1,0:T(8,128)(2,1)S(1)}, u32[]{:S(2)}, u32[]{:S(2)}) collective-permute-start(bf16[320,512]{1,0:T(8,128)(2,1)} %get-tuple-element.13.refs_0_), channel_id=1, source_target_pairs={{0,16},{16,0},{1,17},{17,1},{2,18},{18,2},{3,19},{19,3},{4,20},{20... | collective-permute-start | bytes 983048 | tf_op jit(solution)/shard_map/ppermute | solution.py:231
  120.4 0.7 copy-start.8
  121.2 58.9 %copy-start.6 = (f32[256,512]{1,0:T(8,128)S(1)}, f32[256,512]{1,0:T(8,128)}, u32[]{:S(2)}) copy-start(f32[256,512]{1,0:T(8,128)} %get-tuple-element.12.refs_0_) | copy-start | bytes 1572868
  171.2 37.5 %all-to-all-start.3 = ((bf16[16,80,256]{2,1,0:T(8,128)(2,1)}), bf16[16,80,256]{2,1,0:T(8,128)(2,1)S(1)}, u32[]{:S(2)}, u32[]{:S(2)}) async-start(bf16[16,80,256]{2,1,0:T(8,128)(2,1)} %get-tuple-element.14), calls=%async_computation.3 | async-start | bytes 1310720 | tf_op jit(solution)/shard_map/all_to_all | solution.py:244
  180.1 35.7 %collective-permute-start.10 = (f32[256,512]{1,0:T(8,128)S(1)}, f32[256,512]{1,0:T(8,128)S(1)}, u32[]{:S(2)}, u32[]{:S(2)}) collective-permute-start(f32[256,512]{1,0:T(8,128)S(1)} %copy-done.6), channel_id=1, source_target_pairs={{0,16},{16,0},{1,17},{17,1},{2,18},{18,2},{3,19},{19,3},{4,20},{20... | collective-permute-start | bytes 1572872 | tf_op jit(solution)/shard_map/ppermute | solution.py:231
  208.6 0.9 copy-start.1
  213.4 91.5 %copy-start.9 = (f32[256,32]{0,1:T(8,128)S(1)}, f32[256,32]{0,1:T(8,128)}, u32[]{:S(2)}) copy-start(f32[256,32]{0,1:T(8,128)} %param.7) | copy-start | bytes 98308
  213.4 5.3 %collective-permute-start.12 = (f32[64,256]{1,0:T(8,128)}, f32[64,256]{1,0:T(8,128)S(1)}, u32[]{:S(2)}, u32[]{:S(2)}) collective-permute-start(f32[64,256]{1,0:T(8,128)} %shard_map.79.refs_2_), channel_id=1, source_target_pairs={{0,16},{16,0},{1,17},{17,1},{2,18},{18,2},{3,19},{19,3},{4,20},{20... | collective-permute-start | bytes 196616 | tf_op jit(solution)/shard_map/ppermute | solution.py:231
  215.8 2.9 copy-start.7
  218.7 0.6 copy-start.10
  294.5 21.6 %all-to-all-start.6 = ((f32[16,32,256]{2,1,0:T(8,128)}), f32[16,32,256]{2,1,0:T(8,128)S(1)}, u32[]{:S(2)}, u32[]{:S(2)}) async-start(f32[16,32,256]{2,1,0:T(8,128)} %bitcast.42), calls=%async_computation.6 | async-start | bytes 1048576 | tf_op jit(solution)/shard_map/all_to_all | solution.py:331
  316.1 0.8 copy-start.5

commit v2 on v1

v2 whole, which is shorter than its diff:
```python
import jax
import jax.numpy as jnp
from jax import lax
from jax.experimental import pallas as pl
from jax.experimental.pallas import tpu as pltpu
from jax.sharding import Mesh
from jax.sharding import PartitionSpec as P

W = ("x", "yh", "c")
F = ("yl", "z")
NZ = 16

branch_scale = 0.25
rate_down = 200.0
rate_up = 20.0

bf16 = jnp.bfloat16
f32 = jnp.float32
HIGH = lax.Precision.HIGHEST
VMEM = pltpu.CompilerParams(vmem_limit_bytes=60 * 1024 * 1024)


def dot(a, b, ca, cb, precision=None):
    return lax.dot_general(a, b, (((ca,), (cb,)), ((), ())), precision=precision, preferred_element_type=f32)


def split(value):
    hi = value.astype(bf16)
    return hi, (value - hi.astype(f32)).astype(bf16)


def vmem(n):
    return [pl.BlockSpec(memory_space=pltpu.VMEM)] * n


def hbm(n):
    return [pl.BlockSpec(memory_space=pl.ANY)] * n


def smem():
    return pl.BlockSpec(memory_space=pltpu.SMEM)


def low_kernel(pyl, whole, xo, xr, out):
    n = whole.shape[2]
    rows = xo.shape[1]
    scale = (2 * xo.shape[2]) ** (-0.5)
    own = jnp.zeros((64, rows), f32)
    other = jnp.zeros((64, rows), f32)
    for z in range(NZ):
        own = own + dot(whole[z, :64], xo[0, :, z * n : (z + 1) * n], 1, 1)
        other = other + dot(whole[z, :64], xr[:, z * n : (z + 1) * n], 1, 1)
    first = pyl == 0
    out[:, :rows] = jnp.where(first, own, other) * scale
    out[:, rows:] = jnp.where(first, other, own) * scale


def keys_kernel(step, idx, x_ref, xr_ref, after, y_ref, *rest):
    pieces = rest[:8]
    out, xs, bs, xsem, bsem = rest[8:]
    half = xs.shape[-1]
    rows = xs.shape[1]
    scale = (2 * half) ** (-0.5)
    px, pyh, pc, pyl = idx[0], idx[1], idx[2], idx[3]
    copies = [
        pltpu.make_async_copy(x_ref.at[step, :, pl.ds(pyl * half, half)], xs.at[pyl], xsem.at[0]),
        pltpu.make_async_copy(xr_ref, xs.at[1 - pyl], xsem.at[1]),
    ]
    loads = []
    for k, piece in enumerate(pieces):
        dc, dx = divmod(k, 4)
        for dy in range(2):
            w = lax.rem(pyh + dy, 2) * 2 + lax.rem(pc + dc, 2)
            loads.append(pltpu.make_async_copy(piece.at[dy], bs.at[dx, w], bsem.at[k * 2 + dy]))
    for copy in copies + loads:
        copy.start()
    for copy in copies:
        copy.wait()
    tokens = xs[...].reshape(2 * rows, half)
    for dx in range(4):
        for k in (dx, dx + 4):
            for dy in range(2):
                loads[k * 2 + dy].wait()
        at = pl.ds(lax.rem(px + 4 - dx, 4) * 128, 128)
        part = dot(tokens, bs[dx].reshape(128, half), 1, 1) * scale
        wanted = y_ref[step, :, at].astype(f32)
        for q in range(2):
            rest_of = jnp.where(pyl == q, wanted, 0.0)
            out[q * rows : (q + 1) * rows, at] = (part[q * rows : (q + 1) * rows] - rest_of).astype(out.dtype)


def joined(blocks):
    return jnp.concatenate(
        [jnp.concatenate([blocks[2 * g], blocks[2 * g + 1]], axis=1) for g in range(NZ // 2)], axis=0
    )


def gradient_kernel(total_rows, pyl, own, got, low_own, low_got, blocks, xo, xr, out):
    if blocks.shape[1] == 8:
        up = joined(blocks[...])
    else:
        up = joined(blocks[:, 64:72].astype(f32) + blocks[:, 72:80].astype(f32))
    rows = xo.shape[1]
    low = low_own[...] + low_got[...]
    keys = own[...].astype(f32) + got[...].astype(f32)
    error = (keys + branch_scale * dot(low, up, 0, 0, HIGH)) / total_rows
    back = (branch_scale * dot(up, error, 1, 1, HIGH)).astype(bf16)
    hi, lo = split(branch_scale * dot(low, error, 1, 0, HIGH))
    first, second = back[:, :rows], back[:, rows:]
    own_back = jnp.where(pyl == 0, first, second)
    other_back = jnp.where(pyl == 0, second, first)
    n = xo.shape[2] // NZ
    for z in range(NZ):
        at = slice(z * n, (z + 1) * n)
        out[z, :64] = (dot(own_back, xo[0, :, at], 1, 0) + dot(other_back, xr[:, at], 1, 0)).astype(bf16)
        g, h = z // 2, z % 2
        out[z, 64:72] = hi[8 * g : 8 * g + 8, 256 * h : 256 * h + 256]
        out[z, 72:80] = lo[8 * g : 8 * g + 8, 256 * h : 256 * h + 256]


def summed(parts):
    down = parts[0, :64].astype(f32)
    up = parts[0, 64:72].astype(f32) + parts[0, 72:80].astype(f32)
    for z in range(1, NZ):
        down = down + parts[z, :64].astype(f32)
        up = up + (parts[z, 64:72].astype(f32) + parts[z, 72:80].astype(f32))
    return down, up


def update_kernel(scale, parts, a_ref, b_ref, a_out, b_out, copies):
    down, up = summed(parts)
    a = a_ref[...] - (rate_down * scale) * down
    b = b_ref[...] - rate_up * up
    a_out[...] = a
    a_half = a.astype(bf16)
    hi, lo = split(b)
    b_out[...] = hi.astype(f32) + lo.astype(f32)
    for z in range(NZ):
        copies[z, :64] = a_half
        copies[z, 64:72] = hi
        copies[z, 72:80] = lo


def last_update_kernel(scale, parts, a_ref, b_ref, a_out, copies):
    down, up = summed(parts)
    a_out[...] = a_ref[...] - (rate_down * scale) * down
    b = b_ref[...] - rate_up * up
    for z in range(NZ):
        copies[z] = b


def change_kernel(a_ref, blocks, a_start, blocks_start, out, b_out):
    up = joined(blocks[...])
    left = jnp.concatenate([up, -joined(blocks_start[...])], axis=0)
    right = jnp.concatenate([a_ref[...], a_start[...]], axis=0)
    out[...] = branch_scale * dot(left, right, 0, 0, HIGH)
    b_out[...] = up


def merge_kernel(parts, base, out):
    total = parts[0]
    for w in range(1, parts.shape[0]):
        total = total + parts[w]
    out[...] = base[...] + total * (1.0 / parts.shape[0])


def call(kernel, shapes, *args):
    return pl.pallas_call(
        kernel, out_shape=shapes, in_specs=vmem(len(args)), compiler_params=VMEM
    )(*args)


def shaped(dims, kind):
    return jax.ShapeDtypeStruct(dims, kind)


def with_tokens(kernel, step, idx, shape, tokens, got, args):
    rows, half = got.shape

    def body(s, *refs):
        kernel(s[3], *refs)

    return pl.pallas_call(
        body,
        out_shape=shape,
        grid_spec=pltpu.PrefetchScalarGridSpec(
            num_scalar_prefetch=1,
            grid=(1,),
            in_specs=[pl.BlockSpec(a.shape, lambda i, s, n=a.ndim: (0,) * n) for a in args]
            + [
                pl.BlockSpec((1, rows, half), lambda i, s: (step, 0, s[3])),
                pl.BlockSpec((rows, half), lambda i, s: (0, 0)),
            ],
            out_specs=pl.BlockSpec(shape.shape, lambda i, s, n=len(shape.shape): (0,) * n),
        ),
        compiler_params=VMEM,
    )(idx, *args, tokens, got)


def keys_of(step, idx, tokens, got, after, targets, pieces, kind):
    rows, half = got.shape

    def body(*refs):
        keys_kernel(step, *refs)

    return pl.pallas_call(
        body,
        out_shape=shaped((2 * rows, 512), kind),
        in_specs=[smem()] + hbm(3) + vmem(1) + hbm(8),
        scratch_shapes=[
            pltpu.VMEM((2, rows, half), bf16),
            pltpu.VMEM((4, 4, 32, half), bf16),
            pltpu.SemaphoreType.DMA((2,)),
            pltpu.SemaphoreType.DMA((16,)),
        ],
        compiler_params=VMEM,
    )(idx, tokens, got, after, targets, *pieces)


def swap(value, axis):
    return lax.ppermute(value, axis, [(0, 1), (1, 0)])


def shift(value, axis, by, count):
    return lax.ppermute(value, axis, [(i, (i + by) % count) for i in range(count)])


def exchange_z(parts):
    return lax.all_to_all(parts, "z", 0, 0, tiled=True)


def gather_z(value):
    return exchange_z(jnp.broadcast_to(value, (NZ, *value.shape)))


def whole_step(inputs, targets, base, adapter_a, adapter_b):
    tokens = inputs[0]
    a_start = adapter_a[0]
    _, rows, width = tokens.shape
    half = width // 2
    scale = width ** (-0.5)
    total_rows = float(rows * 2 * NZ)
    idx = jnp.stack([lax.axis_index(n) for n in ("x", "yh", "c", "yl", "z")]).astype(jnp.int32)
    away = (1 - lax.axis_index("yl")) * half
    blocks = adapter_b[0].T.reshape(8, 8, 2, 256).transpose(0, 2, 1, 3).reshape(NZ, 8, 256)
    block = lax.dynamic_index_in_dim(blocks, lax.axis_index("z"), 0, keepdims=False)

    def other_half(step):
        return lax.dynamic_slice(tokens, (step, 0, away), (1, rows, half))[0]

    send = lax.optimization_barrier(other_half(0))
    got0 = swap(send, "yl")
    cols = gather_z(base.T.astype(bf16))
    cols = cols.transpose(1, 0, 2).reshape(cols.shape[1], half)
    pair = jnp.stack([cols, swap(cols, "yh")])
    near = [pair] + [shift(pair, "x", d, 4) for d in (1, 2, 3)]
    a_whole = gather_z(a_start.astype(bf16))
    got1 = swap(other_half(1), "yl")
    pieces = near + [swap(piece, "c") for piece in near]

    low_shape = shaped((64, 2 * rows), f32)
    payload = shaped((NZ, 80, 256), bf16)

    def gradient(step, got, *args):
        return with_tokens(
            lambda *refs: gradient_kernel(total_rows, *refs), step, idx, payload, tokens, got, args
        )

    low = with_tokens(low_kernel, 0, idx, low_shape, tokens, got0, (a_whole,))
    got_low = swap(low, "yl")
    keys = keys_of(0, idx, tokens, got0, low, targets[0], pieces, bf16)
    got_keys = swap(keys, "yl")
    parts = exchange_z(gradient(0, got0, keys, got_keys, low, got_low, blocks))
    keys = keys_of(1, idx, tokens, got1, low, targets[0], pieces, f32)
    got_keys = swap(keys, "yl")

    a_next, block, copies = call(
        lambda *refs: update_kernel(scale, *refs),
        (shaped((64, 256), f32), shaped((8, 256), f32), payload),
        parts,
        a_start,
        block,
    )
    whole = exchange_z(copies)
    low = with_tokens(low_kernel, 1, idx, low_shape, tokens, got1, (whole,))
    got_low = swap(low, "yl")
    parts = exchange_z(gradient(1, got1, keys, got_keys, low, got_low, whole))
    a_last, copies = call(
        lambda *refs: last_update_kernel(scale, *refs),
        (shaped((64, 256), f32), shaped((NZ, 8, 256), f32)),
        parts,
        a_next,
        block,
    )
    blocks_last = exchange_z(copies)
    change, b_last = call(
        change_kernel, (shaped((512, 256), f32), shaped((64, 512), f32)), a_last, blocks_last, a_start, blocks
    )
    merged = lax.all_to_all(change.reshape(16, 32, 256), W, 0, 0, tiled=True)
    new_base = call(merge_kernel, shaped(base.shape[::-1], f32), merged, base.T)
    return (new_base.T, a_last[None], b_last.T[None])


def solution(mesh):
    finer = Mesh(mesh.devices.reshape(4, 2, 2, 2, NZ), (*W, *F))
    return jax.shard_map(
        whole_step,
        mesh=finer,
        in_specs=(
            P(W, None, F, None),
            P(W, None, F, None),
            P(F, W),
            P(W, None, F),
            P(W, None, None),
        ),
        out_specs=(P(F, W), P(W, None, F), P(W, None, None)),
        check_vma=False,
    )
```

time: 322 us -> 325 us (level)
  blocking collectives: 107 us -> 85.3 us
  Pallas kernels: 35.1 us -> 46.6 us
  starting transfers between devices: 86.2 us -> 96.9 us
  waiting for transfers between devices: 75.5 us -> 80.4 us
    all_to_all x3 -> x2, blocking collectives: 107 us -> 63.1 us  [exchange_z(): return lax.all_to_all(parts, 'z', 0, 0, tiled=True)]
    all_to_all x1 -> x4, starting transfers between devices: 8.89 us -> 49.7 us  [exchange_z(): return lax.all_to_all(parts, 'z', 0, 0, tiled=True)]
    all_to_all x3 -> x0, starting transfers between devices: 36.4 us -> none  [the longest x2 26 us: gather_z(): return lax.all_to_all(copies, 'z', 0, 0, tiled=True)]
    all_to_all x0 -> x1, blocking collectives: none -> 22.2 us  [whole_step(): merged = lax.all_to_all(change.reshape(16, 32, 256), W, 0, 0, tiled=True)]
    all_to_all x3 -> x0, waiting for transfers between devices: 21.6 us -> none  [the longest x2 12.9 us: gather_z(): return lax.all_to_all(copies, 'z', 0, 0, tiled=True)]
    all_to_all x1 -> x4, waiting for transfers between devices: 26.2 us -> 40.3 us  [exchange_z(): return lax.all_to_all(parts, 'z', 0, 0, tiled=True)]
    pallas_call x8 -> x10, Pallas kernels: 35.1 us -> 46.6 us  [the longest x2 19.5 us: keys_of(): pl.pallas_call(body, out_shape=shaped((2 * rows, 512), kind), in_specs=[s...]
    ppermute x3, waiting for transfers between devices: 0.01 us -> 7.04 us  [shift(): lax.ppermute(value, axis, [(i, (i + by) % count) for i in range(count)])]
  transfers between devices with their start and end apart: 17 -> 18, of which waited for: 7 -> 8; matrix products, arithmetic and copies ran while one was open for 2% -> 2% of each run, Pallas kernels for 1% -> 5%
where the time goes in v2:
time: 325 us; the launch traced here: 324 us
  starting transfers between devices  96.9 us (30%)
  blocking collectives  85.3 us (26%)
  waiting for transfers between devices  80.4 us (25%)
  Pallas kernels  46.6 us (14%)
  local copies, waits for them, and re-layouts  11.8 us (4%)
    all_to_all x2, blocking collectives, exchange_z(): return lax.all_to_all(parts, 'z', 0, 0, tiled=True)  63.1 us
    all_to_all x4, starting transfers between devices, exchange_z(): return lax.all_to_all(parts, 'z', 0, 0, tiled=True)  49.7 us
    all_to_all x4, waiting for transfers between devices, exchange_z(): return lax.all_to_all(parts, 'z', 0, 0, tiled=True)  40.3 us
    ppermute x11, starting transfers between devices, swap(): return lax.ppermute(value, axis, [(0, 1), (1, 0)])  36.7 us
    ppermute x11, waiting for transfers between devices, swap(): return lax.ppermute(value, axis, [(0, 1), (1, 0)])  33 us
    all_to_all x1, blocking collectives, whole_step(): merged = lax.all_to_all(change.reshape(16, 32, 256), W, 0, 0, tiled=True)  22.2 us
    pallas_call x2, Pallas kernels, keys_of(): pl.pallas_call(body, out_shape=shaped((2 * rows, 512), kind), in_specs=[s...  19.5 us
    pallas_call x4, Pallas kernels, with_tokens(): pl.pallas_call(body, out_shape=shape, grid_spec=pltpu.PrefetchScalarGridS...  19 us
  transfers between devices with their start and end apart: 18, of which 8 were waited for; matrix products, arithmetic and copies ran while one was open for 2% of the time, Pallas kernels for 5%

profile of v2, /device:TPU:1, one launch (start us, length us, event | category | flops | bytes accessed | tf_op | source)
XLA Modules:
  0.0 323.6 jit_solution(2272715328629671284)
XLA Ops:
  0.6 0.8 bitcast_convert_fusion
  1.4 0.7 broadcast_in_dim.13
  2.1 15.7 %all-to-all-start.1 = ((bf16[16,32,256]{2,1,0:T(8,128)(2,1)}), bf16[16,32,256]{2,1,0:T(8,128)(2,1)S(1)}, u32[]{:S(2)}, u32[]{:S(2)}) async-start(bf16[16,32,256]{2,1,0:T(8,128)(2,1)} %broadcast_in_dim.13), calls=%async_computation.1 | async-start | bytes 524288 | tf_op jit(solution)/shard_map/all_to_all | solution.py:229
  17.9 0.8 bitcast_convert_fusion.1
  18.7 12.9 %all-to-all-done.1 = bf16[16,32,256]{2,1,0:T(8,128)(2,1)S(1)} async-done(((bf16[16,32,256]{2,1,0:T(8,128)(2,1)}), bf16[16,32,256]{2,1,0:T(8,128)(2,1)S(1)}, u32[]{:S(2)}, u32[]{:S(2)}) %all-to-all-start.1) | async-done | bytes 262176 | tf_op jit(solution)/shard_map/all_to_all | solution.py:229
  31.6 0.8 broadcast_in_dim.12
  32.5 10.4 %all-to-all-start = ((bf16[16,64,256]{2,1,0:T(8,128)(2,1)}), bf16[16,64,256]{2,1,0:T(8,128)(2,1)}, u32[]{:S(2)}, u32[]{:S(2)}) async-start(bf16[16,64,256]{2,1,0:T(8,128)(2,1)} %broadcast_in_dim.12), calls=%async_computation | async-start | bytes 1048576 | tf_op jit(solution)/shard_map/all_to_all | solution.py:229
  42.9 4.8 %collective-permute-start.2 = (bf16[32,4096]{1,0:T(8,128)(2,1)S(1)}, bf16[32,4096]{1,0:T(8,128)(2,1)S(1)}, u32[]{:S(2)}, u32[]{:S(2)}) collective-permute-start(bf16[32,4096]{1,0:T(8,128)(2,1)S(1)} %bitcast.52), channel_id=1, source_target_pairs={{0,64},{64,0},{1,65},{65,1},{2,66},{66,2},{3,67},{67,3},{4,68},{68... | collective-permute-start | bytes 786440 | tf_op jit(solution)/shard_map/ppermute | solution.py:221
  47.7 3.1 dynamic-slice_bitcast_fusion
  50.8 2.3 collective-permute-start.1
  53.1 0.2 copy.8
  53.3 0.1 stack_reshape.3
  53.4 0.0 collective-permute-done.2
  53.4 0.1 pad_maximum_fusion.refs_5_
  53.5 3.1 collective-permute-start.3
  56.6 4.4 %collective-permute-start.4 = (bf16[2,32,4096]{2,1,0:T(8,128)(2,1)S(1)}, bf16[2,32,4096]{2,1,0:T(8,128)(2,1)S(1)}, u32[]{:S(2)}, u32[]{:S(2)}) collective-permute-start(bf16[2,32,4096]{2,1,0:T(8,128)(2,1)S(1)} %pad_maximum_fusion.refs_5_), channel_id=1, source_target_pairs={{0,256},{128,384},{256,0},{384,128},{1,257},{129,385},{257,1},{385... | collective-permute-start | bytes 1572872 | tf_op jit(solution)/shard_map/ppermute | solution.py:225
  61.0 3.1 collective-permute-start.5
  64.0 4.3 %collective-permute-start.6 = (bf16[2,32,4096]{2,1,0:T(8,128)(2,1)S(1)}, bf16[2,32,4096]{2,1,0:T(8,128)(2,1)}, u32[]{:S(2)}, u32[]{:S(2)}) collective-permute-start(bf16[2,32,4096]{2,1,0:T(8,128)(2,1)S(1)} %pad_maximum_fusion.refs_5_), channel_id=1, source_target_pairs={{0,32},{32,0},{1,33},{33,1},{2,34},{34,2},{3,35},{35,3},{4,36},{36... | collective-permute-start | bytes 1572872 | tf_op jit(solution)/shard_map/ppermute | solution.py:221
  68.4 0.2 collective-permute-done.3.refs_6_
  68.6 5.3 %collective-permute-start.7 = (bf16[2,32,4096]{2,1,0:T(8,128)(2,1)S(1)}, bf16[2,32,4096]{2,1,0:T(8,128)(2,1)}, u32[]{:S(2)}, u32[]{:S(2)}) collective-permute-start(bf16[2,32,4096]{2,1,0:T(8,128)(2,1)S(1)} %collective-permute-done.3.refs_6_), channel_id=1, source_target_pairs={{0,32},{32,0},{1,33},{33,1},{2,34},{34,2},{3,35},{35,3},{4,36},{36... | collective-permute-start | bytes 1572872 | tf_op jit(solution)/shard_map/ppermute | solution.py:221
  73.9 6.8 %collective-permute-done.4.refs_7_ = bf16[2,32,4096]{2,1,0:T(8,128)(2,1)S(1)} collective-permute-done((bf16[2,32,4096]{2,1,0:T(8,128)(2,1)S(1)}, bf16[2,32,4096]{2,1,0:T(8,128)(2,1)S(1)}, u32[]{:S(2)}, u32[]{:S(2)}) %collective-permute-start.4) | collective-permute-done | bytes 524320 | tf_op jit(solution)/shard_map/ppermute | solution.py:225
  80.7 4.3 %collective-permute-start.8 = (bf16[2,32,4096]{2,1,0:T(8,128)(2,1)S(1)}, bf16[2,32,4096]{2,1,0:T(8,128)(2,1)}, u32[]{:S(2)}, u32[]{:S(2)}) collective-permute-start(bf16[2,32,4096]{2,1,0:T(8,128)(2,1)S(1)} %collective-permute-done.4.refs_7_), channel_id=1, source_target_pairs={{0,32},{32,0},{1,33},{33,1},{2,34},{34,2},{3,35},{35,3},{4,36},{36... | collective-permute-start | bytes 1572872 | tf_op jit(solution)/shard_map/ppermute | solution.py:221
  85.1 0.0 collective-permute-done.5.refs_8_
  85.1 1.9 collective-permute-start.9
  87.0 0.6 stack.29.s.refs_0_
  87.6 0.0 collective-permute-done.1.refs_2_.refs_6_
  87.6 1.0 copy-done
  88.6 3.8 %shard_map.76.refs_3_.refs_2_ = f32[64,256]{1,0:T(8,128)} custom-call(s32[5]{0:T(128)} %stack.29.s.refs_0_, bf16[16,64,256]{2,1,0:T(8,128)(2,1)} %all-to-all-done.refs_0_, bf16[2,128,8192]{2,1,0:T(8,128)(2,1)} %bitcast.36, bf16[128,4096]{1,0:T(8,128)(2,1)} %copy-done), custom_call_target="tpu_custom_call" | custom-call | tf_op jit(solution)/shard_map/pallas_call | solution.py:183
  92.4 0.0 collective-permute-done.6.refs_9_
  92.4 0.0 collective-permute-done.7.refs_10_
  92.4 0.0 collective-permute-done.8.refs_11_
  92.5 0.0 copy-start.8
  92.5 9.7 %shard_map.78.refs_0_ = bf16[256,512]{1,0:T(8,128)(2,1)} custom-call(s32[5]{0:T(128)} %stack.29.s.refs_0_, bf16[2,128,8192]{2,1,0:T(8,128)(2,1)} %bitcast.37, bf16[128,4096]{1,0:T(8,128)(2,1)} %copy-done, f32[64,256]{1,0:T(8,128)} %shard_map.76.refs_3_.refs_2_, bf16[2,128,512]{2,1,0:T(8,128)(2,1)} %bitcast.44, bf16[2,32,4096]{2,1,0:T(8,128)(2,1)} %copy-done.3, ...), custom_call_target="tpu_custom_call" | custom-call | tf_op jit(solution)/shard_map/pallas_call | solution.py:206
  102.1 3.0 collective-permute-start.11
  105.1 2.3 collective-permute-start.12
  107.4 5.6 %collective-permute-done.12.refs_3_ = f32[64,256]{1,0:T(8,128)S(1)} collective-permute-done((f32[64,256]{1,0:T(8,128)S(1)}, f32[64,256]{1,0:T(8,128)S(1)}, u32[]{:S(2)}, u32[]{:S(2)}) %collective-permute-start.12) | collective-permute-done | bytes 65568 | tf_op jit(solution)/shard_map/ppermute | solution.py:221
  113.0 0.0 collective-permute-done.11.refs_1_
  113.0 0.6 copy-done.13
  113.6 0.1 copy-done.11
  113.7 5.6 %shard_map.79 = bf16[16,80,256]{2,1,0:T(8,128)(2,1)} custom-call(s32[5]{0:T(128)} %stack.29.s.refs_0_, bf16[256,512]{1,0:T(8,128)(2,1)} %shard_map.78.refs_0_, bf16[256,512]{1,0:T(8,128)(2,1)} %copy-done.11, f32[64,256]{1,0:T(8,128)} %shard_map.76.refs_3_.refs_2_, f32[64,256]{1,0:T(8,128)} %copy-done.13, f32[16,8,256]{2,1,0:T(8,128)} %bitcast.48, ...), custom_call_target="tpu_custom_call" | custom-call | tf_op jit(solution)/shard_map/pallas_call | solution.py:183
  119.3 11.4 %all-to-all-start.2 = ((bf16[16,80,256]{2,1,0:T(8,128)(2,1)}), bf16[16,80,256]{2,1,0:T(8,128)(2,1)S(1)}, u32[]{:S(2)}, u32[]{:S(2)}) async-start(bf16[16,80,256]{2,1,0:T(8,128)(2,1)} %shard_map.79), calls=%async_computation.2 | async-start | bytes 1310720 | tf_op jit(solution)/shard_map/all_to_all | solution.py:229
  130.7 1.3 dynamic-slice_bitcast_fusion.2.refs_2_
  132.0 27.4 %all-to-all-done.2.refs_0_ = bf16[16,80,256]{2,1,0:T(8,128)(2,1)S(1)} async-done(((bf16[16,80,256]{2,1,0:T(8,128)(2,1)}), bf16[16,80,256]{2,1,0:T(8,128)(2,1)S(1)}, u32[]{:S(2)}, u32[]{:S(2)}) %all-to-all-start.2) | async-done | bytes 655392 | tf_op jit(solution)/shard_map/all_to_all | solution.py:229
  159.4 0.8 copy-done.4
  160.2 2.1 shard_map.80
  162.3 12.2 %all-to-all-start.3 = ((bf16[16,80,256]{2,1,0:T(8,128)(2,1)}), bf16[16,80,256]{2,1,0:T(8,128)(2,1)S(1)}, u32[]{:S(2)}, u32[]{:S(2)}) async-start(bf16[16,80,256]{2,1,0:T(8,128)(2,1)} %get-tuple-element.10), calls=%async_computation.3 | async-start | bytes 1310720 | tf_op jit(solution)/shard_map/all_to_all | solution.py:229
  174.5 3.0 collective-permute-start
  177.5 22.6 %collective-permute-done.refs_2_.refs_6_ = bf16[128,4096]{1,0:T(8,128)(2,1)S(1)} collective-permute-done((bf16[128,4096]{1,0:T(8,128)(2,1)S(1)}, bf16[128,4096]{1,0:T(8,128)(2,1)S(1)}, u32[]{:S(2)}, u32[]{:S(2)}) %collective-permute-start) | collective-permute-done | bytes 1048608 | tf_op jit(solution)/shard_map/ppermute | solution.py:221
  200.1 1.0 copy-done.1
  201.1 9.8 %shard_map.77.refs_0_ = f32[256,512]{1,0:T(8,128)} custom-call(s32[5]{0:T(128)} %stack.29.s.refs_0_, bf16[2,128,8192]{2,1,0:T(8,128)(2,1)} %bitcast.39, bf16[128,4096]{1,0:T(8,128)(2,1)} %copy-done.1, f32[64,256]{1,0:T(8,128)} %shard_map.76.refs_3_.refs_2_, bf16[2,128,512]{2,1,0:T(8,128)(2,1)} %bitcast.45, bf16[2,32,4096]{2,1,0:T(8,128)(2,1)} %copy-done.3, ...), custom_call_target="tpu_custom_call" | custom-call | tf_op jit(solution)/shard_map/pallas_call | solution.py:206
  210.9 3.0 collective-permute-start.10
  213.9 0.8 copy-done.2
  214.7 3.9 %shard_map.81.refs_2_ = f32[64,256]{1,0:T(8,128)} custom-call(s32[5]{0:T(128)} %stack.29.s.refs_0_, bf16[16,80,256]{2,1,0:T(8,128)(2,1)} %copy-done.2, bf16[2,128,8192]{2,1,0:T(8,128)(2,1)} %bitcast.40, bf16[128,4096]{1,0:T(8,128)(2,1)} %copy-done.1), custom_call_target="tpu_custom_call" | custom-call | tf_op jit(solution)/shard_map/pallas_call | solution.py:183
  218.6 2.5 collective-permute-start.13
  221.1 3.5 %collective-permute-done.10.refs_1_ = f32[256,512]{1,0:T(8,128)S(1)} collective-permute-done((f32[256,512]{1,0:T(8,128)}, f32[256,512]{1,0:T(8,128)S(1)}, u32[]{:S(2)}, u32[]{:S(2)}) %collective-permute-start.10) | collective-permute-done | bytes 524320 | tf_op jit(solution)/shard_map/ppermute | solution.py:221
  224.5 1.4 collective-permute-done.13.refs_3_
  226.0 0.6 copy-done.12
  226.6 5.7 %shard_map.82 = bf16[16,80,256]{2,1,0:T(8,128)(2,1)} custom-call(s32[5]{0:T(128)} %stack.29.s.refs_0_, f32[256,512]{1,0:T(8,128)} %shard_map.77.refs_0_, f32[256,512]{1,0:T(8,128)} %copy-done.10, f32[64,256]{1,0:T(8,128)} %shard_map.81.refs_2_, f32[64,256]{1,0:T(8,128)} %copy-done.12, bf16[16,80,256]{2,1,0:T(8,128)(2,1)} %copy-done.2, ...), custom_call_target="tpu_custom_call" | custom-call | tf_op jit(solution)/shard_map/pallas_call | solution.py:183
  232.3 42.3 %all_to_all.35.refs_0_ = bf16[16,80,256]{2,1,0:T(8,128)(2,1)} all-to-all(bf16[16,80,256]{2,1,0:T(8,128)(2,1)} %shard_map.82), channel_id=1, replica_groups=mesh['x'=4,'yh'=2,'c'=2,'yl'=2,'z'=16] {'z'}, dimensions={0} | all-to-all | bytes 1310720 | tf_op jit(solution)/shard_map/all_to_all | solution.py:229
  274.6 1.9 shard_map.83
  276.5 20.8 %all_to_all.36.blocks = f32[16,8,256]{2,1,0:T(8,128)} all-to-all(f32[16,8,256]{2,1,0:T(8,128)} %get-tuple-element.14), channel_id=1, replica_groups=mesh['x'=4,'yh'=2,'c'=2,'yl'=2,'z'=16] {'z'}, dimensions={0} | all-to-all | bytes 262144 | tf_op jit(solution)/shard_map/all_to_all | solution.py:229
  297.2 2.4 shard_map.84
  299.7 22.2 %all_to_all.37.parts = f32[16,32,256]{2,1,0:T(8,128)} all-to-all(f32[16,32,256]{2,1,0:T(8,128)} %bitcast.51), channel_id=1, replica_groups=mesh['x'=4,'yh'=2,'c'=2,'yl'=2,'z'=16] {'x','yh','c'}, dimensions={0} | all-to-all | bytes 1048576 | tf_op jit(solution)/shard_map/all_to_all | solution.py:299
  321.9 1.7 shard_map.85
  (24 shorter events, 0.1 us)
Async XLA Ops:
  2.1 29.5 %all-to-all-start.1 = ((bf16[16,32,256]{2,1,0:T(8,128)(2,1)}), bf16[16,32,256]{2,1,0:T(8,128)(2,1)S(1)}, u32[]{:S(2)}, u32[]{:S(2)}) async-start(bf16[16,32,256]{2,1,0:T(8,128)(2,1)} %broadcast_in_dim.13), calls=%async_computation.1 | async-start | bytes 524288 | tf_op jit(solution)/shard_map/all_to_all | solution.py:229
  32.5 55.1 %all-to-all-start = ((bf16[16,64,256]{2,1,0:T(8,128)(2,1)}), bf16[16,64,256]{2,1,0:T(8,128)(2,1)}, u32[]{:S(2)}, u32[]{:S(2)}) async-start(bf16[16,64,256]{2,1,0:T(8,128)(2,1)} %broadcast_in_dim.12), calls=%async_computation | async-start | bytes 1048576 | tf_op jit(solution)/shard_map/all_to_all | solution.py:229
  42.9 10.5 %collective-permute-start.2 = (bf16[32,4096]{1,0:T(8,128)(2,1)S(1)}, bf16[32,4096]{1,0:T(8,128)(2,1)S(1)}, u32[]{:S(2)}, u32[]{:S(2)}) collective-permute-start(bf16[32,4096]{1,0:T(8,128)(2,1)S(1)} %bitcast.52), channel_id=1, source_target_pairs={{0,64},{64,0},{1,65},{65,1},{2,66},{66,2},{3,67},{67,3},{4,68},{68... | collective-permute-start | bytes 786440 | tf_op jit(solution)/shard_map/ppermute | solution.py:221
  50.8 36.8 %collective-permute-start.1 = (bf16[128,4096]{1,0:T(8,128)(2,1)}, bf16[128,4096]{1,0:T(8,128)(2,1)S(1)}, u32[]{:S(2)}, u32[]{:S(2)}) collective-permute-start(bf16[128,4096]{1,0:T(8,128)(2,1)} %get-tuple-element.17), channel_id=1, source_target_pairs={{0,16},{16,0},{1,17},{17,1},{2,18},{18,2},{3,19},{19,3},{4,20},{20... | collective-permute-start | bytes 3145736 | tf_op jit(solution)/shard_map/ppermute | solution.py:221
  53.5 38.9 %copy-start.3 = (bf16[2,32,4096]{2,1,0:T(8,128)(2,1)}, bf16[2,32,4096]{2,1,0:T(8,128)(2,1)S(1)}, u32[]{:S(2)}) copy-start(bf16[2,32,4096]{2,1,0:T(8,128)(2,1)S(1)} %pad_maximum_fusion.refs_5_) | copy-start | bytes 1572868
  53.5 15.1 %collective-permute-start.3 = (bf16[2,32,4096]{2,1,0:T(8,128)(2,1)S(1)}, bf16[2,32,4096]{2,1,0:T(8,128)(2,1)S(1)}, u32[]{:S(2)}, u32[]{:S(2)}) collective-permute-start(bf16[2,32,4096]{2,1,0:T(8,128)(2,1)S(1)} %pad_maximum_fusion.refs_5_), channel_id=1, source_target_pairs={{0,128},{128,256},{256,384},{384,0},{1,129},{129,257},{257,385},{3... | collective-permute-start | bytes 1572872 | tf_op jit(solution)/shard_map/ppermute | solution.py:225
  56.6 24.1 %collective-permute-start.4 = (bf16[2,32,4096]{2,1,0:T(8,128)(2,1)S(1)}, bf16[2,32,4096]{2,1,0:T(8,128)(2,1)S(1)}, u32[]{:S(2)}, u32[]{:S(2)}) collective-permute-start(bf16[2,32,4096]{2,1,0:T(8,128)(2,1)S(1)} %pad_maximum_fusion.refs_5_), channel_id=1, source_target_pairs={{0,256},{128,384},{256,0},{384,128},{1,257},{129,385},{257,1},{385... | collective-permute-start | bytes 1572872 | tf_op jit(solution)/shard_map/ppermute | solution.py:225
  61.0 24.1 %collective-permute-start.5 = (bf16[2,32,4096]{2,1,0:T(8,128)(2,1)S(1)}, bf16[2,32,4096]{2,1,0:T(8,128)(2,1)S(1)}, u32[]{:S(2)}, u32[]{:S(2)}) collective-permute-start(bf16[2,32,4096]{2,1,0:T(8,128)(2,1)S(1)} %pad_maximum_fusion.refs_5_), channel_id=1, source_target_pairs={{0,384},{128,0},{256,128},{384,256},{1,385},{129,1},{257,129},{385... | collective-permute-start | bytes 1572872 | tf_op jit(solution)/shard_map/ppermute | solution.py:225
  64.0 28.3 %collective-permute-start.6 = (bf16[2,32,4096]{2,1,0:T(8,128)(2,1)S(1)}, bf16[2,32,4096]{2,1,0:T(8,128)(2,1)}, u32[]{:S(2)}, u32[]{:S(2)}) collective-permute-start(bf16[2,32,4096]{2,1,0:T(8,128)(2,1)S(1)} %pad_maximum_fusion.refs_5_), channel_id=1, source_target_pairs={{0,32},{32,0},{1,33},{33,1},{2,34},{34,2},{3,35},{35,3},{4,36},{36... | collective-permute-start | bytes 1572872 | tf_op jit(solution)/shard_map/ppermute | solution.py:221
  68.6 23.8 %copy-start.5 = (bf16[2,32,4096]{2,1,0:T(8,128)(2,1)}, bf16[2,32,4096]{2,1,0:T(8,128)(2,1)S(1)}, u32[]{:S(2)}) copy-start(bf16[2,32,4096]{2,1,0:T(8,128)(2,1)S(1)} %collective-permute-done.3.refs_6_) | copy-start | bytes 1572868
  68.6 23.8 %collective-permute-start.7 = (bf16[2,32,4096]{2,1,0:T(8,128)(2,1)S(1)}, bf16[2,32,4096]{2,1,0:T(8,128)(2,1)}, u32[]{:S(2)}, u32[]{:S(2)}) collective-permute-start(bf16[2,32,4096]{2,1,0:T(8,128)(2,1)S(1)} %collective-permute-done.3.refs_6_), channel_id=1, source_target_pairs={{0,32},{32,0},{1,33},{33,1},{2,34},{34,2},{3,35},{35,3},{4,36},{36... | collective-permute-start | bytes 1572872 | tf_op jit(solution)/shard_map/ppermute | solution.py:221
  80.7 11.7 %copy-start.6 = (bf16[2,32,4096]{2,1,0:T(8,128)(2,1)}, bf16[2,32,4096]{2,1,0:T(8,128)(2,1)S(1)}, u32[]{:S(2)}) copy-start(bf16[2,32,4096]{2,1,0:T(8,128)(2,1)S(1)} %collective-permute-done.4.refs_7_) | copy-start | bytes 1572868
  80.7 11.7 %collective-permute-start.8 = (bf16[2,32,4096]{2,1,0:T(8,128)(2,1)S(1)}, bf16[2,32,4096]{2,1,0:T(8,128)(2,1)}, u32[]{:S(2)}, u32[]{:S(2)}) collective-permute-start(bf16[2,32,4096]{2,1,0:T(8,128)(2,1)S(1)} %collective-permute-done.4.refs_7_), channel_id=1, source_target_pairs={{0,32},{32,0},{1,33},{33,1},{2,34},{34,2},{3,35},{35,3},{4,36},{36... | collective-permute-start | bytes 1572872 | tf_op jit(solution)/shard_map/ppermute | solution.py:221
  85.1 7.4 %copy-start.7 = (bf16[2,32,4096]{2,1,0:T(8,128)(2,1)}, bf16[2,32,4096]{2,1,0:T(8,128)(2,1)S(1)}, u32[]{:S(2)}) copy-start(bf16[2,32,4096]{2,1,0:T(8,128)(2,1)S(1)} %collective-permute-done.5.refs_8_) | copy-start | bytes 1572868
  85.1 7.3 %collective-permute-start.9 = (bf16[2,32,4096]{2,1,0:T(8,128)(2,1)S(1)}, bf16[2,32,4096]{2,1,0:T(8,128)(2,1)}, u32[]{:S(2)}, u32[]{:S(2)}) collective-permute-start(bf16[2,32,4096]{2,1,0:T(8,128)(2,1)S(1)} %collective-permute-done.5.refs_8_), channel_id=1, source_target_pairs={{0,32},{32,0},{1,33},{33,1},{2,34},{34,2},{3,35},{35,3},{4,36},{36... | collective-permute-start | bytes 1572872 | tf_op jit(solution)/shard_map/ppermute | solution.py:221
  87.6 1.0 copy-start
  92.5 12.7 %copy-start.8 = (f32[64,256]{1,0:T(8,128)S(1)}, f32[64,256]{1,0:T(8,128)}, u32[]{:S(2)}) copy-start(f32[64,256]{1,0:T(8,128)} %shard_map.76.refs_3_.refs_2_) | copy-start | bytes 196612
  102.1 10.9 %collective-permute-start.11 = (bf16[256,512]{1,0:T(8,128)(2,1)}, bf16[256,512]{1,0:T(8,128)(2,1)S(1)}, u32[]{:S(2)}, u32[]{:S(2)}) collective-permute-start(bf16[256,512]{1,0:T(8,128)(2,1)} %shard_map.78.refs_0_), channel_id=1, source_target_pairs={{0,16},{16,0},{1,17},{17,1},{2,18},{18,2},{3,19},{19,3},{4,20},{20... | collective-permute-start | bytes 786440 | tf_op jit(solution)/shard_map/ppermute | solution.py:221
  105.1 7.9 %collective-permute-start.12 = (f32[64,256]{1,0:T(8,128)S(1)}, f32[64,256]{1,0:T(8,128)S(1)}, u32[]{:S(2)}, u32[]{:S(2)}) collective-permute-start(f32[64,256]{1,0:T(8,128)S(1)} %copy-done.8), channel_id=1, source_target_pairs={{0,16},{16,0},{1,17},{17,1},{2,18},{18,2},{3,19},{19,3},{4,20},{20... | collective-permute-start | bytes 196616 | tf_op jit(solution)/shard_map/ppermute | solution.py:221
  113.0 0.6 copy-start.13
  113.0 0.7 copy-start.11
  113.7 60.8 %copy-start.9 = (bf16[128,4096]{1,0:T(8,128)(2,1)S(1)}, bf16[128,4096]{1,0:T(8,128)(2,1)}, u32[]{:S(2)}) copy-start(bf16[128,4096]{1,0:T(8,128)(2,1)} %get-tuple-element.18) | copy-start | bytes 3145732
  119.3 40.1 %all-to-all-start.2 = ((bf16[16,80,256]{2,1,0:T(8,128)(2,1)}), bf16[16,80,256]{2,1,0:T(8,128)(2,1)S(1)}, u32[]{:S(2)}, u32[]{:S(2)}) async-start(bf16[16,80,256]{2,1,0:T(8,128)(2,1)} %shard_map.79), calls=%async_computation.2 | async-start | bytes 1310720 | tf_op jit(solution)/shard_map/all_to_all | solution.py:229
  159.4 0.8 copy-start.4
  162.3 51.5 %all-to-all-start.3 = ((bf16[16,80,256]{2,1,0:T(8,128)(2,1)}), bf16[16,80,256]{2,1,0:T(8,128)(2,1)S(1)}, u32[]{:S(2)}, u32[]{:S(2)}) async-start(bf16[16,80,256]{2,1,0:T(8,128)(2,1)} %get-tuple-element.10), calls=%async_computation.3 | async-start | bytes 1310720 | tf_op jit(solution)/shard_map/all_to_all | solution.py:229
  174.5 25.5 %collective-permute-start = (bf16[128,4096]{1,0:T(8,128)(2,1)S(1)}, bf16[128,4096]{1,0:T(8,128)(2,1)S(1)}, u32[]{:S(2)}, u32[]{:S(2)}) collective-permute-start(bf16[128,4096]{1,0:T(8,128)(2,1)S(1)} %copy-done.9), channel_id=1, source_target_pairs={{0,16},{16,0},{1,17},{17,1},{2,18},{18,2},{3,19},{19,3},{4,20},{20... | collective-permute-start | bytes 3145736 | tf_op jit(solution)/shard_map/ppermute | solution.py:221
  200.1 1.0 copy-start.1
  210.9 13.7 %collective-permute-start.10 = (f32[256,512]{1,0:T(8,128)}, f32[256,512]{1,0:T(8,128)S(1)}, u32[]{:S(2)}, u32[]{:S(2)}) collective-permute-start(f32[256,512]{1,0:T(8,128)} %shard_map.77.refs_0_), channel_id=1, source_target_pairs={{0,16},{16,0},{1,17},{17,1},{2,18},{18,2},{3,19},{19,3},{4,20},{20... | collective-permute-start | bytes 1572872 | tf_op jit(solution)/shard_map/ppermute | solution.py:221
  213.9 0.8 copy-start.2
  218.6 7.4 %collective-permute-start.13 = (f32[64,256]{1,0:T(8,128)}, f32[64,256]{1,0:T(8,128)S(1)}, u32[]{:S(2)}, u32[]{:S(2)}) collective-permute-start(f32[64,256]{1,0:T(8,128)} %shard_map.81.refs_2_), channel_id=1, source_target_pairs={{0,16},{16,0},{1,17},{17,1},{2,18},{18,2},{3,19},{19,3},{4,20},{20... | collective-permute-start | bytes 196616 | tf_op jit(solution)/shard_map/ppermute | solution.py:221
  224.5 1.4 copy-start.10
  225.9 0.6 copy-start.12

commit v3 on v2

v3 whole, which is shorter than its diff:
```python
import jax
import jax.numpy as jnp
from jax import lax
from jax.experimental import pallas as pl
from jax.experimental.pallas import tpu as pltpu
from jax.sharding import Mesh
from jax.sharding import PartitionSpec as P

W = ("x", "yh", "c")
F = ("yl", "zh", "zl")
Q = ("yl", "zl")
NZ = 8


branch_scale = 0.25
rate_down = 200.0
rate_up = 20.0

bf16 = jnp.bfloat16
f32 = jnp.float32
HIGH = lax.Precision.HIGHEST
VMEM = pltpu.CompilerParams(vmem_limit_bytes=60 * 1024 * 1024)


def dot(a, b, ca, cb, precision=None):
    return lax.dot_general(a, b, (((ca,), (cb,)), ((), ())), precision=precision, preferred_element_type=f32)


def split(value):
    hi = value.astype(bf16)
    return hi, (value - hi.astype(f32)).astype(bf16)


def vmem(n):
    return [pl.BlockSpec(memory_space=pltpu.VMEM)] * n


def hbm(n):
    return [pl.BlockSpec(memory_space=pl.ANY)] * n


def smem():
    return pl.BlockSpec(memory_space=pltpu.SMEM)


def in_order(flag, first, second, axis):
    return jnp.concatenate([jnp.where(flag == 0, first, second), jnp.where(flag == 0, second, first)], axis=axis)


def pack_kernel(step, idx, x_ref, *rest):
    outs, sems = rest[:4], rest[4]
    yl, zl = idx[3], idx[5]
    n = 256
    copies = []
    for k, out in enumerate(outs):
        a, b = k % 2, k // 2
        start = lax.rem(yl + a, 2) * (2 * NZ * n) + lax.rem(zl + b, 2) * n
        for z in range(NZ):
            copies.append(
                pltpu.make_async_copy(
                    x_ref.at[step, :, pl.ds(pl.multiple_of(start + z * 2 * n, n), n)],
                    out.at[:, z * n : (z + 1) * n],
                    sems.at[k * NZ + z],
                )
            )
    for copy in copies:
        copy.start()
    for copy in copies:
        copy.wait()


def low_kernel(scale, idx, whole, own, gy, gz, gd, out):
    yl, zl = idx[3], idx[5]
    n = whole.shape[2]
    pairs = []
    for pair in ((own, gy), (gz, gd)):
        parts = []
        for piece in pair:
            part = dot(whole[0, :64], piece[:, :n], 1, 1)
            for z in range(1, NZ):
                part = part + dot(whole[z, :64], piece[:, z * n : (z + 1) * n], 1, 1)
            parts.append(part * scale)
        pairs.append(in_order(yl, *parts, axis=1))
    for y in range(2):
        out[2 * y + zl] = pairs[0]
        out[2 * y + 1 - zl] = pairs[1]


def keys_kernel(step, scale, idx, *rest):
    x_refs, y_ref, pieces = rest[:4], rest[5], rest[6:14]
    outs, (xs, bs, xsem, bsem) = rest[14:-4], rest[-4:]
    rows, quarter = xs.shape[2:]
    px, pyh, pc, yl, zl = idx[0], idx[1], idx[2], idx[3], idx[5]
    copies = []
    for k, ref in enumerate(x_refs):
        at = xs.at[lax.rem(zl + k // 2, 2), lax.rem(yl + k % 2, 2)]
        copies.append(pltpu.make_async_copy(ref, at, xsem.at[k]))
    loads = []
    for k, piece in enumerate(pieces):
        dc, dx = divmod(k, 4)
        for dy in range(2):
            w = lax.rem(pyh + dy, 2) * 2 + lax.rem(pc + dc, 2)
            loads.append(pltpu.make_async_copy(piece.at[dy], bs.at[dx, w], bsem.at[k * 2 + dy]))
    for copy in copies + loads:
        copy.start()
    for copy in copies:
        copy.wait()
    tokens = xs[...].reshape(4 * rows, quarter)
    for dx in range(4):
        for k in (dx, dx + 4):
            for dy in range(2):
                loads[k * 2 + dy].wait()
        at = pl.ds(pl.multiple_of(lax.rem(px + 4 - dx, 4) * 128, 128), 128)
        part = dot(tokens, bs[dx].reshape(128, quarter), 1, 1) * scale
        wanted = y_ref[step, :, at].astype(f32)
        less = [jnp.where(2 * zl + yl == q, wanted, 0.0) for q in range(4)]
        part = (part - jnp.concatenate(less, axis=0)).astype(bf16)
        pairs = part[: 2 * rows], part[2 * rows :]
        if len(outs) == 1:
            for y in range(2):
                for z in range(2):
                    outs[0][2 * y + z, :, at] = pairs[z]
        else:
            outs[0][:, at] = jnp.where(zl == 0, pairs[0], pairs[1])
            outs[1][:, at] = jnp.where(zl == 0, pairs[1], pairs[0])


def joined(blocks):
    return jnp.concatenate([jnp.concatenate([blocks[z, :8], blocks[z, 8:]], axis=1) for z in range(NZ)], axis=0)


def error_kernel(total_rows, low_parts, blocks, *rest):
    keys_parts, out = rest[:-1], rest[-1]
    if blocks.shape[1] == 16:
        up = joined(blocks[...])
    else:
        up = joined(blocks[:, 64:80].astype(f32) + blocks[:, 80:96].astype(f32))
    if len(keys_parts) == 1:
        keys_parts = [keys_parts[0].at[q] for q in range(4)]
    k = [part[...].astype(f32) for part in keys_parts]
    low = (low_parts[0] + low_parts[1]) + (low_parts[2] + low_parts[3])
    keys = (k[0] + k[1]) + (k[2] + k[3])
    error = (keys + branch_scale * dot(low, up, 0, 0, HIGH)) / total_rows
    tokens = error.shape[0]
    out[:, :tokens] = (branch_scale * dot(up, error, 1, 1, HIGH)).astype(bf16)
    out[:, tokens:] = (branch_scale * dot(low, error, 1, 0, HIGH)).astype(bf16)


def down_kernel(idx, mine, got, own, gy, gz, gd, out):
    yl = idx[3]
    rows = own.shape[0]
    backs = []
    for half in (mine, got):
        first, second = half[:, :rows], half[:, rows : 2 * rows]
        backs += [jnp.where(yl == 0, first, second), jnp.where(yl == 0, second, first)]
    up = (mine[:, 2 * rows :].astype(f32) + got[:, 2 * rows :].astype(f32)).astype(bf16)
    n = out.shape[2]
    for z in range(NZ):
        at = slice(z * n, (z + 1) * n)
        part = dot(backs[0], own[:, at], 1, 0) + dot(backs[1], gy[:, at], 1, 0)
        part = part + (dot(backs[2], gz[:, at], 1, 0) + dot(backs[3], gd[:, at], 1, 0))
        out[z, :64] = part.astype(bf16)
        out[z, 64:72] = up[8 * z : 8 * z + 8, :n]
        out[z, 72:80] = up[8 * z : 8 * z + 8, n:]


def summed(parts):
    result = parts[0].astype(f32)
    for k in range(1, parts.shape[0]):
        result = result + parts[k].astype(f32)
    return result


def update_kernel(scale, parts, a_ref, b_ref, a_out, b_out, copies):
    grads = summed(parts)
    a = a_ref[...] - (rate_down * scale) * grads[:64]
    hi, lo = split(b_ref[...] - rate_up * grads[64:])
    a_out[...] = a
    b_out[...] = hi.astype(f32) + lo.astype(f32)
    a_half = a.astype(bf16)
    for z in range(NZ):
        copies[z, :64] = a_half
        copies[z, 64:80] = hi
        copies[z, 80:96] = lo


def last_update_kernel(scale, parts, a_ref, b_ref, a_out, copies):
    grads = summed(parts)
    a_out[...] = a_ref[...] - (rate_down * scale) * grads[:64]
    b = b_ref[...] - rate_up * grads[64:]
    for z in range(NZ):
        copies[z] = b


def change_kernel(a_ref, blocks, a_start, blocks_start, out, b_out):
    up = joined(blocks[...])
    left = jnp.concatenate([up, -joined(blocks_start[...])], axis=0)
    right = jnp.concatenate([a_ref[...], a_start[...]], axis=0)
    out[...] = branch_scale * dot(left, right, 0, 0, HIGH)
    b_out[...] = up


def merge_kernel(parts, base, out):
    out[...] = base[...] + summed(parts) * (1.0 / parts.shape[0])


def shaped(dims, kind):
    return jax.ShapeDtypeStruct(dims, kind)


def call(kernel, shapes, *args):
    return pl.pallas_call(kernel, out_shape=shapes, in_specs=vmem(len(args)), compiler_params=VMEM)(*args)


def call_at(kernel, shapes, idx, *args):
    return pl.pallas_call(
        kernel, out_shape=shapes, in_specs=[smem()] + vmem(len(args)), compiler_params=VMEM
    )(idx, *args)


def pack(step, idx, tokens):
    def body(*refs):
        pack_kernel(step, *refs)

    rows, quarter = tokens.shape[1], tokens.shape[2] // 4
    return pl.pallas_call(
        body,
        out_shape=[shaped((rows, quarter), bf16)] * 4,
        in_specs=[smem()] + hbm(1),
        out_specs=hbm(4),
        scratch_shapes=[pltpu.SemaphoreType.DMA((4 * NZ,))],
        compiler_params=VMEM,
    )(idx, tokens)


def keys_of(step, scale, idx, xs, after, targets, pieces, shapes):
    rows, quarter = xs[0].shape

    def body(*refs):
        keys_kernel(step, scale, *refs)

    return pl.pallas_call(
        body,
        out_shape=shapes,
        in_specs=[smem()] + hbm(5) + vmem(1) + hbm(8),
        scratch_shapes=[
            pltpu.VMEM((2, 2, rows, quarter), bf16),
            pltpu.VMEM((4, 4, 32, quarter), bf16),
            pltpu.SemaphoreType.DMA((4,)),
            pltpu.SemaphoreType.DMA((16,)),
        ],
        compiler_params=VMEM,
    )(idx, *xs, after, targets, *pieces)


def swap(value, axis):
    return lax.ppermute(value, axis, [(0, 1), (1, 0)])


def swap_both(value):
    return lax.ppermute(value, Q, [(k, 3 - k) for k in range(4)])


def shift(value, axis, by, count):
    return lax.ppermute(value, axis, [(i, (i + by) % count) for i in range(count)])


def exchange(parts, axis):
    return lax.all_to_all(parts, axis, 0, 0, tiled=True)


def gather_z(value):
    return exchange(jnp.broadcast_to(value, (NZ, *value.shape)), "zh")


def whole_step(inputs, targets, base, adapter_a, adapter_b):
    tokens = inputs[0]
    a_start = adapter_a[0]
    _, rows, width = tokens.shape
    scale = width ** (-0.5)
    total_rows = float(rows * 4 * NZ)
    idx = jnp.stack([lax.axis_index(n) for n in (*W, *F[:1], "zh", "zl")]).astype(jnp.int32)
    blocks = adapter_b[0].T.reshape(NZ, 8, 2, 256).transpose(0, 2, 1, 3).reshape(NZ, 16, 256)
    block = lax.dynamic_index_in_dim(blocks, lax.axis_index("zh"), 0, keepdims=False)

    def quarters(step):
        own, to_y, to_z, to_both = pack(step, idx, tokens)
        return (own, swap(to_y, "yl"), swap(to_z, "zl"), swap_both(to_both))

    x0 = quarters(0)
    cols = gather_z(base.T.astype(bf16))
    cols = cols.transpose(1, 0, 2).reshape(cols.shape[1], width // 4)
    pair = jnp.stack([cols, swap(cols, "yh")])
    near = [pair] + [shift(pair, "x", d, 4) for d in (1, 2, 3)]
    whole = gather_z(a_start.astype(bf16))
    pieces = near + [swap(piece, "c") for piece in near]
    x1 = quarters(1)

    low_shape = shaped((4, 64, 2 * rows), f32)
    down_shape = shaped((NZ, 80, 256), bf16)

    def lows(whole, xs):
        part = call_at(lambda *refs: low_kernel(scale, *refs), low_shape, idx, whole, *xs)
        return exchange(part, Q)

    def gradients(xs, *args):
        mine = call(
            lambda *refs: error_kernel(total_rows, *refs), shaped((64, 2 * rows + 512), bf16), *args
        )
        got = swap(mine, "zl")
        return exchange(call_at(down_kernel, down_shape, idx, mine, got, *xs), "zh")

    low = lows(whole, x0)
    keys_shape = shaped((2 * rows, 512), bf16)
    keys = keys_of(0, scale, idx, x0, low, targets[0], pieces, shaped((4, *keys_shape.shape), bf16))
    keys = exchange(keys, Q)
    parts = gradients(x0, low, blocks, keys)

    own, other = keys_of(1, scale, idx, x1, low, targets[0], pieces, (keys_shape, keys_shape))
    keys = (own, swap(own, "yl"), swap(other, "zl"), swap_both(other))
    a_next, block, copies = call(
        lambda *refs: update_kernel(scale, *refs),
        (shaped((64, 256), f32), shaped((16, 256), f32), shaped((NZ, 96, 256), bf16)),
        parts,
        a_start,
        block,
    )
    whole = exchange(copies, "zh")
    low = lows(whole, x1)
    parts = gradients(x1, low, whole, *keys)
    a_last, copies = call(
        lambda *refs: last_update_kernel(scale, *refs),
        (shaped((64, 256), f32), shaped((NZ, 16, 256), f32)),
        parts,
        a_next,
        block,
    )
    blocks_last = exchange(copies, "zh")
    change, b_last = call(
        change_kernel, (shaped((512, 256), f32), shaped((64, 512), f32)), a_last, blocks_last, a_start, blocks
    )
    merged = exchange(change.reshape(16, 32, 256), W)
    new_base = call(merge_kernel, shaped(base.shape[::-1], f32), merged, base.T)
    return (new_base.T, a_last[None], b_last.T[None])


def solution(mesh):
    finer = Mesh(mesh.devices.reshape(4, 2, 2, 2, NZ, 2), (*W, *F))
    return jax.shard_map(
        whole_step,
        mesh=finer,
        in_specs=(
            P(W, None, F, None),
            P(W, None, F, None),
            P(F, W),
            P(W, None, F),
            P(W, None, None),
        ),
        out_specs=(P(F, W), P(W, None, F), P(W, None, None)),
        check_vma=False,
    )
```

time: 325 us -> 465 us (1.43)
  Pallas kernels: 46.6 us -> 176 us
  starting transfers between devices: 96.9 us -> 106 us
    pallas_call x6 -> x8, Pallas kernels: 38.4 us -> 162 us  [the longest x2 131 us: pack(): pl.pallas_call(body, out_shape=[shaped((rows, quarter), bf16)] * 4, in_sp...]
    ppermute x0 -> x3, waiting for transfers between devices: none -> 29.7 us  [swap_both(): return lax.ppermute(value, Q, [(k, 3 - k) for k in range(4)])]
    ppermute x11 -> x13, waiting for transfers between devices: 33 us -> 19.8 us  [swap(): return lax.ppermute(value, axis, [(0, 1), (1, 0)])]
    all_to_all x4 -> x6, waiting for transfers between devices: 40.3 us -> 29 us  [exchange(): return lax.all_to_all(parts, axis, 0, 0, tiled=True)]
    ppermute x3, waiting for transfers between devices: 7.04 us -> 0.01 us  [shift(): lax.ppermute(value, axis, [(i, (i + by) % count) for i in range(count)])]
    ppermute x0 -> x3, starting transfers between devices: none -> 6.88 us  [swap_both(): return lax.ppermute(value, Q, [(k, 3 - k) for k in range(4)])]
    pallas_call x4 -> x6, Pallas kernels: 8.13 us -> 14.6 us  [call(): pl.pallas_call(kernel, out_shape=shapes, in_specs=vmem(len(args)), compil...]
    ppermute x11 -> x13, starting transfers between devices: 36.7 us -> 42.1 us  [swap(): return lax.ppermute(value, axis, [(0, 1), (1, 0)])]
  transfers between devices with their start and end apart: 18 -> 25, of which waited for: 8 -> 12; matrix products, arithmetic and copies ran while one was open for 2% -> 1% of each run, Pallas kernels for 5% -> 31%
where the time goes in v3:
time: 465 us; the launch traced here: 463 us
  Pallas kernels  176 us (38%)
  starting transfers between devices  106 us (23%)
  blocking collectives  89 us (19%)
  waiting for transfers between devices  78.6 us (17%)
  local copies, waits for them, and re-layouts  9.51 us (2%)
    pallas_call x2, Pallas kernels, pack(): pl.pallas_call(body, out_shape=[shaped((rows, quarter), bf16)] * 4, in_sp...  131 us
    all_to_all x4, blocking collectives, exchange(): return lax.all_to_all(parts, axis, 0, 0, tiled=True)  89 us
    all_to_all x6, starting transfers between devices, exchange(): return lax.all_to_all(parts, axis, 0, 0, tiled=True)  46.7 us
    ppermute x13, starting transfers between devices, swap(): return lax.ppermute(value, axis, [(0, 1), (1, 0)])  42.1 us
    ppermute x3, waiting for transfers between devices, swap_both(): return lax.ppermute(value, Q, [(k, 3 - k) for k in range(4)])  29.7 us
    all_to_all x6, waiting for transfers between devices, exchange(): return lax.all_to_all(parts, axis, 0, 0, tiled=True)  29 us
    ppermute x13, waiting for transfers between devices, swap(): return lax.ppermute(value, axis, [(0, 1), (1, 0)])  19.8 us
    pallas_call x2, Pallas kernels, keys_of(): pl.pallas_call(body, out_shape=shapes, in_specs=[smem()] + hbm(5) + vmem(...  18.7 us
  transfers between devices with their start and end apart: 25, of which 12 were waited for; matrix products, arithmetic and copies ran while one was open for 1% of the time, Pallas kernels for 31%

profile of v3, /device:TPU:1, one launch (start us, length us, event | category | flops | bytes accessed | tf_op | source)
XLA Modules:
  0.0 462.5 jit_solution(13989537408938902595)
XLA Ops:
  0.6 0.8 bitcast_convert_fusion
  2.1 15.6 %all-to-all-start.2 = ((bf16[8,32,256]{2,1,0:T(8,128)(2,1)}), bf16[8,32,256]{2,1,0:T(8,128)(2,1)S(1)}, u32[]{:S(2)}, u32[]{:S(2)}) async-start(bf16[8,32,256]{2,1,0:T(8,128)(2,1)} %broadcast_in_dim.13), calls=%async_computation.2 | async-start | bytes 262144 | tf_op jit(solution)/shard_map/all_to_all | solution.py:269
  17.7 0.8 bitcast_convert_fusion.1
  18.5 12.3 %all-to-all-done.2 = bf16[8,32,256]{2,1,0:T(8,128)(2,1)S(1)} async-done(((bf16[8,32,256]{2,1,0:T(8,128)(2,1)}), bf16[8,32,256]{2,1,0:T(8,128)(2,1)S(1)}, u32[]{:S(2)}, u32[]{:S(2)}) %all-to-all-start.2) | async-done | bytes 131104 | tf_op jit(solution)/shard_map/all_to_all | solution.py:269
  30.9 0.7 broadcast_in_dim.12
  31.6 4.2 all-to-all-start
  36.4 65.6 %shard_map.76 = (bf16[128,2048]{1,0:T(8,128)(2,1)}, bf16[128,2048]{1,0:T(8,128)(2,1)}, bf16[128,2048]{1,0:T(8,128)(2,1)}, bf16[128,2048]{1,0:T(8,128)(2,1)}) custom-call(s32[6]{0:T(128)} %stack.33.refs_0_.idx, bf16[2,128,8192]{2,1,0:T(8,128)(2,1)} %bitcast.33), custom_call_target="tpu_custom_call" | custom-call | tf_op jit(solution)/shard_map/pallas_call | solution.py:226
  102.0 3.2 collective-permute-start
  105.2 3.0 collective-permute-start.1
  108.2 2.2 collective-permute-start.2
  110.4 4.8 %collective-permute-start.3 = (bf16[32,2048]{1,0:T(8,128)(2,1)S(1)}, bf16[32,2048]{1,0:T(8,128)(2,1)S(1)}, u32[]{:S(2)}, u32[]{:S(2)}) collective-permute-start(bf16[32,2048]{1,0:T(8,128)(2,1)S(1)} %bitcast.46), channel_id=1, source_target_pairs={{0,64},{64,0},{1,65},{65,1},{2,66},{66,2},{3,67},{67,3},{4,68},{68... | collective-permute-start | bytes 393224 | tf_op jit(solution)/shard_map/ppermute | solution.py:257
  115.3 2.2 collective-permute-done.1.refs_4_.refs_3_.gz
  117.5 11.1 %collective-permute-done.2.refs_5_.refs_4_.gd = bf16[128,2048]{1,0:T(8,128)(2,1)S(1)} collective-permute-done((bf16[128,2048]{1,0:T(8,128)(2,1)}, bf16[128,2048]{1,0:T(8,128)(2,1)S(1)}, u32[]{:S(2)}, u32[]{:S(2)}) %collective-permute-start.2) | collective-permute-done | bytes 524320 | tf_op jit(solution)/shard_map/ppermute | solution.py:261
  128.7 0.8 copy-done.2
  129.6 3.2 shard_map.77
  132.7 3.9 all-to-all-start.1
  136.8 3.1 collective-permute-start.4
  140.0 4.4 collective-permute-start.5
  144.3 3.1 collective-permute-start.6
  147.4 6.6 %collective-permute-start.7 = (bf16[2,32,2048]{2,1,0:T(8,128)(2,1)S(1)}, bf16[2,32,2048]{2,1,0:T(8,128)(2,1)S(1)}, u32[]{:S(2)}, u32[]{:S(2)}) collective-permute-start(bf16[2,32,2048]{2,1,0:T(8,128)(2,1)S(1)} %pad_maximum_fusion.refs_7_), channel_id=1, source_target_pairs={{0,32},{32,0},{1,33},{33,1},{2,34},{34,2},{3,35},{35,3},{4,36},{36... | collective-permute-start | bytes 786440 | tf_op jit(solution)/shard_map/ppermute | solution.py:257
  154.1 1.9 collective-permute-start.8
  156.0 2.4 collective-permute-start.9
  158.5 1.9 collective-permute-start.10
  160.4 1.4 collective-permute-done.10.refs_14_
  162.7 9.5 %shard_map.78 = bf16[4,256,512]{2,1,0:T(8,128)(2,1)} custom-call(s32[6]{0:T(128)} %stack.33.refs_0_.idx, bf16[128,2048]{1,0:T(8,128)(2,1)} %get-tuple-element.20.refs_2_.refs_1_.own, bf16[128,2048]{1,0:T(8,128)(2,1)} %copy-done, bf16[128,2048]{1,0:T(8,128)(2,1)} %copy-done.1, bf16[128,2048]{1,0:T(8,128)(2,1)} %copy-done.2, f32[4,64,256]{2,1,0:T(8,128)} %copy-done.6, ...), custom_call_target="tpu_custom_call" | custom-call | tf_op jit(solution)/shard_map/pallas_call | solution.py:242
  172.2 18.6 %all_to_all.50.refs_2_ = bf16[4,256,512]{2,1,0:T(8,128)(2,1)} all-to-all(bf16[4,256,512]{2,1,0:T(8,128)(2,1)} %shard_map.78), channel_id=1, replica_groups=mesh['x'=4,'yh'=2,'c'=2,'yl'=2,'zh'=8,'zl'=2] {'yl','zl'}, dimensions={0} | all-to-all | bytes 2097152 | tf_op jit(solution)/shard_map/all_to_all | solution.py:269
  190.8 3.4 shard_map.79.mine
  194.2 2.9 collective-permute-start.11
  197.1 2.7 collective-permute-done.11.got
  200.4 2.8 shard_map.80
  203.2 11.5 %all-to-all-start.4 = ((bf16[8,80,256]{2,1,0:T(8,128)(2,1)}), bf16[8,80,256]{2,1,0:T(8,128)(2,1)S(1)}, u32[]{:S(2)}, u32[]{:S(2)}) async-start(bf16[8,80,256]{2,1,0:T(8,128)(2,1)} %shard_map.80), calls=%async_computation.4 | async-start | bytes 655360 | tf_op jit(solution)/shard_map/all_to_all | solution.py:269
  214.6 1.3 dynamic-slice_bitcast_fusion.refs_2_
  216.0 16.7 %all-to-all-done.4.refs_0_ = bf16[8,80,256]{2,1,0:T(8,128)(2,1)S(1)} async-done(((bf16[8,80,256]{2,1,0:T(8,128)(2,1)}), bf16[8,80,256]{2,1,0:T(8,128)(2,1)S(1)}, u32[]{:S(2)}, u32[]{:S(2)}) %all-to-all-start.4) | async-done | bytes 327712 | tf_op jit(solution)/shard_map/all_to_all | solution.py:269
  232.7 0.7 copy-done.9
  233.4 1.9 shard_map.81
  235.3 7.9 %all-to-all-start.5 = ((bf16[8,96,256]{2,1,0:T(8,128)(2,1)}), bf16[8,96,256]{2,1,0:T(8,128)(2,1)S(1)}, u32[]{:S(2)}, u32[]{:S(2)}) async-start(bf16[8,96,256]{2,1,0:T(8,128)(2,1)} %get-tuple-element.24), calls=%async_computation.5 | async-start | bytes 786432 | tf_op jit(solution)/shard_map/all_to_all | solution.py:269
  243.1 65.6 %shard_map.82 = (bf16[128,2048]{1,0:T(8,128)(2,1)}, bf16[128,2048]{1,0:T(8,128)(2,1)}, bf16[128,2048]{1,0:T(8,128)(2,1)}, bf16[128,2048]{1,0:T(8,128)(2,1)}) custom-call(s32[6]{0:T(128)} %stack.33.refs_0_.idx, bf16[2,128,8192]{2,1,0:T(8,128)(2,1)} %bitcast.34), custom_call_target="tpu_custom_call" | custom-call | tf_op jit(solution)/shard_map/pallas_call | solution.py:226
  308.7 3.2 collective-permute-start.12
  311.9 3.6 collective-permute-start.13
  315.5 2.4 collective-permute-start.14
  317.9 4.4 collective-permute-done.12.refs_3_.refs_2_.gy
  322.3 3.8 collective-permute-done.13.refs_4_.refs_3_.gz
  326.0 11.8 %collective-permute-done.14.refs_5_.refs_4_.gd = bf16[128,2048]{1,0:T(8,128)(2,1)S(1)} collective-permute-done((bf16[128,2048]{1,0:T(8,128)(2,1)}, bf16[128,2048]{1,0:T(8,128)(2,1)S(1)}, u32[]{:S(2)}, u32[]{:S(2)}) %collective-permute-start.14) | collective-permute-done | bytes 524320 | tf_op jit(solution)/shard_map/ppermute | solution.py:261
  337.9 0.8 copy-done.5
  338.8 3.2 shard_map.83
  342.0 3.7 all-to-all-start.6
  345.7 9.3 %shard_map.84 = (bf16[256,512]{1,0:T(8,128)(2,1)}, bf16[256,512]{1,0:T(8,128)(2,1)}) custom-call(s32[6]{0:T(128)} %stack.33.refs_0_.idx, bf16[128,2048]{1,0:T(8,128)(2,1)} %get-tuple-element.25.refs_2_.refs_1_.own, bf16[128,2048]{1,0:T(8,128)(2,1)} %copy-done.3, bf16[128,2048]{1,0:T(8,128)(2,1)} %copy-done.4, bf16[128,2048]{1,0:T(8,128)(2,1)} %copy-done.5, ...), custom_call_target="tpu_custom_call" | custom-call | tf_op jit(solution)/shard_map/pallas_call | solution.py:242
  354.9 3.4 collective-permute-start.15
  358.3 3.1 collective-permute-start.16
  361.4 2.3 collective-permute-start.17
  363.8 1.9 collective-permute-done.16.refs_4_
  365.6 6.8 %collective-permute-done.17.refs_5_ = bf16[256,512]{1,0:T(8,128)(2,1)S(1)} collective-permute-done((bf16[256,512]{1,0:T(8,128)(2,1)}, bf16[256,512]{1,0:T(8,128)(2,1)S(1)}, u32[]{:S(2)}, u32[]{:S(2)}) %collective-permute-start.17) | collective-permute-done | bytes 262176 | tf_op jit(solution)/shard_map/ppermute | solution.py:261
  372.4 0.7 copy-done.21
  373.1 0.7 copy-done.17
  373.8 3.4 shard_map.85.mine
  377.2 2.1 collective-permute-start.18
  379.3 3.5 collective-permute-done.18.got
  383.4 2.8 shard_map.86
  386.2 29.1 %all_to_all.51.refs_0_ = bf16[8,80,256]{2,1,0:T(8,128)(2,1)} all-to-all(bf16[8,80,256]{2,1,0:T(8,128)(2,1)} %shard_map.86), channel_id=1, replica_groups=mesh['x'=4,'yh'=2,'c'=2,'yl'=2,'zh'=8,'zl'=2] {'zh'}, dimensions={0} | all-to-all | bytes 655360 | tf_op jit(solution)/shard_map/all_to_all | solution.py:269
  415.3 1.7 shard_map.87
  417.1 18.8 %all_to_all.52.blocks = f32[8,16,256]{2,1,0:T(8,128)} all-to-all(f32[8,16,256]{2,1,0:T(8,128)} %get-tuple-element.34), channel_id=1, replica_groups=mesh['x'=4,'yh'=2,'c'=2,'yl'=2,'zh'=8,'zl'=2] {'zh'}, dimensions={0} | all-to-all | bytes 262144 | tf_op jit(solution)/shard_map/all_to_all | solution.py:269
  435.9 2.5 shard_map.88
  438.4 22.5 %all_to_all.53.parts = f32[16,32,256]{2,1,0:T(8,128)} all-to-all(f32[16,32,256]{2,1,0:T(8,128)} %bitcast.44), channel_id=1, replica_groups=mesh['x'=4,'yh'=2,'c'=2,'yl'=2,'zh'=8,'zl'=2] {'x','yh','c'}, dimensions={0} | all-to-all | bytes 1048576 | tf_op jit(solution)/shard_map/all_to_all | solution.py:269
  460.8 1.7 shard_map.89
  (62 shorter events, 3.8 us)
Async XLA Ops:
  2.1 28.8 %all-to-all-start.2 = ((bf16[8,32,256]{2,1,0:T(8,128)(2,1)}), bf16[8,32,256]{2,1,0:T(8,128)(2,1)S(1)}, u32[]{:S(2)}, u32[]{:S(2)}) async-start(bf16[8,32,256]{2,1,0:T(8,128)(2,1)} %broadcast_in_dim.13), calls=%async_computation.2 | async-start | bytes 262144 | tf_op jit(solution)/shard_map/all_to_all | solution.py:269
  31.6 97.1 %all-to-all-start = ((bf16[8,64,256]{2,1,0:T(8,128)(2,1)}), bf16[8,64,256]{2,1,0:T(8,128)(2,1)S(1)}, u32[]{:S(2)}, u32[]{:S(2)}) async-start(bf16[8,64,256]{2,1,0:T(8,128)(2,1)} %broadcast_in_dim.12), calls=%async_computation | async-start | bytes 524288 | tf_op jit(solution)/shard_map/all_to_all | solution.py:269
  102.0 13.2 %collective-permute-start = (bf16[128,2048]{1,0:T(8,128)(2,1)}, bf16[128,2048]{1,0:T(8,128)(2,1)S(1)}, u32[]{:S(2)}, u32[]{:S(2)}) collective-permute-start(bf16[128,2048]{1,0:T(8,128)(2,1)} %get-tuple-element.21), channel_id=1, source_target_pairs={{0,16},{16,0},{1,17},{17,1},{2,18},{18,2},{3,19},{19,3},{4,20},{20... | collective-permute-start | bytes 1572872 | tf_op jit(solution)/shard_map/ppermute | solution.py:257
  105.2 12.3 %collective-permute-start.1 = (bf16[128,2048]{1,0:T(8,128)(2,1)}, bf16[128,2048]{1,0:T(8,128)(2,1)S(1)}, u32[]{:S(2)}, u32[]{:S(2)}) collective-permute-start(bf16[128,2048]{1,0:T(8,128)(2,1)} %get-tuple-element.22), channel_id=1, source_target_pairs={{0,1},{1,0},{2,3},{3,2},{4,5},{5,4},{6,7},{7,6},{8,9},{9,8},{10,11... | collective-permute-start | bytes 1572872 | tf_op jit(solution)/shard_map/ppermute | solution.py:257
  108.2 20.4 %collective-permute-start.2 = (bf16[128,2048]{1,0:T(8,128)(2,1)}, bf16[128,2048]{1,0:T(8,128)(2,1)S(1)}, u32[]{:S(2)}, u32[]{:S(2)}) collective-permute-start(bf16[128,2048]{1,0:T(8,128)(2,1)} %get-tuple-element.23), channel_id=1, source_target_pairs={{0,17},{1,16},{16,1},{17,0},{2,19},{3,18},{18,3},{19,2},{4,21},{5,... | collective-permute-start | bytes 1572872 | tf_op jit(solution)/shard_map/ppermute | solution.py:261
  110.4 26.3 %collective-permute-start.3 = (bf16[32,2048]{1,0:T(8,128)(2,1)S(1)}, bf16[32,2048]{1,0:T(8,128)(2,1)S(1)}, u32[]{:S(2)}, u32[]{:S(2)}) collective-permute-start(bf16[32,2048]{1,0:T(8,128)(2,1)S(1)} %bitcast.46), channel_id=1, source_target_pairs={{0,64},{64,0},{1,65},{65,1},{2,66},{66,2},{3,67},{67,3},{4,68},{68... | collective-permute-start | bytes 393224 | tf_op jit(solution)/shard_map/ppermute | solution.py:257
  115.3 13.4 %copy-start = (bf16[128,2048]{1,0:T(8,128)(2,1)}, bf16[128,2048]{1,0:T(8,128)(2,1)S(1)}, u32[]{:S(2)}) copy-start(bf16[128,2048]{1,0:T(8,128)(2,1)S(1)} %collective-permute-done.refs_3_.refs_2_.gy) | copy-start | bytes 1572868
  117.5 11.1 %copy-start.1 = (bf16[128,2048]{1,0:T(8,128)(2,1)}, bf16[128,2048]{1,0:T(8,128)(2,1)S(1)}, u32[]{:S(2)}) copy-start(bf16[128,2048]{1,0:T(8,128)(2,1)S(1)} %collective-permute-done.1.refs_4_.refs_3_.gz) | copy-start | bytes 1572868
  128.6 0.8 copy-start.2
  128.7 0.9 copy-start.18
  132.7 29.2 %all-to-all-start.1 = ((f32[4,64,256]{2,1,0:T(8,128)}), f32[4,64,256]{2,1,0:T(8,128)S(1)}, u32[]{:S(2)}, u32[]{:S(2)}) async-start(f32[4,64,256]{2,1,0:T(8,128)} %shard_map.77), calls=%async_computation.1 | async-start | bytes 524288 | tf_op jit(solution)/shard_map/all_to_all | solution.py:269
  136.8 25.1 %copy-start.8 = (bf16[2,32,2048]{2,1,0:T(8,128)(2,1)}, bf16[2,32,2048]{2,1,0:T(8,128)(2,1)S(1)}, u32[]{:S(2)}) copy-start(bf16[2,32,2048]{2,1,0:T(8,128)(2,1)S(1)} %pad_maximum_fusion.refs_7_) | copy-start | bytes 786436
  136.8 17.2 %collective-permute-start.4 = (bf16[2,32,2048]{2,1,0:T(8,128)(2,1)S(1)}, bf16[2,32,2048]{2,1,0:T(8,128)(2,1)S(1)}, u32[]{:S(2)}, u32[]{:S(2)}) collective-permute-start(bf16[2,32,2048]{2,1,0:T(8,128)(2,1)S(1)} %pad_maximum_fusion.refs_7_), channel_id=1, source_target_pairs={{0,128},{128,256},{256,384},{384,0},{1,129},{129,257},{257,385},{3... | collective-permute-start | bytes 786440 | tf_op jit(solution)/shard_map/ppermute | solution.py:265
  140.0 16.0 %collective-permute-start.5 = (bf16[2,32,2048]{2,1,0:T(8,128)(2,1)S(1)}, bf16[2,32,2048]{2,1,0:T(8,128)(2,1)S(1)}, u32[]{:S(2)}, u32[]{:S(2)}) collective-permute-start(bf16[2,32,2048]{2,1,0:T(8,128)(2,1)S(1)} %pad_maximum_fusion.refs_7_), channel_id=1, source_target_pairs={{0,256},{128,384},{256,0},{384,128},{1,257},{129,385},{257,1},{385... | collective-permute-start | bytes 786440 | tf_op jit(solution)/shard_map/ppermute | solution.py:265
  144.3 14.1 %collective-permute-start.6 = (bf16[2,32,2048]{2,1,0:T(8,128)(2,1)S(1)}, bf16[2,32,2048]{2,1,0:T(8,128)(2,1)S(1)}, u32[]{:S(2)}, u32[]{:S(2)}) collective-permute-start(bf16[2,32,2048]{2,1,0:T(8,128)(2,1)S(1)} %pad_maximum_fusion.refs_7_), channel_id=1, source_target_pairs={{0,384},{128,0},{256,128},{384,256},{1,385},{129,1},{257,129},{385... | collective-permute-start | bytes 786440 | tf_op jit(solution)/shard_map/ppermute | solution.py:265
  147.4 13.0 %collective-permute-start.7 = (bf16[2,32,2048]{2,1,0:T(8,128)(2,1)S(1)}, bf16[2,32,2048]{2,1,0:T(8,128)(2,1)S(1)}, u32[]{:S(2)}, u32[]{:S(2)}) collective-permute-start(bf16[2,32,2048]{2,1,0:T(8,128)(2,1)S(1)} %pad_maximum_fusion.refs_7_), channel_id=1, source_target_pairs={{0,32},{32,0},{1,33},{33,1},{2,34},{34,2},{3,35},{35,3},{4,36},{36... | collective-permute-start | bytes 786440 | tf_op jit(solution)/shard_map/ppermute | solution.py:257
  154.1 7.8 %copy-start.10 = (bf16[2,32,2048]{2,1,0:T(8,128)(2,1)}, bf16[2,32,2048]{2,1,0:T(8,128)(2,1)S(1)}, u32[]{:S(2)}) copy-start(bf16[2,32,2048]{2,1,0:T(8,128)(2,1)S(1)} %collective-permute-done.4.refs_8_) | copy-start | bytes 786436
  154.1 6.3 %collective-permute-start.8 = (bf16[2,32,2048]{2,1,0:T(8,128)(2,1)S(1)}, bf16[2,32,2048]{2,1,0:T(8,128)(2,1)S(1)}, u32[]{:S(2)}, u32[]{:S(2)}) collective-permute-start(bf16[2,32,2048]{2,1,0:T(8,128)(2,1)S(1)} %collective-permute-done.4.refs_8_), channel_id=1, source_target_pairs={{0,32},{32,0},{1,33},{33,1},{2,34},{34,2},{3,35},{35,3},{4,36},{36... | collective-permute-start | bytes 786440 | tf_op jit(solution)/shard_map/ppermute | solution.py:257
  156.0 5.9 %copy-start.11 = (bf16[2,32,2048]{2,1,0:T(8,128)(2,1)}, bf16[2,32,2048]{2,1,0:T(8,128)(2,1)S(1)}, u32[]{:S(2)}) copy-start(bf16[2,32,2048]{2,1,0:T(8,128)(2,1)S(1)} %collective-permute-done.5.refs_9_) | copy-start | bytes 786436
  156.0 4.4 collective-permute-start.9
  158.4 3.5 copy-start.12
  158.5 3.4 collective-permute-start.10
  160.4 1.5 copy-start.13
  160.4 1.5 copy-start.14
  160.4 1.5 copy-start.15
  161.9 0.7 copy-start.16
  161.9 0.8 copy-start.6
  194.2 5.6 %collective-permute-start.11 = (bf16[64,768]{1,0:T(8,128)(2,1)}, bf16[64,768]{1,0:T(8,128)(2,1)S(1)}, u32[]{:S(2)}, u32[]{:S(2)}) collective-permute-start(bf16[64,768]{1,0:T(8,128)(2,1)} %shard_map.79.mine), channel_id=1, source_target_pairs={{0,1},{1,0},{2,3},{3,2},{4,5},{5,4},{6,7},{7,6},{8,9},{9,8},{10,11... | collective-permute-start | bytes 294920 | tf_op jit(solution)/shard_map/ppermute | solution.py:257
  199.8 0.6 copy-start.23
  203.2 29.5 %all-to-all-start.4 = ((bf16[8,80,256]{2,1,0:T(8,128)(2,1)}), bf16[8,80,256]{2,1,0:T(8,128)(2,1)S(1)}, u32[]{:S(2)}, u32[]{:S(2)}) async-start(bf16[8,80,256]{2,1,0:T(8,128)(2,1)} %shard_map.80), calls=%async_computation.4 | async-start | bytes 655360 | tf_op jit(solution)/shard_map/all_to_all | solution.py:269
  232.7 0.7 copy-start.9
  235.3 102.6 %all-to-all-start.5 = ((bf16[8,96,256]{2,1,0:T(8,128)(2,1)}), bf16[8,96,256]{2,1,0:T(8,128)(2,1)S(1)}, u32[]{:S(2)}, u32[]{:S(2)}) async-start(bf16[8,96,256]{2,1,0:T(8,128)(2,1)} %get-tuple-element.24), calls=%async_computation.5 | async-start | bytes 786432 | tf_op jit(solution)/shard_map/all_to_all | solution.py:269
  308.7 13.5 %collective-permute-start.12 = (bf16[128,2048]{1,0:T(8,128)(2,1)}, bf16[128,2048]{1,0:T(8,128)(2,1)S(1)}, u32[]{:S(2)}, u32[]{:S(2)}) collective-permute-start(bf16[128,2048]{1,0:T(8,128)(2,1)} %get-tuple-element.26), channel_id=1, source_target_pairs={{0,16},{16,0},{1,17},{17,1},{2,18},{18,2},{3,19},{19,3},{4,20},{20... | collective-permute-start | bytes 1572872 | tf_op jit(solution)/shard_map/ppermute | solution.py:257
  311.9 14.1 %collective-permute-start.13 = (bf16[128,2048]{1,0:T(8,128)(2,1)}, bf16[128,2048]{1,0:T(8,128)(2,1)S(1)}, u32[]{:S(2)}, u32[]{:S(2)}) collective-permute-start(bf16[128,2048]{1,0:T(8,128)(2,1)} %get-tuple-element.27), channel_id=1, source_target_pairs={{0,1},{1,0},{2,3},{3,2},{4,5},{5,4},{6,7},{7,6},{8,9},{9,8},{10,11... | collective-permute-start | bytes 1572872 | tf_op jit(solution)/shard_map/ppermute | solution.py:257
  315.5 22.3 %collective-permute-start.14 = (bf16[128,2048]{1,0:T(8,128)(2,1)}, bf16[128,2048]{1,0:T(8,128)(2,1)S(1)}, u32[]{:S(2)}, u32[]{:S(2)}) collective-permute-start(bf16[128,2048]{1,0:T(8,128)(2,1)} %get-tuple-element.28), channel_id=1, source_target_pairs={{0,17},{1,16},{16,1},{17,0},{2,19},{3,18},{18,3},{19,2},{4,21},{5,... | collective-permute-start | bytes 1572872 | tf_op jit(solution)/shard_map/ppermute | solution.py:261
  322.3 15.6 %copy-start.3 = (bf16[128,2048]{1,0:T(8,128)(2,1)}, bf16[128,2048]{1,0:T(8,128)(2,1)S(1)}, u32[]{:S(2)}) copy-start(bf16[128,2048]{1,0:T(8,128)(2,1)S(1)} %collective-permute-done.12.refs_3_.refs_2_.gy) | copy-start | bytes 1572868
  326.0 11.8 %copy-start.4 = (bf16[128,2048]{1,0:T(8,128)(2,1)}, bf16[128,2048]{1,0:T(8,128)(2,1)S(1)}, u32[]{:S(2)}) copy-start(bf16[128,2048]{1,0:T(8,128)(2,1)S(1)} %collective-permute-done.13.refs_4_.refs_3_.gz) | copy-start | bytes 1572868
  337.9 0.8 copy-start.5
  337.9 0.9 copy-start.7
  342.0 30.4 %all-to-all-start.6 = ((f32[4,64,256]{2,1,0:T(8,128)}), f32[4,64,256]{2,1,0:T(8,128)S(1)}, u32[]{:S(2)}, u32[]{:S(2)}) async-start(f32[4,64,256]{2,1,0:T(8,128)} %shard_map.83), calls=%async_computation.6 | async-start | bytes 524288 | tf_op jit(solution)/shard_map/all_to_all | solution.py:269
  354.9 8.8 %collective-permute-start.15 = (bf16[256,512]{1,0:T(8,128)(2,1)}, bf16[256,512]{1,0:T(8,128)(2,1)S(1)}, u32[]{:S(2)}, u32[]{:S(2)}) collective-permute-start(bf16[256,512]{1,0:T(8,128)(2,1)} %get-tuple-element.29.refs_2_), channel_id=1, source_target_pairs={{0,16},{16,0},{1,17},{17,1},{2,18},{18,2},{3,19},{19,3},{4,20},{20... | collective-permute-start | bytes 786440 | tf_op jit(solution)/shard_map/ppermute | solution.py:257
  358.3 7.3 %collective-permute-start.16 = (bf16[256,512]{1,0:T(8,128)(2,1)}, bf16[256,512]{1,0:T(8,128)(2,1)S(1)}, u32[]{:S(2)}, u32[]{:S(2)}) collective-permute-start(bf16[256,512]{1,0:T(8,128)(2,1)} %get-tuple-element.30), channel_id=1, source_target_pairs={{0,1},{1,0},{2,3},{3,2},{4,5},{5,4},{6,7},{7,6},{8,9},{9,8},{10,11... | collective-permute-start | bytes 786440 | tf_op jit(solution)/shard_map/ppermute | solution.py:257
  361.4 11.0 %collective-permute-start.17 = (bf16[256,512]{1,0:T(8,128)(2,1)}, bf16[256,512]{1,0:T(8,128)(2,1)S(1)}, u32[]{:S(2)}, u32[]{:S(2)}) collective-permute-start(bf16[256,512]{1,0:T(8,128)(2,1)} %get-tuple-element.30), channel_id=1, source_target_pairs={{0,17},{1,16},{16,1},{17,0},{2,19},{3,18},{18,3},{19,2},{4,21},{5,... | collective-permute-start | bytes 786440 | tf_op jit(solution)/shard_map/ppermute | solution.py:261
  363.7 8.7 %copy-start.19 = (bf16[256,512]{1,0:T(8,128)(2,1)}, bf16[256,512]{1,0:T(8,128)(2,1)S(1)}, u32[]{:S(2)}) copy-start(bf16[256,512]{1,0:T(8,128)(2,1)S(1)} %collective-permute-done.15.refs_3_) | copy-start | bytes 786436
  365.6 6.8 %copy-start.20 = (bf16[256,512]{1,0:T(8,128)(2,1)}, bf16[256,512]{1,0:T(8,128)(2,1)S(1)}, u32[]{:S(2)}) copy-start(bf16[256,512]{1,0:T(8,128)(2,1)S(1)} %collective-permute-done.16.refs_4_) | copy-start | bytes 786436
  372.4 0.7 copy-start.21
  373.1 0.7 copy-start.17
  377.2 5.6 %collective-permute-start.18 = (bf16[64,768]{1,0:T(8,128)(2,1)}, bf16[64,768]{1,0:T(8,128)(2,1)S(1)}, u32[]{:S(2)}, u32[]{:S(2)}) collective-permute-start(bf16[64,768]{1,0:T(8,128)(2,1)} %shard_map.85.mine), channel_id=1, source_target_pairs={{0,1},{1,0},{2,3},{3,2},{4,5},{5,4},{6,7},{7,6},{8,9},{9,8},{10,11... | collective-permute-start | bytes 294920 | tf_op jit(solution)/shard_map/ppermute | solution.py:257
  382.8 0.7 copy-start.22

commit v4 on v3

v4 whole, which is shorter than its diff:
```python
import jax
import jax.numpy as jnp
from jax import lax
from jax.experimental import pallas as pl
from jax.experimental.pallas import tpu as pltpu
from jax.sharding import Mesh
from jax.sharding import PartitionSpec as P

W = ("x", "yh", "c")
F = ("yl", "zh", "zl")
Q = ("yl", "zl")
NZ = 8


branch_scale = 0.25
rate_down = 200.0
rate_up = 20.0

bf16 = jnp.bfloat16
f32 = jnp.float32
HIGH = lax.Precision.HIGHEST
VMEM = pltpu.CompilerParams(vmem_limit_bytes=60 * 1024 * 1024)


def dot(a, b, ca, cb, precision=None):
    return lax.dot_general(a, b, (((ca,), (cb,)), ((), ())), precision=precision, preferred_element_type=f32)


def split(value):
    hi = value.astype(bf16)
    return hi, (value - hi.astype(f32)).astype(bf16)


def vmem(n):
    return [pl.BlockSpec(memory_space=pltpu.VMEM)] * n


def hbm(n):
    return [pl.BlockSpec(memory_space=pl.ANY)] * n


def smem():
    return pl.BlockSpec(memory_space=pltpu.SMEM)


def pack_kernel(idx, x_ref, *outs):
    yl, zl = idx[3], idx[5]
    n = 256
    for k, out in enumerate(outs):
        start = lax.rem(yl + k % 2, 2) * (2 * NZ * n) + lax.rem(zl + k // 2, 2) * n
        for z in range(NZ):
            out[0, :, z * n : (z + 1) * n] = x_ref[0, :, pl.ds(pl.multiple_of(start + z * 2 * n, n), n)]


def wide(value):
    return jnp.concatenate([value[16 * k : 16 * k + 16] for k in range(4)], axis=1)


def tall(value):
    n = value.shape[1] // 4
    return jnp.concatenate([value[:, k * n : k * n + n] for k in range(4)], axis=0)


def group_at(idx, k):
    return 2 * lax.rem(idx[3] + k % 2, 2) + lax.rem(idx[5] + k // 2, 2)


def partial_low(whole, tokens):
    n = whole.shape[2]
    part = dot(whole[0, :64], tokens[:, :n], 1, 1)
    for z in range(1, NZ):
        part = part + dot(whole[z, :64], tokens[:, z * n : (z + 1) * n], 1, 1)
    return part


def keys_kernel(step, scale, idx, *rest):
    x_refs, a_ref, y_ref, pieces = rest[:4], rest[4], rest[5], rest[6:14]
    outs, (xs, bs, xsem, bsem) = rest[14:-4], rest[-4:]
    rows, quarter = xs.shape[1:]
    px, pyh, pc = idx[0], idx[1], idx[2]
    places = [group_at(idx, k) for k in range(4)]
    copies = [pltpu.make_async_copy(ref.at[step], xs.at[k], xsem.at[k]) for k, ref in enumerate(x_refs)]
    loads = []
    for k, piece in enumerate(pieces):
        dc, dx = divmod(k, 4)
        for dy in range(2):
            w = lax.rem(pyh + dy, 2) * 2 + lax.rem(pc + dc, 2)
            loads.append(pltpu.make_async_copy(piece.at[dy], bs.at[dx, w], bsem.at[k * 2 + dy]))
    for copy in copies + loads:
        copy.start()
    for copy in copies:
        copy.wait()
    if step == 0:
        for k in range(4):
            hi, lo = split(partial_low(a_ref, xs[k]) * scale)
            outs[0][places[k], rows : rows + 16] = wide(hi)
            outs[0][places[k], rows + 16 :] = wide(lo)
    tokens = xs[...].reshape(4 * rows, quarter)
    for dx in range(4):
        for k in (dx, dx + 4):
            for dy in range(2):
                loads[k * 2 + dy].wait()
        at = pl.ds(pl.multiple_of(lax.rem(px + 4 - dx, 4) * 128, 128), 128)
        part = dot(tokens, bs[dx].reshape(128, quarter), 1, 1) * scale
        for k in range(4):
            value = part[k * rows : (k + 1) * rows]
            if k == 0:
                value = value - y_ref[step, :, at].astype(f32)
            if step == 0:
                outs[0][places[k], :rows, at] = value.astype(bf16)
            else:
                outs[k][:, at] = value.astype(bf16)


def low_kernel(scale, idx, whole, *rest):
    x_refs, out = rest[:4], rest[4]
    for k in range(4):
        at = group_at(idx, k)
        hi, lo = split(partial_low(whole, x_refs[k][0]) * scale)
        out[at, :64, :128] = hi
        out[at, :64, 128:] = lo
        out[at, 64:] = jnp.concatenate([whole[z, 64:] for z in range(NZ)], axis=0)


def quarter_of(blocks):
    value = blocks[:, :128].astype(f32) + blocks[:, 128:].astype(f32)
    halves = [
        jnp.concatenate([value[8 * (4 * r + c) : 8 * (4 * r + c) + 8] for c in range(4)], axis=1) for r in range(2)
    ]
    return jnp.concatenate(halves, axis=0)


def error_of(total_rows, keys, low, up, out):
    error = (keys + branch_scale * dot(low, up, 0, 0, HIGH)) / total_rows
    back = wide((branch_scale * dot(up, error, 1, 1, HIGH)).astype(bf16))
    hi, lo = split(branch_scale * dot(low, error, 1, 0, HIGH))
    for q in range(4):
        out[q, :16] = back
        out[q, 16:32] = hi[16 * q : 16 * q + 16]
        out[q, 32:] = lo[16 * q : 16 * q + 16]


def first_error_kernel(total_rows, parts, up_ref, out):
    rows = parts.shape[1] - 32
    k = [parts[q, :rows].astype(f32) for q in range(4)]
    low = [tall(parts[q, rows : rows + 16]).astype(f32) + tall(parts[q, rows + 16 :]).astype(f32) for q in range(4)]
    error_of(total_rows, (k[0] + k[1]) + (k[2] + k[3]), (low[0] + low[1]) + (low[2] + low[3]), up_ref[...], out)


def second_error_kernel(total_rows, parts, own, by_y, by_z, by_both, out):
    keys = (own[...].astype(f32) + by_y[...].astype(f32)) + (by_z[...].astype(f32) + by_both[...].astype(f32))
    low = [parts[q, :64, :128].astype(f32) + parts[q, :64, 128:].astype(f32) for q in range(4)]
    up = jnp.concatenate([quarter_of(parts[q, 64:]) for q in range(4)], axis=0)
    error_of(total_rows, keys, (low[0] + low[1]) + (low[2] + low[3]), up, out)


def down_kernel(idx, parts, *rest):
    x_refs, out = rest[:4], rest[4]
    backs = [tall(parts[group_at(idx, k), :16]) for k in range(4)]
    grads = [parts[q, 16:32].astype(f32) + parts[q, 32:].astype(f32) for q in range(4)]
    hi, lo = split((grads[0] + grads[1]) + (grads[2] + grads[3]))
    n = out.shape[2]
    for z in range(NZ):
        at = slice(z * n, (z + 1) * n)
        part = [dot(backs[k], x_refs[k][0, :, at], 1, 0) for k in range(4)]
        out[z, :64] = ((part[0] + part[1]) + (part[2] + part[3])).astype(bf16)
        r, c = z // 4, z % 4
        out[z, 64:, :128] = hi[8 * r : 8 * r + 8, 128 * c : 128 * c + 128]
        out[z, 64:, 128:] = lo[8 * r : 8 * r + 8, 128 * c : 128 * c + 128]


def summed(parts):
    result = parts[0].astype(f32)
    for k in range(1, parts.shape[0]):
        result = result + parts[k].astype(f32)
    return result


def update_kernel(scale, parts, a_ref, b_ref, a_out, b_out, copies):
    grads = summed(parts)
    a = a_ref[...] - (rate_down * scale) * grads[:64]
    hi, lo = split(b_ref[...] - rate_up * (grads[64:, :128] + grads[64:, 128:]))
    a_out[...] = a
    b_out[...] = hi.astype(f32) + lo.astype(f32)
    a_half = a.astype(bf16)
    for z in range(NZ):
        copies[z, :64] = a_half
        copies[z, 64:, :128] = hi
        copies[z, 64:, 128:] = lo


def last_update_kernel(scale, parts, a_ref, b_ref, a_out, copies):
    grads = summed(parts)
    a_out[...] = a_ref[...] - (rate_down * scale) * grads[:64]
    b = b_ref[...] - rate_up * (grads[64:, :128] + grads[64:, 128:])
    for k in range(4 * NZ):
        copies[k] = b


def change_kernel(a_ref, blocks, a_start, up_start, out, b_out):
    rows = []
    for q in range(4):
        yl, zl = q // 2, q % 2
        for r in range(2):
            at = [yl * 2 * NZ + (4 * r + c) * 2 + zl for c in range(4)]
            rows.append(jnp.concatenate([blocks[k] for k in at], axis=1))
    up = jnp.concatenate(rows, axis=0)
    left = jnp.concatenate([up, -up_start[...]], axis=0)
    right = jnp.concatenate([a_ref[...], a_start[...]], axis=0)
    out[...] = branch_scale * dot(left, right, 0, 0, HIGH)
    b_out[...] = up


def merge_kernel(parts, base, out):
    out[...] = base[...] + summed(parts) * (1.0 / parts.shape[0])


def shaped(dims, kind):
    return jax.ShapeDtypeStruct(dims, kind)


def call(kernel, shapes, *args):
    return pl.pallas_call(kernel, out_shape=shapes, in_specs=vmem(len(args)), compiler_params=VMEM)(*args)


def pack(idx, tokens):
    steps, rows, width = tokens.shape
    quarter = width // 4
    return pl.pallas_call(
        pack_kernel,
        out_shape=[shaped((steps, rows, quarter), bf16)] * 4,
        grid_spec=pltpu.PrefetchScalarGridSpec(
            num_scalar_prefetch=1,
            grid=(steps,),
            in_specs=[pl.BlockSpec((1, rows, width), lambda i, s: (i, 0, 0))],
            out_specs=[pl.BlockSpec((1, rows, quarter), lambda i, s: (i, 0, 0))] * 4,
        ),
        compiler_params=VMEM,
    )(idx, tokens)


def with_tokens(kernel, step, shape, idx, args, xs):
    _, rows, quarter = xs[0].shape
    return pl.pallas_call(
        kernel,
        out_shape=shape,
        grid_spec=pltpu.PrefetchScalarGridSpec(
            num_scalar_prefetch=1,
            grid=(1,),
            in_specs=[pl.BlockSpec(a.shape, lambda i, s, n=a.ndim: (0,) * n) for a in args]
            + [pl.BlockSpec((1, rows, quarter), lambda i, s: (step, 0, 0))] * 4,
            out_specs=pl.BlockSpec(shape.shape, lambda i, s, n=len(shape.shape): (0,) * n),
        ),
        compiler_params=VMEM,
    )(idx, *args, *xs)


def keys_of(step, scale, idx, xs, whole, targets, pieces, shapes):
    _, rows, quarter = xs[0].shape

    def body(*refs):
        keys_kernel(step, scale, *refs)

    return pl.pallas_call(
        body,
        out_shape=shapes,
        in_specs=[smem()] + hbm(4) + vmem(2) + hbm(8),
        scratch_shapes=[
            pltpu.VMEM((4, rows, quarter), bf16),
            pltpu.VMEM((4, 4, 32, quarter), bf16),
            pltpu.SemaphoreType.DMA((4,)),
            pltpu.SemaphoreType.DMA((16,)),
        ],
        compiler_params=VMEM,
    )(idx, *xs, whole, targets, *pieces)


def swap(value, axis):
    return lax.ppermute(value, axis, [(0, 1), (1, 0)])


def swap_both(value):
    return lax.ppermute(value, Q, [(k, 3 - k) for k in range(4)])


def shift(value, axis, by, count):
    return lax.ppermute(value, axis, [(i, (i + by) % count) for i in range(count)])


def exchange(parts, axis):
    return lax.all_to_all(parts, axis, 0, 0, tiled=True)


def gather_z(value):
    return exchange(jnp.broadcast_to(value, (NZ, *value.shape)), "zh")


def whole_step(inputs, targets, base, adapter_a, adapter_b):
    tokens = inputs[0]
    a_start = adapter_a[0]
    _, rows, width = tokens.shape
    scale = width ** (-0.5)
    total_rows = float(rows * 4 * NZ)
    idx = jnp.stack([lax.axis_index(n) for n in (*W, *F[:1], "zh", "zl")]).astype(jnp.int32)
    up_start = adapter_b[0].T
    group = 2 * lax.axis_index("yl") + lax.axis_index("zl")
    z = lax.axis_index("zh")
    block = lax.dynamic_slice(up_start, (16 * group + 8 * (z // 4), 128 * (z % 4)), (8, 128))

    own, to_y, to_z, to_both = pack(idx, tokens)
    xs = (own, swap(to_y, "yl"), swap(to_z, "zl"), swap_both(to_both))
    cols = gather_z(base.T.astype(bf16))
    cols = cols.transpose(1, 0, 2).reshape(cols.shape[1], width // 4)
    pair = jnp.stack([cols, swap(cols, "yh")])
    near = [pair] + [shift(pair, "x", d, 4) for d in (1, 2, 3)]
    whole = gather_z(a_start.astype(bf16))
    pieces = near + [swap(piece, "c") for piece in near]

    keys_shape = shaped((rows, 512), bf16)
    error_shape = shaped((4, 48, 512), bf16)
    down_shape = shaped((NZ, 72, 256), bf16)

    def gradients(step, mine):
        shared = exchange(mine, Q)
        return exchange(with_tokens(down_kernel, step, down_shape, idx, (shared,), xs), "zh")

    keys = keys_of(0, scale, idx, xs, whole, targets[0], pieces, shaped((4, rows + 32, 512), bf16))
    parts = exchange(keys, Q)
    mine = call(lambda *refs: first_error_kernel(total_rows, *refs), error_shape, parts, up_start)
    parts = gradients(0, mine)

    keys = keys_of(1, scale, idx, xs, whole, targets[0], pieces, [keys_shape] * 4)
    keys = (keys[0], swap(keys[1], "yl"), swap(keys[2], "zl"), swap_both(keys[3]))
    a_next, block, copies = call(
        lambda *refs: update_kernel(scale, *refs),
        (shaped((64, 256), f32), shaped((8, 128), f32), down_shape),
        parts,
        a_start,
        block,
    )
    whole = exchange(copies, "zh")
    low = with_tokens(
        lambda *refs: low_kernel(scale, *refs), 1, shaped((4, 128, 256), bf16), idx, (whole,), xs
    )
    low = exchange(low, Q)
    mine = call(lambda *refs: second_error_kernel(total_rows, *refs), error_shape, low, *keys)
    parts = gradients(1, mine)
    a_last, copies = call(
        lambda *refs: last_update_kernel(scale, *refs),
        (shaped((64, 256), f32), shaped((4 * NZ, 8, 128), f32)),
        parts,
        a_next,
        block,
    )
    blocks = exchange(copies, F)
    change, b_last = call(
        change_kernel, (shaped((512, 256), f32), shaped((64, 512), f32)), a_last, blocks, a_start, up_start
    )
    merged = exchange(change.reshape(16, 32, 256), W)
    new_base = call(merge_kernel, shaped(base.shape[::-1], f32), merged, base.T)
    return (new_base.T, a_last[None], b_last.T[None])


def solution(mesh):
    finer = Mesh(mesh.devices.reshape(4, 2, 2, 2, NZ, 2), (*W, *F))
    return jax.shard_map(
        whole_step,
        mesh=finer,
        in_specs=(
            P(W, None, F, None),
            P(W, None, F, None),
            P(F, W),
            P(W, None, F),
            P(W, None, None),
        ),
        out_specs=(P(F, W), P(W, None, F), P(W, None, None)),
        check_vma=False,
    )
```

time: 465 us -> 298 us (0.64)
  Pallas kernels: 176 us -> 47.7 us
  waiting for transfers between devices: 78.6 us -> 32.2 us
  blocking collectives: 89 us -> 118 us
  starting transfers between devices: 106 us -> 87.3 us
    pallas_call x8 -> x6, Pallas kernels: 162 us -> 34.6 us  [the longest x2 19.4 us: keys_of(): pl.pallas_call(body, out_shape=shapes, in_specs=[smem()] + hbm(4) + vmem(...]
    all_to_all x4 -> x7, blocking collectives: 89 us -> 118 us  [exchange(): return lax.all_to_all(parts, axis, 0, 0, tiled=True)]
    ppermute x3 -> x2, waiting for transfers between devices: 29.7 us -> 3.96 us  [swap_both(): return lax.ppermute(value, Q, [(k, 3 - k) for k in range(4)])]
    ppermute x13 -> x9, waiting for transfers between devices: 19.8 us -> 4 us  [swap(): return lax.ppermute(value, axis, [(0, 1), (1, 0)])]
    all_to_all x6 -> x4, starting transfers between devices: 46.7 us -> 37.4 us  [exchange(): return lax.all_to_all(parts, axis, 0, 0, tiled=True)]
    ppermute x13 -> x9, starting transfers between devices: 42.1 us -> 34.7 us  [swap(): return lax.ppermute(value, axis, [(0, 1), (1, 0)])]
    all_to_all x6 -> x4, waiting for transfers between devices: 29 us -> 22 us  [exchange(): return lax.all_to_all(parts, axis, 0, 0, tiled=True)]
  transfers between devices with their start and end apart: 25 -> 18, of which waited for: 12 -> 7; matrix products, arithmetic and copies ran while one was open for 1% -> 2% of each run, Pallas kernels for 31% -> 5%
where the time goes in v4:
time: 298 us; the launch traced here: 297 us
  blocking collectives  118 us (40%)
  starting transfers between devices  87.3 us (29%)
  Pallas kernels  47.7 us (16%)
  waiting for transfers between devices  32.2 us (11%)
  local copies, waits for them, and re-layouts  8.55 us (3%)
    all_to_all x7, blocking collectives, exchange(): return lax.all_to_all(parts, axis, 0, 0, tiled=True)  118 us
    all_to_all x4, starting transfers between devices, exchange(): return lax.all_to_all(parts, axis, 0, 0, tiled=True)  37.4 us
    ppermute x9, starting transfers between devices, swap(): return lax.ppermute(value, axis, [(0, 1), (1, 0)])  34.7 us
    all_to_all x4, waiting for transfers between devices, exchange(): return lax.all_to_all(parts, axis, 0, 0, tiled=True)  22 us
    pallas_call x2, Pallas kernels, keys_of(): pl.pallas_call(body, out_shape=shapes, in_specs=[smem()] + hbm(4) + vmem(...  19.4 us
    pallas_call x6, Pallas kernels, call(): pl.pallas_call(kernel, out_shape=shapes, in_specs=vmem(len(args)), compil...  13.1 us
    ppermute x3, starting transfers between devices, shift(): lax.ppermute(value, axis, [(i, (i + by) % count) for i in range(count)])  10.7 us
    pallas_call x3, Pallas kernels, with_tokens(): pl.pallas_call(kernel, out_shape=shape, grid_spec=pltpu.PrefetchScalarGri...  10.6 us
  transfers between devices with their start and end apart: 18, of which 7 were waited for; matrix products, arithmetic and copies ran while one was open for 2% of the time, Pallas kernels for 5%

profile of v4, /device:TPU:1, one launch (start us, length us, event | category | flops | bytes accessed | tf_op | source)
XLA Modules:
  0.0 296.6 jit_solution(3005395910065785777)
XLA Ops:
  0.6 0.0 copy-start.8
  0.6 0.8 bitcast_convert_fusion
  1.4 0.7 broadcast_in_dim.13
  2.1 15.6 %all-to-all-start.1 = ((bf16[8,32,256]{2,1,0:T(8,128)(2,1)}), bf16[8,32,256]{2,1,0:T(8,128)(2,1)S(1)}, u32[]{:S(2)}, u32[]{:S(2)}) async-start(bf16[8,32,256]{2,1,0:T(8,128)(2,1)} %broadcast_in_dim.13), calls=%async_computation.1 | async-start | bytes 262144 | tf_op jit(solution)/shard_map/all_to_all | solution.py:291
  17.7 0.6 stack.33.idx.refs_0_
  18.4 4.6 %shard_map.76 = (bf16[2,128,2048]{2,1,0:T(8,128)(2,1)}, bf16[2,128,2048]{2,1,0:T(8,128)(2,1)}, bf16[2,128,2048]{2,1,0:T(8,128)(2,1)}, bf16[2,128,2048]{2,1,0:T(8,128)(2,1)}) custom-call(s32[6]{0:T(128)} %stack.33.idx.refs_0_, bf16[2,128,8192]{2,1,0:T(8,128)(2,1)} %bitcast.29), custom_call_target="tpu_custom_call" | custom-call | tf_op jit(solution)/shard_map/pallas_call | solution.py:229
  23.0 3.2 %collective-permute-start = (bf16[2,128,2048]{2,1,0:T(8,128)(2,1)}, bf16[2,128,2048]{2,1,0:T(8,128)(2,1)S(1)}, u32[]{:S(2)}, u32[]{:S(2)}) collective-permute-start(bf16[2,128,2048]{2,1,0:T(8,128)(2,1)} %get-tuple-element.19), channel_id=1, source_target_pairs={{0,16},{16,0},{1,17},{17,1},{2,18},{18,2},{3,19},{19,3},{4,20},{20... | collective-permute-start | bytes 3145736 | tf_op jit(solution)/shard_map/ppermute | solution.py:279
  26.2 2.6 collective-permute-start.1
  28.8 2.5 collective-permute-start.2
  31.3 0.7 copy.10
  32.0 4.8 %collective-permute-start.3 = (bf16[32,2048]{1,0:T(8,128)(2,1)}, bf16[32,2048]{1,0:T(8,128)(2,1)}, u32[]{:S(2)}, u32[]{:S(2)}) collective-permute-start(bf16[32,2048]{1,0:T(8,128)(2,1)} %bitcast.25), channel_id=1, source_target_pairs={{0,64},{64,0},{1,65},{65,1},{2,66},{66,2},{3,67},{67,3},{4,68},{68... | collective-permute-start | bytes 393224 | tf_op jit(solution)/shard_map/ppermute | solution.py:279
  36.9 0.7 broadcast_in_dim.12
  37.6 11.5 %all-to-all-start = ((bf16[8,64,256]{2,1,0:T(8,128)(2,1)}), bf16[8,64,256]{2,1,0:T(8,128)(2,1)S(1)}, u32[]{:S(2)}, u32[]{:S(2)}) async-start(bf16[8,64,256]{2,1,0:T(8,128)(2,1)} %broadcast_in_dim.12), calls=%async_computation | async-start | bytes 524288 | tf_op jit(solution)/shard_map/all_to_all | solution.py:291
  49.1 0.7 copy.8
  49.8 1.0 stack_reshape.3
  50.8 3.1 %collective-permute-done.3 = bf16[32,2048]{1,0:T(8,128)(2,1)} collective-permute-done((bf16[32,2048]{1,0:T(8,128)(2,1)}, bf16[32,2048]{1,0:T(8,128)(2,1)}, u32[]{:S(2)}, u32[]{:S(2)}) %collective-permute-start.3) | collective-permute-done | bytes 131104 | tf_op jit(solution)/shard_map/ppermute | solution.py:279
  53.9 0.9 pad_maximum_fusion.refs_7_
  54.8 4.4 %collective-permute-start.6 = (bf16[2,32,2048]{2,1,0:T(8,128)(2,1)S(1)}, bf16[2,32,2048]{2,1,0:T(8,128)(2,1)}, u32[]{:S(2)}, u32[]{:S(2)}) collective-permute-start(bf16[2,32,2048]{2,1,0:T(8,128)(2,1)S(1)} %pad_maximum_fusion.refs_7_), channel_id=1, source_target_pairs={{0,384},{128,0},{256,128},{384,256},{1,385},{129,1},{257,129},{385... | collective-permute-start | bytes 786440 | tf_op jit(solution)/shard_map/ppermute | solution.py:287
  59.2 1.9 collective-permute-start.4
  61.1 1.4 collective-permute-done.6.refs_10_
  62.5 4.4 %collective-permute-start.5 = (bf16[2,32,2048]{2,1,0:T(8,128)(2,1)S(1)}, bf16[2,32,2048]{2,1,0:T(8,128)(2,1)}, u32[]{:S(2)}, u32[]{:S(2)}) collective-permute-start(bf16[2,32,2048]{2,1,0:T(8,128)(2,1)S(1)} %pad_maximum_fusion.refs_7_), channel_id=1, source_target_pairs={{0,256},{128,384},{256,0},{384,128},{1,257},{129,385},{257,1},{385... | collective-permute-start | bytes 786440 | tf_op jit(solution)/shard_map/ppermute | solution.py:287
  66.9 0.8 collective-permute-done.4.refs_8_
  67.7 11.4 %collective-permute-start.7 = (bf16[2,32,2048]{2,1,0:T(8,128)(2,1)S(1)}, bf16[2,32,2048]{2,1,0:T(8,128)(2,1)S(1)}, u32[]{:S(2)}, u32[]{:S(2)}) collective-permute-start(bf16[2,32,2048]{2,1,0:T(8,128)(2,1)S(1)} %pad_maximum_fusion.refs_7_), channel_id=1, source_target_pairs={{0,32},{32,0},{1,33},{33,1},{2,34},{34,2},{3,35},{35,3},{4,36},{36... | collective-permute-start | bytes 786440 | tf_op jit(solution)/shard_map/ppermute | solution.py:279
  79.0 0.0 collective-permute-done.5.refs_9_
  79.1 1.9 collective-permute-start.10
  81.0 0.0 collective-permute-done.7.refs_11_
  81.0 2.4 collective-permute-start.8
  83.5 1.9 collective-permute-start.9
  85.4 6.8 %all-to-all-done.refs_5_ = bf16[8,64,256]{2,1,0:T(8,128)(2,1)S(1)} async-done(((bf16[8,64,256]{2,1,0:T(8,128)(2,1)}), bf16[8,64,256]{2,1,0:T(8,128)(2,1)S(1)}, u32[]{:S(2)}, u32[]{:S(2)}) %all-to-all-start) | async-done | bytes 262176 | tf_op jit(solution)/shard_map/all_to_all | solution.py:291
  92.2 0.0 collective-permute-done.1.refs_3_.rest_2_.refs_4_
  92.2 0.0 collective-permute-done.2.refs_4_.rest_3_.refs_5_
  92.2 0.7 copy-done.3
  92.9 0.4 copy-done.1
  93.3 0.3 copy-done.2
  93.6 10.2 %shard_map.77 = bf16[4,160,512]{2,1,0:T(8,128)(2,1)} custom-call(s32[6]{0:T(128)} %stack.33.idx.refs_0_, bf16[2,128,2048]{2,1,0:T(8,128)(2,1)} %get-tuple-element.18.refs_1_.rest_0_.refs_2_, bf16[2,128,2048]{2,1,0:T(8,128)(2,1)} %copy-done, bf16[2,128,2048]{2,1,0:T(8,128)(2,1)} %copy-done.1, bf16[2,128,2048]{2,1,0:T(8,128)(2,1)} %copy-done.2, ...), custom_call_target="tpu_custom_call" | custom-call | tf_op jit(solution)/shard_map/pallas_call | solution.py:264
  103.8 10.9 %all_to_all.55.refs_0_ = bf16[4,160,512]{2,1,0:T(8,128)(2,1)} all-to-all(bf16[4,160,512]{2,1,0:T(8,128)(2,1)} %shard_map.77), channel_id=1, replica_groups=mesh['x'=4,'yh'=2,'c'=2,'yl'=2,'zh'=8,'zl'=2] {'yl','zl'}, dimensions={0} | all-to-all | bytes 1310720 | tf_op jit(solution)/shard_map/all_to_all | solution.py:291
  114.7 2.7 shard_map.78
  117.4 8.5 %all_to_all.56.parts = bf16[4,48,512]{2,1,0:T(8,128)(2,1)} all-to-all(bf16[4,48,512]{2,1,0:T(8,128)(2,1)} %shard_map.78), channel_id=1, replica_groups=mesh['x'=4,'yh'=2,'c'=2,'yl'=2,'zh'=8,'zl'=2] {'yl','zl'}, dimensions={0} | all-to-all | bytes 393216 | tf_op jit(solution)/shard_map/all_to_all | solution.py:291
  125.8 3.4 %shard_map.79 = bf16[8,72,256]{2,1,0:T(8,128)(2,1)} custom-call(s32[6]{0:T(128)} %stack.33.idx.refs_0_, bf16[4,48,512]{2,1,0:T(8,128)(2,1)} %all_to_all.56.parts, bf16[2,128,2048]{2,1,0:T(8,128)(2,1)} %get-tuple-element.18.refs_1_.rest_0_.refs_2_, bf16[2,128,2048]{2,1,0:T(8,128)(2,1)} %copy-done, bf16[2,128,2048]{2,1,0:T(8,128)(2,1)} %copy-done.1, ...), custom_call_target="tpu_custom_call" | custom-call | tf_op jit(solution)/shard_map/pallas_call | solution.py:244
  129.2 6.9 %all-to-all-start.4 = ((bf16[8,72,256]{2,1,0:T(8,128)(2,1)}), bf16[8,72,256]{2,1,0:T(8,128)(2,1)S(1)}, u32[]{:S(2)}, u32[]{:S(2)}) async-start(bf16[8,72,256]{2,1,0:T(8,128)(2,1)} %shard_map.79), calls=%async_computation.4 | async-start | bytes 589824 | tf_op jit(solution)/shard_map/all_to_all | solution.py:291
  136.1 1.3 dynamic-slice_bitcast_fusion.refs_2_
  137.4 15.3 %all-to-all-done.4.refs_0_ = bf16[8,72,256]{2,1,0:T(8,128)(2,1)S(1)} async-done(((bf16[8,72,256]{2,1,0:T(8,128)(2,1)}), bf16[8,72,256]{2,1,0:T(8,128)(2,1)S(1)}, u32[]{:S(2)}, u32[]{:S(2)}) %all-to-all-start.4) | async-done | bytes 294944 | tf_op jit(solution)/shard_map/all_to_all | solution.py:291
  152.7 0.7 copy-done.5
  153.4 1.8 shard_map.80
  155.2 25.0 %all_to_all.57.refs_1_ = bf16[8,72,256]{2,1,0:T(8,128)(2,1)} all-to-all(bf16[8,72,256]{2,1,0:T(8,128)(2,1)} %get-tuple-element.22), channel_id=1, replica_groups=mesh['x'=4,'yh'=2,'c'=2,'yl'=2,'zh'=8,'zl'=2] {'zh'}, dimensions={0} | all-to-all | bytes 589824 | tf_op jit(solution)/shard_map/all_to_all | solution.py:291
  180.2 3.8 %shard_map.81 = bf16[4,128,256]{2,1,0:T(8,128)(2,1)} custom-call(s32[6]{0:T(128)} %stack.33.idx.refs_0_, bf16[8,72,256]{2,1,0:T(8,128)(2,1)} %all_to_all.57.refs_1_, bf16[2,128,2048]{2,1,0:T(8,128)(2,1)} %get-tuple-element.18.refs_1_.rest_0_.refs_2_, bf16[2,128,2048]{2,1,0:T(8,128)(2,1)} %copy-done, bf16[2,128,2048]{2,1,0:T(8,128)(2,1)} %copy-done.1, ...), custom_call_target="tpu_custom_call" | custom-call | tf_op jit(solution)/shard_map/pallas_call | solution.py:244
  184.0 3.4 %all-to-all-start.6 = ((bf16[4,128,256]{2,1,0:T(8,128)(2,1)}), bf16[4,128,256]{2,1,0:T(8,128)(2,1)S(1)}, u32[]{:S(2)}, u32[]{:S(2)}) async-start(bf16[4,128,256]{2,1,0:T(8,128)(2,1)} %shard_map.81), calls=%async_computation.6 | async-start | bytes 524288 | tf_op jit(solution)/shard_map/all_to_all | solution.py:291
  187.4 9.2 %shard_map.82 = (bf16[128,512]{1,0:T(8,128)(2,1)}, bf16[128,512]{1,0:T(8,128)(2,1)}, bf16[128,512]{1,0:T(8,128)(2,1)}, bf16[128,512]{1,0:T(8,128)(2,1)}) custom-call(s32[6]{0:T(128)} %stack.33.idx.refs_0_, bf16[2,128,2048]{2,1,0:T(8,128)(2,1)} %get-tuple-element.18.refs_1_.rest_0_.refs_2_, bf16[2,128,2048]{2,1,0:T(8,128)(2,1)} %copy-done, ...), custom_call_target="tpu_custom_call" | custom-call | tf_op jit(solution)/shard_map/pallas_call | solution.py:264
  196.6 3.4 %collective-permute-start.11 = (bf16[128,512]{1,0:T(8,128)(2,1)}, bf16[128,512]{1,0:T(8,128)(2,1)S(1)}, u32[]{:S(2)}, u32[]{:S(2)}) collective-permute-start(bf16[128,512]{1,0:T(8,128)(2,1)} %get-tuple-element.24), channel_id=1, source_target_pairs={{0,16},{16,0},{1,17},{17,1},{2,18},{18,2},{3,19},{19,3},{4,20},{20... | collective-permute-start | bytes 393224 | tf_op jit(solution)/shard_map/ppermute | solution.py:279
  200.1 3.0 %collective-permute-start.12 = (bf16[128,512]{1,0:T(8,128)(2,1)}, bf16[128,512]{1,0:T(8,128)(2,1)S(1)}, u32[]{:S(2)}, u32[]{:S(2)}) collective-permute-start(bf16[128,512]{1,0:T(8,128)(2,1)} %get-tuple-element.25), channel_id=1, source_target_pairs={{0,1},{1,0},{2,3},{3,2},{4,5},{5,4},{6,7},{7,6},{8,9},{9,8},{10,11... | collective-permute-start | bytes 393224 | tf_op jit(solution)/shard_map/ppermute | solution.py:279
  203.1 2.0 collective-permute-start.13
  205.1 0.9 collective-permute-done.12.refs_3_
  206.0 4.0 %collective-permute-done.13.refs_4_ = bf16[128,512]{1,0:T(8,128)(2,1)S(1)} collective-permute-done((bf16[128,512]{1,0:T(8,128)(2,1)}, bf16[128,512]{1,0:T(8,128)(2,1)S(1)}, u32[]{:S(2)}, u32[]{:S(2)}) %collective-permute-start.13) | collective-permute-done | bytes 131104 | tf_op jit(solution)/shard_map/ppermute | solution.py:283
  210.0 0.6 copy-done.11
  210.6 0.1 copy-done.6
  210.8 2.7 shard_map.83
  213.5 8.5 %all_to_all.58.parts = bf16[4,48,512]{2,1,0:T(8,128)(2,1)} all-to-all(bf16[4,48,512]{2,1,0:T(8,128)(2,1)} %shard_map.83), channel_id=1, replica_groups=mesh['x'=4,'yh'=2,'c'=2,'yl'=2,'zh'=8,'zl'=2] {'yl','zl'}, dimensions={0} | all-to-all | bytes 393216 | tf_op jit(solution)/shard_map/all_to_all | solution.py:291
  221.9 3.4 %shard_map.84 = bf16[8,72,256]{2,1,0:T(8,128)(2,1)} custom-call(s32[6]{0:T(128)} %stack.33.idx.refs_0_, bf16[4,48,512]{2,1,0:T(8,128)(2,1)} %all_to_all.58.parts, bf16[2,128,2048]{2,1,0:T(8,128)(2,1)} %get-tuple-element.18.refs_1_.rest_0_.refs_2_, bf16[2,128,2048]{2,1,0:T(8,128)(2,1)} %copy-done, bf16[2,128,2048]{2,1,0:T(8,128)(2,1)} %copy-done.1, ...), custom_call_target="tpu_custom_call" | custom-call | tf_op jit(solution)/shard_map/pallas_call | solution.py:244
  225.3 22.7 %all_to_all.59.refs_0_ = bf16[8,72,256]{2,1,0:T(8,128)(2,1)} all-to-all(bf16[8,72,256]{2,1,0:T(8,128)(2,1)} %shard_map.84), channel_id=1, replica_groups=mesh['x'=4,'yh'=2,'c'=2,'yl'=2,'zh'=8,'zl'=2] {'zh'}, dimensions={0} | all-to-all | bytes 589824 | tf_op jit(solution)/shard_map/all_to_all | solution.py:291
  248.0 1.7 shard_map.85
  249.7 19.1 %all_to_all.60.blocks = f32[32,8,128]{2,1,0:T(8,128)} all-to-all(f32[32,8,128]{2,1,0:T(8,128)} %get-tuple-element.30), channel_id=1, replica_groups=mesh['x'=4,'yh'=2,'c'=2,'yl'=2,'zh'=8,'zl'=2] {'yl','zh','zl'}, dimensions={0} | all-to-all | bytes 262144 | tf_op jit(solution)/shard_map/all_to_all | solution.py:291
  268.8 2.5 shard_map.86
  271.2 23.6 %all_to_all.61.parts = f32[16,32,256]{2,1,0:T(8,128)} all-to-all(f32[16,32,256]{2,1,0:T(8,128)} %bitcast.38), channel_id=1, replica_groups=mesh['x'=4,'yh'=2,'c'=2,'yl'=2,'zh'=8,'zl'=2] {'x','yh','c'}, dimensions={0} | all-to-all | bytes 1048576 | tf_op jit(solution)/shard_map/all_to_all | solution.py:291
  294.9 1.7 shard_map.87
  (25 shorter events, 0.1 us)
Async XLA Ops:
  0.6 36.2 %copy-start.8 = (f32[1,64,256]{2,1,0:T(8,128)S(1)}, f32[1,64,256]{2,1,0:T(8,128)}, u32[]{:S(2)}) copy-start(f32[1,64,256]{2,1,0:T(8,128)} %param.8) | copy-start | bytes 196612
  2.1 29.2 %all-to-all-start.1 = ((bf16[8,32,256]{2,1,0:T(8,128)(2,1)}), bf16[8,32,256]{2,1,0:T(8,128)(2,1)S(1)}, u32[]{:S(2)}, u32[]{:S(2)}) async-start(bf16[8,32,256]{2,1,0:T(8,128)(2,1)} %broadcast_in_dim.13), calls=%async_computation.1 | async-start | bytes 262144 | tf_op jit(solution)/shard_map/all_to_all | solution.py:291
  23.0 60.5 %collective-permute-start = (bf16[2,128,2048]{2,1,0:T(8,128)(2,1)}, bf16[2,128,2048]{2,1,0:T(8,128)(2,1)S(1)}, u32[]{:S(2)}, u32[]{:S(2)}) collective-permute-start(bf16[2,128,2048]{2,1,0:T(8,128)(2,1)} %get-tuple-element.19), channel_id=1, source_target_pairs={{0,16},{16,0},{1,17},{17,1},{2,18},{18,2},{3,19},{19,3},{4,20},{20... | collective-permute-start | bytes 3145736 | tf_op jit(solution)/shard_map/ppermute | solution.py:279
  26.2 66.0 %collective-permute-start.1 = (bf16[2,128,2048]{2,1,0:T(8,128)(2,1)}, bf16[2,128,2048]{2,1,0:T(8,128)(2,1)S(1)}, u32[]{:S(2)}, u32[]{:S(2)}) collective-permute-start(bf16[2,128,2048]{2,1,0:T(8,128)(2,1)} %get-tuple-element.20), channel_id=1, source_target_pairs={{0,1},{1,0},{2,3},{3,2},{4,5},{5,4},{6,7},{7,6},{8,9},{9,8},{10,11... | collective-permute-start | bytes 3145736 | tf_op jit(solution)/shard_map/ppermute | solution.py:279
  28.8 63.4 %collective-permute-start.2 = (bf16[2,128,2048]{2,1,0:T(8,128)(2,1)}, bf16[2,128,2048]{2,1,0:T(8,128)(2,1)S(1)}, u32[]{:S(2)}, u32[]{:S(2)}) collective-permute-start(bf16[2,128,2048]{2,1,0:T(8,128)(2,1)} %get-tuple-element.21), channel_id=1, source_target_pairs={{0,17},{1,16},{16,1},{17,0},{2,19},{3,18},{18,3},{19,2},{4,21},{5,... | collective-permute-start | bytes 3145736 | tf_op jit(solution)/shard_map/ppermute | solution.py:283
  32.0 21.9 %collective-permute-start.3 = (bf16[32,2048]{1,0:T(8,128)(2,1)}, bf16[32,2048]{1,0:T(8,128)(2,1)}, u32[]{:S(2)}, u32[]{:S(2)}) collective-permute-start(bf16[32,2048]{1,0:T(8,128)(2,1)} %bitcast.25), channel_id=1, source_target_pairs={{0,64},{64,0},{1,65},{65,1},{2,66},{66,2},{3,67},{67,3},{4,68},{68... | collective-permute-start | bytes 393224 | tf_op jit(solution)/shard_map/ppermute | solution.py:279
  37.6 54.6 %all-to-all-start = ((bf16[8,64,256]{2,1,0:T(8,128)(2,1)}), bf16[8,64,256]{2,1,0:T(8,128)(2,1)S(1)}, u32[]{:S(2)}, u32[]{:S(2)}) async-start(bf16[8,64,256]{2,1,0:T(8,128)(2,1)} %broadcast_in_dim.12), calls=%async_computation | async-start | bytes 524288 | tf_op jit(solution)/shard_map/all_to_all | solution.py:291
  54.8 28.6 %copy-start.4 = (bf16[2,32,2048]{2,1,0:T(8,128)(2,1)}, bf16[2,32,2048]{2,1,0:T(8,128)(2,1)S(1)}, u32[]{:S(2)}) copy-start(bf16[2,32,2048]{2,1,0:T(8,128)(2,1)S(1)} %pad_maximum_fusion.refs_7_) | copy-start | bytes 786436
  54.8 7.7 %collective-permute-start.6 = (bf16[2,32,2048]{2,1,0:T(8,128)(2,1)S(1)}, bf16[2,32,2048]{2,1,0:T(8,128)(2,1)}, u32[]{:S(2)}, u32[]{:S(2)}) collective-permute-start(bf16[2,32,2048]{2,1,0:T(8,128)(2,1)S(1)} %pad_maximum_fusion.refs_7_), channel_id=1, source_target_pairs={{0,384},{128,0},{256,128},{384,256},{1,385},{129,1},{257,129},{385... | collective-permute-start | bytes 786440 | tf_op jit(solution)/shard_map/ppermute | solution.py:287
  59.2 8.5 %collective-permute-start.4 = (bf16[2,32,2048]{2,1,0:T(8,128)(2,1)S(1)}, bf16[2,32,2048]{2,1,0:T(8,128)(2,1)}, u32[]{:S(2)}, u32[]{:S(2)}) collective-permute-start(bf16[2,32,2048]{2,1,0:T(8,128)(2,1)S(1)} %pad_maximum_fusion.refs_7_), channel_id=1, source_target_pairs={{0,128},{128,256},{256,384},{384,0},{1,129},{129,257},{257,385},{3... | collective-permute-start | bytes 786440 | tf_op jit(solution)/shard_map/ppermute | solution.py:287
  62.5 16.5 %collective-permute-start.5 = (bf16[2,32,2048]{2,1,0:T(8,128)(2,1)S(1)}, bf16[2,32,2048]{2,1,0:T(8,128)(2,1)}, u32[]{:S(2)}, u32[]{:S(2)}) collective-permute-start(bf16[2,32,2048]{2,1,0:T(8,128)(2,1)S(1)} %pad_maximum_fusion.refs_7_), channel_id=1, source_target_pairs={{0,256},{128,384},{256,0},{384,128},{1,257},{129,385},{257,1},{385... | collective-permute-start | bytes 786440 | tf_op jit(solution)/shard_map/ppermute | solution.py:287
  67.7 13.3 %collective-permute-start.7 = (bf16[2,32,2048]{2,1,0:T(8,128)(2,1)S(1)}, bf16[2,32,2048]{2,1,0:T(8,128)(2,1)S(1)}, u32[]{:S(2)}, u32[]{:S(2)}) collective-permute-start(bf16[2,32,2048]{2,1,0:T(8,128)(2,1)S(1)} %pad_maximum_fusion.refs_7_), channel_id=1, source_target_pairs={{0,32},{32,0},{1,33},{33,1},{2,34},{34,2},{3,35},{35,3},{4,36},{36... | collective-permute-start | bytes 786440 | tf_op jit(solution)/shard_map/ppermute | solution.py:279
  79.1 13.1 %collective-permute-start.10 = (bf16[2,32,2048]{2,1,0:T(8,128)(2,1)}, bf16[2,32,2048]{2,1,0:T(8,128)(2,1)}, u32[]{:S(2)}, u32[]{:S(2)}) collective-permute-start(bf16[2,32,2048]{2,1,0:T(8,128)(2,1)} %collective-permute-done.6.refs_10_), channel_id=1, source_target_pairs={{0,32},{32,0},{1,33},{33,1},{2,34},{34,2},{3,35},{35,3},{4,36},{36... | collective-permute-start | bytes 786440 | tf_op jit(solution)/shard_map/ppermute | solution.py:279
  81.0 2.4 copy-start.7
  81.0 11.2 %collective-permute-start.8 = (bf16[2,32,2048]{2,1,0:T(8,128)(2,1)}, bf16[2,32,2048]{2,1,0:T(8,128)(2,1)}, u32[]{:S(2)}, u32[]{:S(2)}) collective-permute-start(bf16[2,32,2048]{2,1,0:T(8,128)(2,1)} %collective-permute-done.4.refs_8_), channel_id=1, source_target_pairs={{0,32},{32,0},{1,33},{33,1},{2,34},{34,2},{3,35},{35,3},{4,36},{36... | collective-permute-start | bytes 786440 | tf_op jit(solution)/shard_map/ppermute | solution.py:279
  83.5 8.8 %copy-start = (bf16[2,128,2048]{2,1,0:T(8,128)(2,1)}, bf16[2,128,2048]{2,1,0:T(8,128)(2,1)S(1)}, u32[]{:S(2)}) copy-start(bf16[2,128,2048]{2,1,0:T(8,128)(2,1)S(1)} %collective-permute-done.refs_2_.rest_1_.refs_3_) | copy-start | bytes 3145732
  83.5 8.8 %collective-permute-start.9 = (bf16[2,32,2048]{2,1,0:T(8,128)(2,1)}, bf16[2,32,2048]{2,1,0:T(8,128)(2,1)}, u32[]{:S(2)}, u32[]{:S(2)}) collective-permute-start(bf16[2,32,2048]{2,1,0:T(8,128)(2,1)} %collective-permute-done.5.refs_9_), channel_id=1, source_target_pairs={{0,32},{32,0},{1,33},{33,1},{2,34},{34,2},{3,35},{35,3},{4,36},{36... | collective-permute-start | bytes 786440 | tf_op jit(solution)/shard_map/ppermute | solution.py:279
  92.2 0.8 copy-start.3
  92.2 1.1 copy-start.1
  92.2 1.4 copy-start.2
  129.2 23.4 %all-to-all-start.4 = ((bf16[8,72,256]{2,1,0:T(8,128)(2,1)}), bf16[8,72,256]{2,1,0:T(8,128)(2,1)S(1)}, u32[]{:S(2)}, u32[]{:S(2)}) async-start(bf16[8,72,256]{2,1,0:T(8,128)(2,1)} %shard_map.79), calls=%async_computation.4 | async-start | bytes 589824 | tf_op jit(solution)/shard_map/all_to_all | solution.py:291
  152.7 0.7 copy-start.5
  184.0 26.0 %all-to-all-start.6 = ((bf16[4,128,256]{2,1,0:T(8,128)(2,1)}), bf16[4,128,256]{2,1,0:T(8,128)(2,1)S(1)}, u32[]{:S(2)}, u32[]{:S(2)}) async-start(bf16[4,128,256]{2,1,0:T(8,128)(2,1)} %shard_map.81), calls=%async_computation.6 | async-start | bytes 524288 | tf_op jit(solution)/shard_map/all_to_all | solution.py:291
  196.6 8.5 %collective-permute-start.11 = (bf16[128,512]{1,0:T(8,128)(2,1)}, bf16[128,512]{1,0:T(8,128)(2,1)S(1)}, u32[]{:S(2)}, u32[]{:S(2)}) collective-permute-start(bf16[128,512]{1,0:T(8,128)(2,1)} %get-tuple-element.24), channel_id=1, source_target_pairs={{0,16},{16,0},{1,17},{17,1},{2,18},{18,2},{3,19},{19,3},{4,20},{20... | collective-permute-start | bytes 393224 | tf_op jit(solution)/shard_map/ppermute | solution.py:279
  200.1 5.9 %collective-permute-start.12 = (bf16[128,512]{1,0:T(8,128)(2,1)}, bf16[128,512]{1,0:T(8,128)(2,1)S(1)}, u32[]{:S(2)}, u32[]{:S(2)}) collective-permute-start(bf16[128,512]{1,0:T(8,128)(2,1)} %get-tuple-element.25), channel_id=1, source_target_pairs={{0,1},{1,0},{2,3},{3,2},{4,5},{5,4},{6,7},{7,6},{8,9},{9,8},{10,11... | collective-permute-start | bytes 393224 | tf_op jit(solution)/shard_map/ppermute | solution.py:279
  203.1 6.9 %collective-permute-start.13 = (bf16[128,512]{1,0:T(8,128)(2,1)}, bf16[128,512]{1,0:T(8,128)(2,1)S(1)}, u32[]{:S(2)}, u32[]{:S(2)}) collective-permute-start(bf16[128,512]{1,0:T(8,128)(2,1)} %get-tuple-element.26), channel_id=1, source_target_pairs={{0,17},{1,16},{16,1},{17,0},{2,19},{3,18},{18,3},{19,2},{4,21},{5,... | collective-permute-start | bytes 393224 | tf_op jit(solution)/shard_map/ppermute | solution.py:283
  205.1 4.9 %copy-start.9 = (bf16[128,512]{1,0:T(8,128)(2,1)}, bf16[128,512]{1,0:T(8,128)(2,1)S(1)}, u32[]{:S(2)}) copy-start(bf16[128,512]{1,0:T(8,128)(2,1)S(1)} %collective-permute-done.11.refs_2_) | copy-start | bytes 393220
  206.0 4.0 %copy-start.10 = (bf16[128,512]{1,0:T(8,128)(2,1)}, bf16[128,512]{1,0:T(8,128)(2,1)S(1)}, u32[]{:S(2)}) copy-start(bf16[128,512]{1,0:T(8,128)(2,1)S(1)} %collective-permute-done.12.refs_3_) | copy-start | bytes 393220
  210.0 0.7 copy-start.11
  210.0 0.8 copy-start.6

commit v5 on v4

--- a/solution.py
+++ b/solution.py
@@ -35,10 +35,6 @@
     return [pl.BlockSpec(memory_space=pltpu.VMEM)] * n
 
 
-def hbm(n):
-    return [pl.BlockSpec(memory_space=pl.ANY)] * n
-
-
 def smem():
     return pl.BlockSpec(memory_space=pltpu.SMEM)
 
@@ -66,60 +62,49 @@
 
 
 def partial_low(whole, tokens):
-    n = whole.shape[2]
-    part = dot(whole[0, :64], tokens[:, :n], 1, 1)
-    for z in range(1, NZ):
-        part = part + dot(whole[z, :64], tokens[:, z * n : (z + 1) * n], 1, 1)
-    return part
+    return dot(jnp.concatenate([whole[z, :64] for z in range(NZ)], axis=1), tokens, 1, 1)
 
 
 def keys_kernel(step, scale, idx, *rest):
-    x_refs, a_ref, y_ref, pieces = rest[:4], rest[4], rest[5], rest[6:14]
-    outs, (xs, bs, xsem, bsem) = rest[14:-4], rest[-4:]
-    rows, quarter = xs.shape[1:]
+    x_refs, pieces, y_ref, out, bs = rest[:4], rest[4:12], rest[12], rest[-2], rest[-1]
+    rows, quarter = x_refs[0].shape[1:]
     px, pyh, pc = idx[0], idx[1], idx[2]
     places = [group_at(idx, k) for k in range(4)]
-    copies = [pltpu.make_async_copy(ref.at[step], xs.at[k], xsem.at[k]) for k, ref in enumerate(x_refs)]
-    loads = []
-    for k, piece in enumerate(pieces):
-        dc, dx = divmod(k, 4)
-        for dy in range(2):
-            w = lax.rem(pyh + dy, 2) * 2 + lax.rem(pc + dc, 2)
-            loads.append(pltpu.make_async_copy(piece.at[dy], bs.at[dx, w], bsem.at[k * 2 + dy]))
-    for copy in copies + loads:
-        copy.start()
-    for copy in copies:
-        copy.wait()
+    tokens = jnp.concatenate([ref[0] for ref in x_refs], axis=0)
     if step == 0:
+        low = partial_low(rest[13], tokens) * scale
         for k in range(4):
-            hi, lo = split(partial_low(a_ref, xs[k]) * scale)
-            outs[0][places[k], rows : rows + 16] = wide(hi)
-            outs[0][places[k], rows + 16 :] = wide(lo)
-    tokens = xs[...].reshape(4 * rows, quarter)
+            hi, lo = split(low[:, k * rows : (k + 1) * rows])
+            out[places[k], rows : rows + 16] = wide(hi)
+            out[places[k], rows + 16 :] = wide(lo)
     for dx in range(4):
-        for k in (dx, dx + 4):
+        for dc in range(2):
             for dy in range(2):
-                loads[k * 2 + dy].wait()
+                w = lax.rem(pyh + dy, 2) * 2 + lax.rem(pc + dc, 2)
+                bs[dx, w] = pieces[4 * dc + dx][dy]
         at = pl.ds(pl.multiple_of(lax.rem(px + 4 - dx, 4) * 128, 128), 128)
         part = dot(tokens, bs[dx].reshape(128, quarter), 1, 1) * scale
         for k in range(4):
             value = part[k * rows : (k + 1) * rows]
             if k == 0:
-                value = value - y_ref[step, :, at].astype(f32)
-            if step == 0:
-                outs[0][places[k], :rows, at] = value.astype(bf16)
-            else:
-                outs[k][:, at] = value.astype(bf16)
-
-
-def low_kernel(scale, idx, whole, *rest):
-    x_refs, out = rest[:4], rest[4]
+                value = value - y_ref[0, :, at].astype(f32)
+            out[places[k], :rows, at] = value.astype(bf16)
+
+
+def low_kernel(scale, idx, keys, whole, *rest):
+    x_refs, out, held, sem = rest[:4], rest[4], rest[5], rest[6]
+    rows = x_refs[0].shape[1]
+    low = partial_low(whole, jnp.concatenate([ref[0] for ref in x_refs], axis=0)) * scale
+    quarter = jnp.concatenate([whole[z, 64:] for z in range(NZ)], axis=0)
     for k in range(4):
         at = group_at(idx, k)
-        hi, lo = split(partial_low(whole, x_refs[k][0]) * scale)
-        out[at, :64, :128] = hi
-        out[at, :64, 128:] = lo
-        out[at, 64:] = jnp.concatenate([whole[z, 64:] for z in range(NZ)], axis=0)
+        hi, lo = split(low[:, k * rows : (k + 1) * rows])
+        held[at, :, :128] = hi
+        held[at, :, 128:256] = lo
+        held[at, :, 256:] = quarter
+    copy = pltpu.make_async_copy(held, out.at[:, rows:, :], sem)
+    copy.start()
+    copy.wait()
 
 
 def quarter_of(blocks):
@@ -147,26 +132,31 @@
     error_of(total_rows, (k[0] + k[1]) + (k[2] + k[3]), (low[0] + low[1]) + (low[2] + low[3]), up_ref[...], out)
 
 
-def second_error_kernel(total_rows, parts, own, by_y, by_z, by_both, out):
-    keys = (own[...].astype(f32) + by_y[...].astype(f32)) + (by_z[...].astype(f32) + by_both[...].astype(f32))
-    low = [parts[q, :64, :128].astype(f32) + parts[q, :64, 128:].astype(f32) for q in range(4)]
-    up = jnp.concatenate([quarter_of(parts[q, 64:]) for q in range(4)], axis=0)
-    error_of(total_rows, keys, (low[0] + low[1]) + (low[2] + low[3]), up, out)
-
-
-def down_kernel(idx, parts, *rest):
+def second_error_kernel(total_rows, parts, out, up_out):
+    rows = parts.shape[1] - 64
+    k = [parts[q, :rows].astype(f32) for q in range(4)]
+    low = [parts[q, rows:, :128].astype(f32) + parts[q, rows:, 128:256].astype(f32) for q in range(4)]
+    up = jnp.concatenate([quarter_of(parts[q, rows:, 256:]) for q in range(4)], axis=0)
+    up_out[...] = up
+    error_of(total_rows, (k[0] + k[1]) + (k[2] + k[3]), (low[0] + low[1]) + (low[2] + low[3]), up, out)
+
+
+def down_kernel(whole_quarter, idx, parts, *rest):
     x_refs, out = rest[:4], rest[4]
-    backs = [tall(parts[group_at(idx, k), :16]) for k in range(4)]
+    back = jnp.concatenate([tall(parts[group_at(idx, k), :16]) for k in range(4)], axis=1)
     grads = [parts[q, 16:32].astype(f32) + parts[q, 32:].astype(f32) for q in range(4)]
     hi, lo = split((grads[0] + grads[1]) + (grads[2] + grads[3]))
+    tokens = jnp.concatenate([ref[0] for ref in x_refs], axis=0)
     n = out.shape[2]
     for z in range(NZ):
-        at = slice(z * n, (z + 1) * n)
-        part = [dot(backs[k], x_refs[k][0, :, at], 1, 0) for k in range(4)]
-        out[z, :64] = ((part[0] + part[1]) + (part[2] + part[3])).astype(bf16)
+        out[z, :64] = dot(back, tokens[:, z * n : (z + 1) * n], 1, 0).astype(bf16)
         r, c = z // 4, z % 4
-        out[z, 64:, :128] = hi[8 * r : 8 * r + 8, 128 * c : 128 * c + 128]
-        out[z, 64:, 128:] = lo[8 * r : 8 * r + 8, 128 * c : 128 * c + 128]
+        if whole_quarter:
+            out[z, 64:80] = hi[:, :n]
+            out[z, 80:96] = hi[:, n:]
+        else:
+            out[z, 64:, :128] = hi[8 * r : 8 * r + 8, 128 * c : 128 * c + 128]
+            out[z, 64:, 128:] = lo[8 * r : 8 * r + 8, 128 * c : 128 * c + 128]
 
 
 def summed(parts):
@@ -176,12 +166,11 @@
     return result
 
 
-def update_kernel(scale, parts, a_ref, b_ref, a_out, b_out, copies):
+def update_kernel(scale, parts, a_ref, b_ref, a_out, copies):
     grads = summed(parts)
     a = a_ref[...] - (rate_down * scale) * grads[:64]
     hi, lo = split(b_ref[...] - rate_up * (grads[64:, :128] + grads[64:, 128:]))
     a_out[...] = a
-    b_out[...] = hi.astype(f32) + lo.astype(f32)
     a_half = a.astype(bf16)
     for z in range(NZ):
         copies[z, :64] = a_half
@@ -189,25 +178,20 @@
         copies[z, 64:, 128:] = lo
 
 
-def last_update_kernel(scale, parts, a_ref, b_ref, a_out, copies):
+def last_update_kernel(scale, idx, parts, a_ref, up_ref, a_out, copies):
     grads = summed(parts)
     a_out[...] = a_ref[...] - (rate_down * scale) * grads[:64]
-    b = b_ref[...] - rate_up * (grads[64:, :128] + grads[64:, 128:])
-    for k in range(4 * NZ):
-        copies[k] = b
-
-
-def change_kernel(a_ref, blocks, a_start, up_start, out, b_out):
-    rows = []
+    at = pl.ds(pl.multiple_of(16 * group_at(idx, 0), 16), 16)
+    b = up_ref[at, :] - rate_up * jnp.concatenate([grads[64:80], grads[80:96]], axis=1)
     for q in range(4):
-        yl, zl = q // 2, q % 2
-        for r in range(2):
-            at = [yl * 2 * NZ + (4 * r + c) * 2 + zl for c in range(4)]
-            rows.append(jnp.concatenate([blocks[k] for k in at], axis=1))
-    up = jnp.concatenate(rows, axis=0)
+        copies[q] = b
+
+
+def change_kernel(a_ref, quarters, a_start, up_start, out, b_out):
+    up = jnp.concatenate([quarters[q] for q in range(4)], axis=0)
     left = jnp.concatenate([up, -up_start[...]], axis=0)
     right = jnp.concatenate([a_ref[...], a_start[...]], axis=0)
-    out[...] = branch_scale * dot(left, right, 0, 0, HIGH)
+    out[...] = (branch_scale * dot(left, right, 0, 0, HIGH)).astype(bf16)
     b_out[...] = up
 
 
@@ -255,7 +239,7 @@
     )(idx, *args, *xs)
 
 
-def keys_of(step, scale, idx, xs, whole, targets, pieces, shapes):
+def keys_of(step, scale, idx, shape, xs, targets, pieces, *more):
     _, rows, quarter = xs[0].shape
 
     def body(*refs):
@@ -263,16 +247,41 @@
 
     return pl.pallas_call(
         body,
-        out_shape=shapes,
-        in_specs=[smem()] + hbm(4) + vmem(2) + hbm(8),
-        scratch_shapes=[
-            pltpu.VMEM((4, rows, quarter), bf16),
-            pltpu.VMEM((4, 4, 32, quarter), bf16),
-            pltpu.SemaphoreType.DMA((4,)),
-            pltpu.SemaphoreType.DMA((16,)),
-        ],
-        compiler_params=VMEM,
-    )(idx, *xs, whole, targets, *pieces)
+        out_shape=shape,
+        grid_spec=pltpu.PrefetchScalarGridSpec(
+            num_scalar_prefetch=1,
+            grid=(1,),
+            in_specs=[pl.BlockSpec((1, rows, quarter), lambda i, s: (step, 0, 0))] * 4
+            + [pl.BlockSpec(a.shape, lambda i, s: (0, 0, 0)) for a in pieces]
+            + [pl.BlockSpec((1, rows, 512), lambda i, s: (step, 0, 0))]
+            + [pl.BlockSpec(a.shape, lambda i, s: (0, 0, 0)) for a in more],
+            out_specs=pl.BlockSpec((4, rows + 32 * (1 - step), 512), lambda i, s: (0, 0, 0)),
+            scratch_shapes=[pltpu.VMEM((4, 4, 32, quarter), bf16)],
+        ),
+        compiler_params=VMEM,
+    )(idx, *xs, *pieces, targets, *more)
+
+
+def low_of(scale, idx, keys, whole, xs):
+    _, rows, quarter = xs[0].shape
+
+    def body(*refs):
+        low_kernel(scale, *refs)
+
+    return pl.pallas_call(
+        body,
+        out_shape=shaped(keys.shape, bf16),
+        grid_spec=pltpu.PrefetchScalarGridSpec(
+            num_scalar_prefetch=1,
+            grid=(1,),
+            in_specs=[pl.BlockSpec(memory_space=pl.ANY), pl.BlockSpec(whole.shape, lambda i, s: (0, 0, 0))]
+            + [pl.BlockSpec((1, rows, quarter), lambda i, s: (1, 0, 0))] * 4,
+            out_specs=pl.BlockSpec(memory_space=pl.ANY),
+            scratch_shapes=[pltpu.VMEM((4, 64, 512), bf16), pltpu.SemaphoreType.DMA],
+        ),
+        input_output_aliases={1: 0},
+        compiler_params=VMEM,
+    )(idx, keys, whole, *xs)
 
 
 def swap(value, axis):
@@ -316,45 +325,45 @@
     whole = gather_z(a_start.astype(bf16))
     pieces = near + [swap(piece, "c") for piece in near]
 
-    keys_shape = shaped((rows, 512), bf16)
     error_shape = shaped((4, 48, 512), bf16)
-    down_shape = shaped((NZ, 72, 256), bf16)
 
     def gradients(step, mine):
         shared = exchange(mine, Q)
-        return exchange(with_tokens(down_kernel, step, down_shape, idx, (shared,), xs), "zh")
-
-    keys = keys_of(0, scale, idx, xs, whole, targets[0], pieces, shaped((4, rows + 32, 512), bf16))
+
+        def body(*refs):
+            down_kernel(step == 1, *refs)
+
+        shape = shaped((NZ, 96 if step else 72, 256), bf16)
+        return exchange(with_tokens(body, step, shape, idx, (shared,), xs), "zh")
+
+    keys = keys_of(0, scale, idx, shaped((4, rows + 32, 512), bf16), xs, targets[0], pieces, whole)
     parts = exchange(keys, Q)
     mine = call(lambda *refs: first_error_kernel(total_rows, *refs), error_shape, parts, up_start)
     parts = gradients(0, mine)
 
-    keys = keys_of(1, scale, idx, xs, whole, targets[0], pieces, [keys_shape] * 4)
-    keys = (keys[0], swap(keys[1], "yl"), swap(keys[2], "zl"), swap_both(keys[3]))
-    a_next, block, copies = call(
+    keys = keys_of(1, scale, idx, shaped((4, rows + 64, 512), bf16), xs, targets[0], pieces)
+    a_next, copies = call(
         lambda *refs: update_kernel(scale, *refs),
-        (shaped((64, 256), f32), shaped((8, 128), f32), down_shape),
+        (shaped((64, 256), f32), shaped((NZ, 72, 256), bf16)),
         parts,
         a_start,
         block,
     )
     whole = exchange(copies, "zh")
-    low = with_tokens(
-        lambda *refs: low_kernel(scale, *refs), 1, shaped((4, 128, 256), bf16), idx, (whole,), xs
+    low = exchange(low_of(scale, idx, keys, whole, xs), Q)
+    mine, up_next = call(
+        lambda *refs: second_error_kernel(total_rows, *refs), (error_shape, shaped((64, 512), f32)), low
     )
-    low = exchange(low, Q)
-    mine = call(lambda *refs: second_error_kernel(total_rows, *refs), error_shape, low, *keys)
     parts = gradients(1, mine)
-    a_last, copies = call(
+    a_last, copies = pl.pallas_call(
         lambda *refs: last_update_kernel(scale, *refs),
-        (shaped((64, 256), f32), shaped((4 * NZ, 8, 128), f32)),
-        parts,
-        a_next,
-        block,
-    )
-    blocks = exchange(copies, F)
+        out_shape=(shaped((64, 256), f32), shaped((4, 16, 512), f32)),
+        in_specs=[smem()] + vmem(3),
+        compiler_params=VMEM,
+    )(idx, parts, a_next, up_next)
+    quarters = exchange(copies, Q)
     change, b_last = call(
-        change_kernel, (shaped((512, 256), f32), shaped((64, 512), f32)), a_last, blocks, a_start, up_start
+        change_kernel, (shaped((512, 256), bf16), shaped((64, 512), f32)), a_last, quarters, a_start, up_start
     )
     merged = exchange(change.reshape(16, 32, 256), W)
     new_base = call(merge_kernel, shaped(base.shape[::-1], f32), merged, base.T)

time: 298 us -> 274 us (0.919)
  blocking collectives: 118 us -> 100 us
  waiting for transfers between devices: 32.2 us -> 39.1 us
  Pallas kernels: 47.7 us -> 41.1 us
  starting transfers between devices: 87.3 us -> 82.6 us
    all_to_all x7, blocking collectives: 118 us -> 100 us  [exchange(): return lax.all_to_all(parts, axis, 0, 0, tiled=True)]
    all_to_all x4, waiting for transfers between devices: 22 us -> 32.3 us  [exchange(): return lax.all_to_all(parts, axis, 0, 0, tiled=True)]
    ppermute x9 -> x7, starting transfers between devices: 34.7 us -> 28.3 us  [swap(): return lax.ppermute(value, axis, [(0, 1), (1, 0)])]
    ppermute x2 -> x1, waiting for transfers between devices: 3.96 us -> 0.01 us  [swap_both(): return lax.ppermute(value, Q, [(k, 3 - k) for k in range(4)])]
    pallas_call x3 -> x2, Pallas kernels: 10.6 us -> 6.91 us  [with_tokens(): pl.pallas_call(kernel, out_shape=shape, grid_spec=pltpu.PrefetchScalarGri...]
    all_to_all x4, starting transfers between devices: 37.4 us -> 41 us  [exchange(): return lax.all_to_all(parts, axis, 0, 0, tiled=True)]
    pallas_call x6 -> x5, Pallas kernels: 13.1 us -> 11.1 us  [call(): pl.pallas_call(kernel, out_shape=shapes, in_specs=vmem(len(args)), compil...]
    pallas_call x2 -> x4, Pallas kernels: 19.4 us -> 18.5 us  [the longest x2 13 us: keys_of(): pl.pallas_call(body, out_shape=shape, grid_spec=pltpu.PrefetchScalarGridS...]
  transfers between devices with their start and end apart: 18 -> 15, of which waited for: 7 -> 6; matrix products, arithmetic and copies ran while one was open for 2% -> 2% of each run, Pallas kernels for 5% -> 4%
where the time goes in v5:
time: 274 us; the launch traced here: 272 us
  blocking collectives  100 us (36%)
  starting transfers between devices  82.6 us (30%)
  Pallas kernels  41.1 us (15%)
  waiting for transfers between devices  39.1 us (14%)
  local copies, waits for them, and re-layouts  6.79 us (2%)
    all_to_all x7, blocking collectives, exchange(): return lax.all_to_all(parts, axis, 0, 0, tiled=True)  100 us
    all_to_all x4, starting transfers between devices, exchange(): return lax.all_to_all(parts, axis, 0, 0, tiled=True)  41 us
    all_to_all x4, waiting for transfers between devices, exchange(): return lax.all_to_all(parts, axis, 0, 0, tiled=True)  32.3 us
    ppermute x7, starting transfers between devices, swap(): return lax.ppermute(value, axis, [(0, 1), (1, 0)])  28.3 us
    pallas_call x2, Pallas kernels, keys_of(): pl.pallas_call(body, out_shape=shape, grid_spec=pltpu.PrefetchScalarGridS...  13 us
    pallas_call x5, Pallas kernels, call(): pl.pallas_call(kernel, out_shape=shapes, in_specs=vmem(len(args)), compil...  11.1 us
    ppermute x3, starting transfers between devices, shift(): lax.ppermute(value, axis, [(i, (i + by) % count) for i in range(count)])  10.8 us
    pallas_call x2, Pallas kernels, with_tokens(): pl.pallas_call(kernel, out_shape=shape, grid_spec=pltpu.PrefetchScalarGri...  6.91 us
  transfers between devices with their start and end apart: 15, of which 6 were waited for; matrix products, arithmetic and copies ran while one was open for 2% of the time, Pallas kernels for 4%

profile of v5, /device:TPU:1, one launch (start us, length us, event | category | flops | bytes accessed | tf_op | source)
XLA Modules:
  0.0 272.2 jit_solution(5180319167285055814)
XLA Ops:
  0.6 0.0 copy-start.7
  0.6 0.8 bitcast_convert_fusion.1
  1.4 0.7 broadcast_in_dim.12
  2.1 15.6 %all-to-all-start = ((bf16[8,32,256]{2,1,0:T(8,128)(2,1)}), bf16[8,32,256]{2,1,0:T(8,128)(2,1)S(1)}, u32[]{:S(2)}, u32[]{:S(2)}) async-start(bf16[8,32,256]{2,1,0:T(8,128)(2,1)} %broadcast_in_dim.12), calls=%async_computation | async-start | bytes 262144 | tf_op jit(solution)/shard_map/all_to_all | solution.py:300
  17.7 0.6 stack.33.idx.refs_0_
  18.3 4.6 %shard_map.76 = (bf16[2,128,2048]{2,1,0:T(8,128)(2,1)}, bf16[2,128,2048]{2,1,0:T(8,128)(2,1)}, bf16[2,128,2048]{2,1,0:T(8,128)(2,1)}, bf16[2,128,2048]{2,1,0:T(8,128)(2,1)}) custom-call(s32[6]{0:T(128)} %stack.33.idx.refs_0_, bf16[2,128,8192]{2,1,0:T(8,128)(2,1)} %bitcast.29), custom_call_target="tpu_custom_call" | custom-call | tf_op jit(solution)/shard_map/pallas_call | solution.py:213
  22.9 3.2 %collective-permute-start = (bf16[2,128,2048]{2,1,0:T(8,128)(2,1)}, bf16[2,128,2048]{2,1,0:T(8,128)(2,1)S(1)}, u32[]{:S(2)}, u32[]{:S(2)}) collective-permute-start(bf16[2,128,2048]{2,1,0:T(8,128)(2,1)} %get-tuple-element.16), channel_id=1, source_target_pairs={{0,16},{16,0},{1,17},{17,1},{2,18},{18,2},{3,19},{19,3},{4,20},{20... | collective-permute-start | bytes 3145736 | tf_op jit(solution)/shard_map/ppermute | solution.py:288
  26.1 2.6 collective-permute-start.1
  28.8 2.5 collective-permute-start.2
  31.3 0.0 all-to-all-done
  31.3 0.7 copy.11
  32.0 4.8 %collective-permute-start.3 = (bf16[32,2048]{1,0:T(8,128)(2,1)}, bf16[32,2048]{1,0:T(8,128)(2,1)}, u32[]{:S(2)}, u32[]{:S(2)}) collective-permute-start(bf16[32,2048]{1,0:T(8,128)(2,1)} %bitcast.25), channel_id=1, source_target_pairs={{0,64},{64,0},{1,65},{65,1},{2,66},{66,2},{3,67},{67,3},{4,68},{68... | collective-permute-start | bytes 393224 | tf_op jit(solution)/shard_map/ppermute | solution.py:288
  36.8 0.7 broadcast_in_dim.13
  37.5 11.5 %all-to-all-start.1 = ((bf16[8,64,256]{2,1,0:T(8,128)(2,1)}), bf16[8,64,256]{2,1,0:T(8,128)(2,1)}, u32[]{:S(2)}, u32[]{:S(2)}) async-start(bf16[8,64,256]{2,1,0:T(8,128)(2,1)} %broadcast_in_dim.13), calls=%async_computation.1 | async-start | bytes 524288 | tf_op jit(solution)/shard_map/all_to_all | solution.py:300
  49.0 0.1 copy.9
  49.1 0.1 stack_reshape.3
  49.1 4.7 %collective-permute-done.3 = bf16[32,2048]{1,0:T(8,128)(2,1)} collective-permute-done((bf16[32,2048]{1,0:T(8,128)(2,1)}, bf16[32,2048]{1,0:T(8,128)(2,1)}, u32[]{:S(2)}, u32[]{:S(2)}) %collective-permute-start.3) | collective-permute-done | bytes 131104 | tf_op jit(solution)/shard_map/ppermute | solution.py:288
  53.8 0.9 pad_maximum_fusion.refs_5_
  54.8 0.0 copy-start.3
  54.8 4.4 %collective-permute-start.6 = (bf16[2,32,2048]{2,1,0:T(8,128)(2,1)S(1)}, bf16[2,32,2048]{2,1,0:T(8,128)(2,1)}, u32[]{:S(2)}, u32[]{:S(2)}) collective-permute-start(bf16[2,32,2048]{2,1,0:T(8,128)(2,1)S(1)} %pad_maximum_fusion.refs_5_), channel_id=1, source_target_pairs={{0,384},{128,0},{256,128},{384,256},{1,385},{129,1},{257,129},{385... | collective-permute-start | bytes 786440 | tf_op jit(solution)/shard_map/ppermute | solution.py:296
  59.2 1.9 collective-permute-start.4
  61.1 1.4 collective-permute-done.6.refs_8_
  62.5 4.5 %collective-permute-start.5 = (bf16[2,32,2048]{2,1,0:T(8,128)(2,1)S(1)}, bf16[2,32,2048]{2,1,0:T(8,128)(2,1)}, u32[]{:S(2)}, u32[]{:S(2)}) collective-permute-start(bf16[2,32,2048]{2,1,0:T(8,128)(2,1)S(1)} %pad_maximum_fusion.refs_5_), channel_id=1, source_target_pairs={{0,256},{128,384},{256,0},{384,128},{1,257},{129,385},{257,1},{385... | collective-permute-start | bytes 786440 | tf_op jit(solution)/shard_map/ppermute | solution.py:296
  66.9 0.7 collective-permute-done.4.refs_6_
  67.6 11.4 %collective-permute-start.7 = (bf16[2,32,2048]{2,1,0:T(8,128)(2,1)S(1)}, bf16[2,32,2048]{2,1,0:T(8,128)(2,1)S(1)}, u32[]{:S(2)}, u32[]{:S(2)}) collective-permute-start(bf16[2,32,2048]{2,1,0:T(8,128)(2,1)S(1)} %pad_maximum_fusion.refs_5_), channel_id=1, source_target_pairs={{0,32},{32,0},{1,33},{33,1},{2,34},{34,2},{3,35},{35,3},{4,36},{36... | collective-permute-start | bytes 786440 | tf_op jit(solution)/shard_map/ppermute | solution.py:288
  79.0 0.0 collective-permute-done.5.refs_7_
  79.0 1.9 collective-permute-start.10
  80.9 0.0 collective-permute-done.7.refs_9_
  81.0 2.4 collective-permute-start.8
  83.4 0.0 collective-permute-done.refs_2_.refs_3_.refs_4_
  83.4 1.9 collective-permute-start.9
  85.3 6.9 %all-to-all-done.1.refs_14_ = bf16[8,64,256]{2,1,0:T(8,128)(2,1)} async-done(((bf16[8,64,256]{2,1,0:T(8,128)(2,1)}), bf16[8,64,256]{2,1,0:T(8,128)(2,1)}, u32[]{:S(2)}, u32[]{:S(2)}) %all-to-all-start.1) | async-done | bytes 262176 | tf_op jit(solution)/shard_map/all_to_all | solution.py:300
  92.2 0.0 collective-permute-done.1.refs_3_.refs_4_.refs_5_
  92.2 0.0 collective-permute-done.2.refs_4_.refs_5_.refs_6_
  92.2 0.0 collective-permute-done.10.refs_12_
  92.3 0.0 collective-permute-done.8.refs_10_
  92.3 0.0 collective-permute-done.9.refs_11_
  92.3 0.9 copy-done.1
  93.2 0.3 copy-done.2
  93.5 6.9 %shard_map.78 = bf16[4,160,512]{2,1,0:T(8,128)(2,1)} custom-call(s32[6]{0:T(128)} %stack.33.idx.refs_0_, bf16[2,128,2048]{2,1,0:T(8,128)(2,1)} %get-tuple-element.15.refs_1_.refs_2_.refs_3_, bf16[2,128,2048]{2,1,0:T(8,128)(2,1)} %copy-done, bf16[2,128,2048]{2,1,0:T(8,128)(2,1)} %copy-done.1, bf16[2,128,2048]{2,1,0:T(8,128)(2,1)} %copy-done.2, ...), custom_call_target="tpu_custom_call" | custom-call | tf_op jit(solution)/shard_map/pallas_call | solution.py:248
  100.4 10.9 %all_to_all.55.refs_0_ = bf16[4,160,512]{2,1,0:T(8,128)(2,1)} all-to-all(bf16[4,160,512]{2,1,0:T(8,128)(2,1)} %shard_map.78), channel_id=1, replica_groups=mesh['x'=4,'yh'=2,'c'=2,'yl'=2,'zh'=8,'zl'=2] {'yl','zl'}, dimensions={0} | all-to-all | bytes 1310720 | tf_op jit(solution)/shard_map/all_to_all | solution.py:300
  111.3 2.7 shard_map.79
  114.0 8.5 %all_to_all.56.refs_1_ = bf16[4,48,512]{2,1,0:T(8,128)(2,1)} all-to-all(bf16[4,48,512]{2,1,0:T(8,128)(2,1)} %shard_map.79), channel_id=1, replica_groups=mesh['x'=4,'yh'=2,'c'=2,'yl'=2,'zh'=8,'zl'=2] {'yl','zl'}, dimensions={0} | all-to-all | bytes 393216 | tf_op jit(solution)/shard_map/all_to_all | solution.py:300
  122.4 3.4 %shard_map.80 = bf16[8,72,256]{2,1,0:T(8,128)(2,1)} custom-call(s32[6]{0:T(128)} %stack.33.idx.refs_0_, bf16[4,48,512]{2,1,0:T(8,128)(2,1)} %all_to_all.56.refs_1_, bf16[2,128,2048]{2,1,0:T(8,128)(2,1)} %get-tuple-element.15.refs_1_.refs_2_.refs_3_, bf16[2,128,2048]{2,1,0:T(8,128)(2,1)} %copy-done, bf16[2,128,2048]{2,1,0:T(8,128)(2,1)} %copy-done.1, ...), custom_call_target="tpu_custom_call" | custom-call | tf_op jit(solution)/shard_map/pallas_call | solution.py:228
  125.9 6.8 %all-to-all-start.4 = ((bf16[8,72,256]{2,1,0:T(8,128)(2,1)}), bf16[8,72,256]{2,1,0:T(8,128)(2,1)S(1)}, u32[]{:S(2)}, u32[]{:S(2)}) async-start(bf16[8,72,256]{2,1,0:T(8,128)(2,1)} %shard_map.80), calls=%async_computation.4 | async-start | bytes 589824 | tf_op jit(solution)/shard_map/all_to_all | solution.py:300
  132.7 1.3 dynamic-slice_bitcast_fusion.refs_2_
  134.0 15.3 %all-to-all-done.4.refs_0_ = bf16[8,72,256]{2,1,0:T(8,128)(2,1)S(1)} async-done(((bf16[8,72,256]{2,1,0:T(8,128)(2,1)}), bf16[8,72,256]{2,1,0:T(8,128)(2,1)S(1)}, u32[]{:S(2)}, u32[]{:S(2)}) %all-to-all-start.4) | async-done | bytes 294944 | tf_op jit(solution)/shard_map/all_to_all | solution.py:300
  149.3 0.7 copy-done.5
  150.0 1.8 shard_map.81
  151.8 7.1 %all-to-all-start.5 = ((bf16[8,72,256]{2,1,0:T(8,128)(2,1)}), bf16[8,72,256]{2,1,0:T(8,128)(2,1)S(1)}, u32[]{:S(2)}, u32[]{:S(2)}) async-start(bf16[8,72,256]{2,1,0:T(8,128)(2,1)} %get-tuple-element.19), calls=%async_computation.5 | async-start | bytes 589824 | tf_op jit(solution)/shard_map/all_to_all | solution.py:300
  158.9 6.1 %shard_map.77.refs_1_ = bf16[4,192,512]{2,1,0:T(8,128)(2,1)} custom-call(s32[6]{0:T(128)} %stack.33.idx.refs_0_, bf16[2,128,2048]{2,1,0:T(8,128)(2,1)} %get-tuple-element.15.refs_1_.refs_2_.refs_3_, bf16[2,128,2048]{2,1,0:T(8,128)(2,1)} %copy-done, bf16[2,128,2048]{2,1,0:T(8,128)(2,1)} %copy-done.1, bf16[2,128,2048]{2,1,0:T(8,128)(2,1)} %copy-done.2, ...), custom_call_target="tpu_custom_call" | custom-call | tf_op jit(solution)/shard_map/pallas_call | solution.py:248
  165.0 10.1 %all-to-all-done.5.refs_2_ = bf16[8,72,256]{2,1,0:T(8,128)(2,1)S(1)} async-done(((bf16[8,72,256]{2,1,0:T(8,128)(2,1)}), bf16[8,72,256]{2,1,0:T(8,128)(2,1)S(1)}, u32[]{:S(2)}, u32[]{:S(2)}) %all-to-all-start.5) | async-done | bytes 294944 | tf_op jit(solution)/shard_map/all_to_all | solution.py:300
  175.1 0.7 copy-done.4
  175.8 3.8 %shard_map.82 = bf16[4,192,512]{2,1,0:T(8,128)(2,1)} custom-call(s32[6]{0:T(128)} %stack.33.idx.refs_0_, bf16[4,192,512]{2,1,0:T(8,128)(2,1)} %shard_map.77.refs_1_, bf16[8,72,256]{2,1,0:T(8,128)(2,1)} %copy-done.4, bf16[2,128,2048]{2,1,0:T(8,128)(2,1)} %get-tuple-element.15.refs_1_.refs_2_.refs_3_, ...), custom_call_target="tpu_custom_call", output_to_operand_aliasing={{}: (1, {})} | custom-call | tf_op jit(solution)/shard_map/pallas_call | solution.py:271
  179.6 11.7 %all_to_all.57.refs_0_ = bf16[4,192,512]{2,1,0:T(8,128)(2,1)} all-to-all(bf16[4,192,512]{2,1,0:T(8,128)(2,1)} %shard_map.82), channel_id=1, replica_groups=mesh['x'=4,'yh'=2,'c'=2,'yl'=2,'zh'=8,'zl'=2] {'yl','zl'}, dimensions={0} | all-to-all | bytes 1572864 | tf_op jit(solution)/shard_map/all_to_all | solution.py:300
  191.3 2.7 shard_map.83
  194.0 8.5 %all_to_all.58.refs_1_ = bf16[4,48,512]{2,1,0:T(8,128)(2,1)} all-to-all(bf16[4,48,512]{2,1,0:T(8,128)(2,1)} %get-tuple-element.20), channel_id=1, replica_groups=mesh['x'=4,'yh'=2,'c'=2,'yl'=2,'zh'=8,'zl'=2] {'yl','zl'}, dimensions={0} | all-to-all | bytes 393216 | tf_op jit(solution)/shard_map/all_to_all | solution.py:300
  202.4 3.5 %shard_map.84 = bf16[8,96,256]{2,1,0:T(8,128)(2,1)} custom-call(s32[6]{0:T(128)} %stack.33.idx.refs_0_, bf16[4,48,512]{2,1,0:T(8,128)(2,1)} %all_to_all.58.refs_1_, bf16[2,128,2048]{2,1,0:T(8,128)(2,1)} %get-tuple-element.15.refs_1_.refs_2_.refs_3_, bf16[2,128,2048]{2,1,0:T(8,128)(2,1)} %copy-done, bf16[2,128,2048]{2,1,0:T(8,128)(2,1)} %copy-done.1, ...), custom_call_target="tpu_custom_call" | custom-call | tf_op jit(solution)/shard_map/pallas_call | solution.py:228
  205.9 30.6 %all_to_all.59.refs_1_ = bf16[8,96,256]{2,1,0:T(8,128)(2,1)} all-to-all(bf16[8,96,256]{2,1,0:T(8,128)(2,1)} %shard_map.84), channel_id=1, replica_groups=mesh['x'=4,'yh'=2,'c'=2,'yl'=2,'zh'=8,'zl'=2] {'zh'}, dimensions={0} | all-to-all | bytes 786432 | tf_op jit(solution)/shard_map/all_to_all | solution.py:300
  236.5 1.8 shard_map.85
  238.3 7.9 %all_to_all.60.quarters = f32[4,16,512]{2,1,0:T(8,128)} all-to-all(f32[4,16,512]{2,1,0:T(8,128)} %get-tuple-element.24), channel_id=1, replica_groups=mesh['x'=4,'yh'=2,'c'=2,'yl'=2,'zh'=8,'zl'=2] {'yl','zl'}, dimensions={0} | all-to-all | bytes 262144 | tf_op jit(solution)/shard_map/all_to_all | solution.py:300
  246.2 2.4 shard_map.86
  248.6 22.0 %all_to_all.61.parts = bf16[16,32,256]{2,1,0:T(8,128)(2,1)} all-to-all(bf16[16,32,256]{2,1,0:T(8,128)(2,1)} %bitcast.38), channel_id=1, replica_groups=mesh['x'=4,'yh'=2,'c'=2,'yl'=2,'zh'=8,'zl'=2] {'x','yh','c'}, dimensions={0} | all-to-all | bytes 524288 | tf_op jit(solution)/shard_map/all_to_all | solution.py:300
  270.6 1.6 shard_map.87
  (11 shorter events, 0.0 us)
Async XLA Ops:
  0.6 36.2 %copy-start.7 = (f32[1,64,256]{2,1,0:T(8,128)S(1)}, f32[1,64,256]{2,1,0:T(8,128)}, u32[]{:S(2)}) copy-start(f32[1,64,256]{2,1,0:T(8,128)} %param.8) | copy-start | bytes 196612
  2.1 29.2 %all-to-all-start = ((bf16[8,32,256]{2,1,0:T(8,128)(2,1)}), bf16[8,32,256]{2,1,0:T(8,128)(2,1)S(1)}, u32[]{:S(2)}, u32[]{:S(2)}) async-start(bf16[8,32,256]{2,1,0:T(8,128)(2,1)} %broadcast_in_dim.12), calls=%async_computation | async-start | bytes 262144 | tf_op jit(solution)/shard_map/all_to_all | solution.py:300
  22.9 60.5 %collective-permute-start = (bf16[2,128,2048]{2,1,0:T(8,128)(2,1)}, bf16[2,128,2048]{2,1,0:T(8,128)(2,1)S(1)}, u32[]{:S(2)}, u32[]{:S(2)}) collective-permute-start(bf16[2,128,2048]{2,1,0:T(8,128)(2,1)} %get-tuple-element.16), channel_id=1, source_target_pairs={{0,16},{16,0},{1,17},{17,1},{2,18},{18,2},{3,19},{19,3},{4,20},{20... | collective-permute-start | bytes 3145736 | tf_op jit(solution)/shard_map/ppermute | solution.py:288
  26.1 66.1 %collective-permute-start.1 = (bf16[2,128,2048]{2,1,0:T(8,128)(2,1)}, bf16[2,128,2048]{2,1,0:T(8,128)(2,1)S(1)}, u32[]{:S(2)}, u32[]{:S(2)}) collective-permute-start(bf16[2,128,2048]{2,1,0:T(8,128)(2,1)} %get-tuple-element.17), channel_id=1, source_target_pairs={{0,1},{1,0},{2,3},{3,2},{4,5},{5,4},{6,7},{7,6},{8,9},{9,8},{10,11... | collective-permute-start | bytes 3145736 | tf_op jit(solution)/shard_map/ppermute | solution.py:288
  28.8 63.5 %collective-permute-start.2 = (bf16[2,128,2048]{2,1,0:T(8,128)(2,1)}, bf16[2,128,2048]{2,1,0:T(8,128)(2,1)S(1)}, u32[]{:S(2)}, u32[]{:S(2)}) collective-permute-start(bf16[2,128,2048]{2,1,0:T(8,128)(2,1)} %get-tuple-element.18), channel_id=1, source_target_pairs={{0,17},{1,16},{16,1},{17,0},{2,19},{3,18},{18,3},{19,2},{4,21},{5,... | collective-permute-start | bytes 3145736 | tf_op jit(solution)/shard_map/ppermute | solution.py:292
  32.0 21.9 %collective-permute-start.3 = (bf16[32,2048]{1,0:T(8,128)(2,1)}, bf16[32,2048]{1,0:T(8,128)(2,1)}, u32[]{:S(2)}, u32[]{:S(2)}) collective-permute-start(bf16[32,2048]{1,0:T(8,128)(2,1)} %bitcast.25), channel_id=1, source_target_pairs={{0,64},{64,0},{1,65},{65,1},{2,66},{66,2},{3,67},{67,3},{4,68},{68... | collective-permute-start | bytes 393224 | tf_op jit(solution)/shard_map/ppermute | solution.py:288
  37.5 54.7 %all-to-all-start.1 = ((bf16[8,64,256]{2,1,0:T(8,128)(2,1)}), bf16[8,64,256]{2,1,0:T(8,128)(2,1)}, u32[]{:S(2)}, u32[]{:S(2)}) async-start(bf16[8,64,256]{2,1,0:T(8,128)(2,1)} %broadcast_in_dim.13), calls=%async_computation.1 | async-start | bytes 524288 | tf_op jit(solution)/shard_map/all_to_all | solution.py:300
  54.8 37.5 %copy-start.3 = (bf16[2,32,2048]{2,1,0:T(8,128)(2,1)}, bf16[2,32,2048]{2,1,0:T(8,128)(2,1)S(1)}, u32[]{:S(2)}) copy-start(bf16[2,32,2048]{2,1,0:T(8,128)(2,1)S(1)} %pad_maximum_fusion.refs_5_) | copy-start | bytes 786436
  54.8 7.7 %collective-permute-start.6 = (bf16[2,32,2048]{2,1,0:T(8,128)(2,1)S(1)}, bf16[2,32,2048]{2,1,0:T(8,128)(2,1)}, u32[]{:S(2)}, u32[]{:S(2)}) collective-permute-start(bf16[2,32,2048]{2,1,0:T(8,128)(2,1)S(1)} %pad_maximum_fusion.refs_5_), channel_id=1, source_target_pairs={{0,384},{128,0},{256,128},{384,256},{1,385},{129,1},{257,129},{385... | collective-permute-start | bytes 786440 | tf_op jit(solution)/shard_map/ppermute | solution.py:296
  59.2 8.5 %collective-permute-start.4 = (bf16[2,32,2048]{2,1,0:T(8,128)(2,1)S(1)}, bf16[2,32,2048]{2,1,0:T(8,128)(2,1)}, u32[]{:S(2)}, u32[]{:S(2)}) collective-permute-start(bf16[2,32,2048]{2,1,0:T(8,128)(2,1)S(1)} %pad_maximum_fusion.refs_5_), channel_id=1, source_target_pairs={{0,128},{128,256},{256,384},{384,0},{1,129},{129,257},{257,385},{3... | collective-permute-start | bytes 786440 | tf_op jit(solution)/shard_map/ppermute | solution.py:296
  62.5 16.5 %collective-permute-start.5 = (bf16[2,32,2048]{2,1,0:T(8,128)(2,1)S(1)}, bf16[2,32,2048]{2,1,0:T(8,128)(2,1)}, u32[]{:S(2)}, u32[]{:S(2)}) collective-permute-start(bf16[2,32,2048]{2,1,0:T(8,128)(2,1)S(1)} %pad_maximum_fusion.refs_5_), channel_id=1, source_target_pairs={{0,256},{128,384},{256,0},{384,128},{1,257},{129,385},{257,1},{385... | collective-permute-start | bytes 786440 | tf_op jit(solution)/shard_map/ppermute | solution.py:296
  67.6 13.3 %collective-permute-start.7 = (bf16[2,32,2048]{2,1,0:T(8,128)(2,1)S(1)}, bf16[2,32,2048]{2,1,0:T(8,128)(2,1)S(1)}, u32[]{:S(2)}, u32[]{:S(2)}) collective-permute-start(bf16[2,32,2048]{2,1,0:T(8,128)(2,1)S(1)} %pad_maximum_fusion.refs_5_), channel_id=1, source_target_pairs={{0,32},{32,0},{1,33},{33,1},{2,34},{34,2},{3,35},{35,3},{4,36},{36... | collective-permute-start | bytes 786440 | tf_op jit(solution)/shard_map/ppermute | solution.py:288
  79.0 13.2 %collective-permute-start.10 = (bf16[2,32,2048]{2,1,0:T(8,128)(2,1)}, bf16[2,32,2048]{2,1,0:T(8,128)(2,1)}, u32[]{:S(2)}, u32[]{:S(2)}) collective-permute-start(bf16[2,32,2048]{2,1,0:T(8,128)(2,1)} %collective-permute-done.6.refs_8_), channel_id=1, source_target_pairs={{0,32},{32,0},{1,33},{33,1},{2,34},{34,2},{3,35},{35,3},{4,36},{36... | collective-permute-start | bytes 786440 | tf_op jit(solution)/shard_map/ppermute | solution.py:288
  80.9 2.4 copy-start.6
  81.0 11.3 %collective-permute-start.8 = (bf16[2,32,2048]{2,1,0:T(8,128)(2,1)}, bf16[2,32,2048]{2,1,0:T(8,128)(2,1)}, u32[]{:S(2)}, u32[]{:S(2)}) collective-permute-start(bf16[2,32,2048]{2,1,0:T(8,128)(2,1)} %collective-permute-done.4.refs_6_), channel_id=1, source_target_pairs={{0,32},{32,0},{1,33},{33,1},{2,34},{34,2},{3,35},{35,3},{4,36},{36... | collective-permute-start | bytes 786440 | tf_op jit(solution)/shard_map/ppermute | solution.py:288
  83.4 8.9 %copy-start = (bf16[2,128,2048]{2,1,0:T(8,128)(2,1)}, bf16[2,128,2048]{2,1,0:T(8,128)(2,1)S(1)}, u32[]{:S(2)}) copy-start(bf16[2,128,2048]{2,1,0:T(8,128)(2,1)S(1)} %collective-permute-done.refs_2_.refs_3_.refs_4_) | copy-start | bytes 3145732
  83.4 8.9 %collective-permute-start.9 = (bf16[2,32,2048]{2,1,0:T(8,128)(2,1)}, bf16[2,32,2048]{2,1,0:T(8,128)(2,1)}, u32[]{:S(2)}, u32[]{:S(2)}) collective-permute-start(bf16[2,32,2048]{2,1,0:T(8,128)(2,1)} %collective-permute-done.5.refs_7_), channel_id=1, source_target_pairs={{0,32},{32,0},{1,33},{33,1},{2,34},{34,2},{3,35},{35,3},{4,36},{36... | collective-permute-start | bytes 786440 | tf_op jit(solution)/shard_map/ppermute | solution.py:288
  92.2 1.0 copy-start.1
  92.2 1.3 copy-start.2
  125.9 23.4 %all-to-all-start.4 = ((bf16[8,72,256]{2,1,0:T(8,128)(2,1)}), bf16[8,72,256]{2,1,0:T(8,128)(2,1)S(1)}, u32[]{:S(2)}, u32[]{:S(2)}) async-start(bf16[8,72,256]{2,1,0:T(8,128)(2,1)} %shard_map.80), calls=%async_computation.4 | async-start | bytes 589824 | tf_op jit(solution)/shard_map/all_to_all | solution.py:300
  149.3 0.7 copy-start.5
  151.8 23.3 %all-to-all-start.5 = ((bf16[8,72,256]{2,1,0:T(8,128)(2,1)}), bf16[8,72,256]{2,1,0:T(8,128)(2,1)S(1)}, u32[]{:S(2)}, u32[]{:S(2)}) async-start(bf16[8,72,256]{2,1,0:T(8,128)(2,1)} %get-tuple-element.19), calls=%async_computation.5 | async-start | bytes 589824 | tf_op jit(solution)/shard_map/all_to_all | solution.py:300
  175.1 0.7 copy-start.4

commit v6 on v5

--- a/solution.py
+++ b/solution.py
@@ -39,13 +39,21 @@
     return pl.BlockSpec(memory_space=pltpu.SMEM)
 
 
-def pack_kernel(idx, x_ref, *outs):
+def start_kernel(base, a_ref, out):
+    for z in range(NZ):
+        out[z, :32] = base[...].astype(bf16)
+        out[z, 32:] = a_ref[...].astype(bf16)
+
+
+def pack_kernel(idx, x_ref, own, to_y, to_z0, to_z1, to_both0, to_both1):
     yl, zl = idx[3], idx[5]
     n = 256
-    for k, out in enumerate(outs):
+    for k, outs in enumerate(((own,), (to_y,), (to_z0, to_z1), (to_both0, to_both1))):
         start = lax.rem(yl + k % 2, 2) * (2 * NZ * n) + lax.rem(zl + k // 2, 2) * n
-        for z in range(NZ):
-            out[0, :, z * n : (z + 1) * n] = x_ref[0, :, pl.ds(pl.multiple_of(start + z * 2 * n, n), n)]
+        for step in range(2):
+            out = outs[0].at[step] if len(outs) == 1 else outs[step].at[0]
+            for z in range(NZ):
+                out[:, z * n : (z + 1) * n] = x_ref[step, :, pl.ds(pl.multiple_of(start + z * 2 * n, n), n)]
 
 
 def wide(value):
@@ -61,29 +69,25 @@
     return 2 * lax.rem(idx[3] + k % 2, 2) + lax.rem(idx[5] + k // 2, 2)
 
 
-def partial_low(whole, tokens):
-    return dot(jnp.concatenate([whole[z, :64] for z in range(NZ)], axis=1), tokens, 1, 1)
-
-
 def keys_kernel(step, scale, idx, *rest):
-    x_refs, pieces, y_ref, out, bs = rest[:4], rest[4:12], rest[12], rest[-2], rest[-1]
+    x_refs, pieces, y_ref, out, bs = rest[:4], rest[4:6], rest[6], rest[-2], rest[-1]
     rows, quarter = x_refs[0].shape[1:]
-    px, pyh, pc = idx[0], idx[1], idx[2]
     places = [group_at(idx, k) for k in range(4)]
     tokens = jnp.concatenate([ref[0] for ref in x_refs], axis=0)
     if step == 0:
-        low = partial_low(rest[13], tokens) * scale
+        whole = rest[7]
+        a_half = jnp.concatenate([whole[z, 32:] for z in range(NZ)], axis=1)
+        low = dot(a_half, tokens, 1, 1) * scale
         for k in range(4):
             hi, lo = split(low[:, k * rows : (k + 1) * rows])
             out[places[k], rows : rows + 16] = wide(hi)
             out[places[k], rows + 16 :] = wide(lo)
-    for dx in range(4):
+    for x in range(4):
         for dc in range(2):
-            for dy in range(2):
-                w = lax.rem(pyh + dy, 2) * 2 + lax.rem(pc + dc, 2)
-                bs[dx, w] = pieces[4 * dc + dx][dy]
-        at = pl.ds(pl.multiple_of(lax.rem(px + 4 - dx, 4) * 128, 128), 128)
-        part = dot(tokens, bs[dx].reshape(128, quarter), 1, 1) * scale
+            for y in range(2):
+                bs[x, 2 * y + lax.rem(idx[2] + dc, 2)] = pieces[dc][2 * x + y]
+        at = slice(x * 128, x * 128 + 128)
+        part = dot(tokens, bs[x].reshape(128, quarter), 1, 1) * scale
         for k in range(4):
             value = part[k * rows : (k + 1) * rows]
             if k == 0:
@@ -94,7 +98,8 @@
 def low_kernel(scale, idx, keys, whole, *rest):
     x_refs, out, held, sem = rest[:4], rest[4], rest[5], rest[6]
     rows = x_refs[0].shape[1]
-    low = partial_low(whole, jnp.concatenate([ref[0] for ref in x_refs], axis=0)) * scale
+    a_half = jnp.concatenate([whole[z, :64] for z in range(NZ)], axis=1)
+    low = dot(a_half, jnp.concatenate([ref[0] for ref in x_refs], axis=0), 1, 1) * scale
     quarter = jnp.concatenate([whole[z, 64:] for z in range(NZ)], axis=0)
     for k in range(4):
         at = group_at(idx, k)
@@ -209,22 +214,23 @@
 
 def pack(idx, tokens):
     steps, rows, width = tokens.shape
-    quarter = width // 4
+    both = shaped((steps, rows, width // 4), bf16)
+    single = shaped((1, rows, width // 4), bf16)
     return pl.pallas_call(
         pack_kernel,
-        out_shape=[shaped((steps, rows, quarter), bf16)] * 4,
-        grid_spec=pltpu.PrefetchScalarGridSpec(
-            num_scalar_prefetch=1,
-            grid=(steps,),
-            in_specs=[pl.BlockSpec((1, rows, width), lambda i, s: (i, 0, 0))],
-            out_specs=[pl.BlockSpec((1, rows, quarter), lambda i, s: (i, 0, 0))] * 4,
-        ),
+        out_shape=[both, both] + [single] * 4,
+        in_specs=[smem()] + vmem(1),
         compiler_params=VMEM,
     )(idx, tokens)
 
 
+def token_specs(step, xs):
+    return [
+        pl.BlockSpec((1, *x.shape[1:]), lambda i, s, at=step if x.shape[0] > 1 else 0: (at, 0, 0)) for x in xs
+    ]
+
+
 def with_tokens(kernel, step, shape, idx, args, xs):
-    _, rows, quarter = xs[0].shape
     return pl.pallas_call(
         kernel,
         out_shape=shape,
@@ -232,7 +238,7 @@
             num_scalar_prefetch=1,
             grid=(1,),
             in_specs=[pl.BlockSpec(a.shape, lambda i, s, n=a.ndim: (0,) * n) for a in args]
-            + [pl.BlockSpec((1, rows, quarter), lambda i, s: (step, 0, 0))] * 4,
+            + token_specs(step, xs),
             out_specs=pl.BlockSpec(shape.shape, lambda i, s, n=len(shape.shape): (0,) * n),
         ),
         compiler_params=VMEM,
@@ -251,7 +257,7 @@
         grid_spec=pltpu.PrefetchScalarGridSpec(
             num_scalar_prefetch=1,
             grid=(1,),
-            in_specs=[pl.BlockSpec((1, rows, quarter), lambda i, s: (step, 0, 0))] * 4
+            in_specs=token_specs(step, xs)
             + [pl.BlockSpec(a.shape, lambda i, s: (0, 0, 0)) for a in pieces]
             + [pl.BlockSpec((1, rows, 512), lambda i, s: (step, 0, 0))]
             + [pl.BlockSpec(a.shape, lambda i, s: (0, 0, 0)) for a in more],
@@ -263,8 +269,6 @@
 
 
 def low_of(scale, idx, keys, whole, xs):
-    _, rows, quarter = xs[0].shape
-
     def body(*refs):
         low_kernel(scale, *refs)
 
@@ -275,7 +279,7 @@
             num_scalar_prefetch=1,
             grid=(1,),
             in_specs=[pl.BlockSpec(memory_space=pl.ANY), pl.BlockSpec(whole.shape, lambda i, s: (0, 0, 0))]
-            + [pl.BlockSpec((1, rows, quarter), lambda i, s: (1, 0, 0))] * 4,
+            + token_specs(1, xs),
             out_specs=pl.BlockSpec(memory_space=pl.ANY),
             scratch_shapes=[pltpu.VMEM((4, 64, 512), bf16), pltpu.SemaphoreType.DMA],
         ),
@@ -292,16 +296,8 @@
     return lax.ppermute(value, Q, [(k, 3 - k) for k in range(4)])
 
 
-def shift(value, axis, by, count):
-    return lax.ppermute(value, axis, [(i, (i + by) % count) for i in range(count)])
-
-
 def exchange(parts, axis):
     return lax.all_to_all(parts, axis, 0, 0, tiled=True)
-
-
-def gather_z(value):
-    return exchange(jnp.broadcast_to(value, (NZ, *value.shape)), "zh")
 
 
 def whole_step(inputs, targets, base, adapter_a, adapter_b):
@@ -316,14 +312,13 @@
     z = lax.axis_index("zh")
     block = lax.dynamic_slice(up_start, (16 * group + 8 * (z // 4), 128 * (z % 4)), (8, 128))
 
-    own, to_y, to_z, to_both = pack(idx, tokens)
-    xs = (own, swap(to_y, "yl"), swap(to_z, "zl"), swap_both(to_both))
-    cols = gather_z(base.T.astype(bf16))
-    cols = cols.transpose(1, 0, 2).reshape(cols.shape[1], width // 4)
-    pair = jnp.stack([cols, swap(cols, "yh")])
-    near = [pair] + [shift(pair, "x", d, 4) for d in (1, 2, 3)]
-    whole = gather_z(a_start.astype(bf16))
-    pieces = near + [swap(piece, "c") for piece in near]
+    own, to_y, *rest = pack(idx, tokens)
+    by_y = swap(to_y, "yl")
+    xs = [(own, by_y, swap(rest[j], "zl"), swap_both(rest[2 + j])) for j in range(2)]
+    whole = exchange(call(start_kernel, shaped((NZ, 96, 256), bf16), base.T, a_start), "zh")
+    cols = whole[:, :32].transpose(1, 0, 2).reshape(32, width // 4)
+    near = exchange(jnp.broadcast_to(cols, (8, *cols.shape)), ("x", "yh"))
+    pieces = (near, swap(near, "c"))
 
     error_shape = shaped((4, 48, 512), bf16)
 
@@ -334,14 +329,14 @@
             down_kernel(step == 1, *refs)
 
         shape = shaped((NZ, 96 if step else 72, 256), bf16)
-        return exchange(with_tokens(body, step, shape, idx, (shared,), xs), "zh")
-
-    keys = keys_of(0, scale, idx, shaped((4, rows + 32, 512), bf16), xs, targets[0], pieces, whole)
+        return exchange(with_tokens(body, step, shape, idx, (shared,), xs[step]), "zh")
+
+    keys = keys_of(0, scale, idx, shaped((4, rows + 32, 512), bf16), xs[0], targets[0], pieces, whole)
     parts = exchange(keys, Q)
     mine = call(lambda *refs: first_error_kernel(total_rows, *refs), error_shape, parts, up_start)
     parts = gradients(0, mine)
 
-    keys = keys_of(1, scale, idx, shaped((4, rows + 64, 512), bf16), xs, targets[0], pieces)
+    keys = keys_of(1, scale, idx, shaped((4, rows + 64, 512), bf16), xs[1], targets[0], pieces)
     a_next, copies = call(
         lambda *refs: update_kernel(scale, *refs),
         (shaped((64, 256), f32), shaped((NZ, 72, 256), bf16)),
@@ -350,7 +345,7 @@
         block,
     )
     whole = exchange(copies, "zh")
-    low = exchange(low_of(scale, idx, keys, whole, xs), Q)
+    low = exchange(low_of(scale, idx, keys, whole, xs[1]), Q)
     mine, up_next = call(
         lambda *refs: second_error_kernel(total_rows, *refs), (error_shape, shaped((64, 512), f32)), low
     )

time: 274 us -> 313 us (1.14)
  blocking collectives: 100 us -> 149 us
  starting transfers between devices: 82.6 us -> 41.3 us
  waiting for transfers between devices: 39.1 us -> 70.4 us
    all_to_all x7 -> x8, blocking collectives: 100 us -> 149 us  [exchange(): return lax.all_to_all(parts, axis, 0, 0, tiled=True)]
    ppermute x7 -> x4, waiting for transfers between devices: 4.72 us -> 29.2 us  [swap(): return lax.ppermute(value, axis, [(0, 1), (1, 0)])]
    ppermute x1 -> x2, waiting for transfers between devices: 0.01 us -> 22.3 us  [swap_both(): return lax.ppermute(value, Q, [(k, 3 - k) for k in range(4)])]
    all_to_all x4 -> x3, starting transfers between devices: 41 us -> 20.3 us  [exchange(): return lax.all_to_all(parts, axis, 0, 0, tiled=True)]
    ppermute x7 -> x4, starting transfers between devices: 28.3 us -> 14.4 us  [swap(): return lax.ppermute(value, axis, [(0, 1), (1, 0)])]
    all_to_all x4 -> x3, waiting for transfers between devices: 32.3 us -> 18.9 us  [exchange(): return lax.all_to_all(parts, axis, 0, 0, tiled=True)]
    ppermute x3 -> x0, starting transfers between devices: 10.8 us -> none  [shift(): lax.ppermute(value, axis, [(i, (i + by) % count) for i in range(count)])]
    ppermute x1 -> x2, starting transfers between devices: 2.52 us -> 6.61 us  [swap_both(): return lax.ppermute(value, Q, [(k, 3 - k) for k in range(4)])]
  transfers between devices with their start and end apart: 15 -> 9, of which waited for: 6 -> 6; matrix products, arithmetic and copies ran while one was open for 2% -> 1% of each run, Pallas kernels for 4% -> 3%
where the time goes in v6:
time: 313 us; the launch traced here: 311 us
  blocking collectives  149 us (48%)
  waiting for transfers between devices  70.4 us (22%)
  Pallas kernels  42.9 us (14%)
  starting transfers between devices  41.3 us (13%)
  local copies, waits for them, and re-layouts  7.04 us (2%)
    all_to_all x8, blocking collectives, exchange(): return lax.all_to_all(parts, axis, 0, 0, tiled=True)  149 us
    ppermute x4, waiting for transfers between devices, swap(): return lax.ppermute(value, axis, [(0, 1), (1, 0)])  29.2 us
    ppermute x2, waiting for transfers between devices, swap_both(): return lax.ppermute(value, Q, [(k, 3 - k) for k in range(4)])  22.3 us
    all_to_all x3, starting transfers between devices, exchange(): return lax.all_to_all(parts, axis, 0, 0, tiled=True)  20.3 us
    all_to_all x3, waiting for transfers between devices, exchange(): return lax.all_to_all(parts, axis, 0, 0, tiled=True)  18.9 us
    ppermute x4, starting transfers between devices, swap(): return lax.ppermute(value, axis, [(0, 1), (1, 0)])  14.4 us
    pallas_call x2, Pallas kernels, keys_of(): pl.pallas_call(body, out_shape=shape, grid_spec=pltpu.PrefetchScalarGridS...  12.9 us
    pallas_call x6, Pallas kernels, call(): pl.pallas_call(kernel, out_shape=shapes, in_specs=vmem(len(args)), compil...  12.8 us
  transfers between devices with their start and end apart: 9, of which 6 were waited for; matrix products, arithmetic and copies ran while one was open for 1% of the time, Pallas kernels for 3%

profile of v6, /device:TPU:1, one launch (start us, length us, event | category | flops | bytes accessed | tf_op | source)
XLA Modules:
  0.0 311.3 jit_solution(7391883748315247301)
XLA Ops:
  0.6 1.6 shard_map.77
  2.3 38.4 %all_to_all.55.refs_8_ = bf16[8,96,256]{2,1,0:T(8,128)(2,1)S(1)} all-to-all(bf16[8,96,256]{2,1,0:T(8,128)(2,1)} %shard_map.77), channel_id=1, replica_groups=mesh['x'=4,'yh'=2,'c'=2,'yl'=2,'zh'=8,'zl'=2] {'zh'}, dimensions={0} | all-to-all | bytes 786432 | tf_op jit(solution)/shard_map/all_to_all | solution.py:300
  40.7 0.0 copy-start.5
  40.8 1.1 broadcast_in_dim.9
  41.8 6.7 %all-to-all-start.1 = ((bf16[8,32,2048]{2,1,0:T(8,128)(2,1)}), bf16[8,32,2048]{2,1,0:T(8,128)(2,1)S(1)}, u32[]{:S(2)}, u32[]{:S(2)}) async-start(bf16[8,32,2048]{2,1,0:T(8,128)(2,1)} %broadcast_in_dim.9), calls=%async_computation.1 | async-start | bytes 2097152 | tf_op jit(solution)/shard_map/all_to_all | solution.py:300
  48.5 0.7 stack.27.idx.refs_0_
  49.2 4.7 %shard_map.76 = (bf16[2,128,2048]{2,1,0:T(8,128)(2,1)}, bf16[2,128,2048]{2,1,0:T(8,128)(2,1)}, bf16[1,128,2048]{2,1,0:T(8,128)(2,1)}, bf16[1,128,2048]{2,1,0:T(8...) custom-call(s32[6]{0:T(128)} %stack.27.idx.refs_0_, bf16[2,128,8192]{2,1,0:T(8,128)(2,1)} %bitcast.27), custom_call_target="tpu_custom_call" | custom-call | tf_op jit(solution)/shard_map/pallas_call | solution.py:219
  53.9 2.3 collective-permute-start
  56.2 3.7 %all-to-all-done.1.refs_5_ = bf16[8,32,2048]{2,1,0:T(8,128)(2,1)S(1)} async-done(((bf16[8,32,2048]{2,1,0:T(8,128)(2,1)}), bf16[8,32,2048]{2,1,0:T(8,128)(2,1)S(1)}, u32[]{:S(2)}, u32[]{:S(2)}) %all-to-all-start.1) | async-done | bytes 1048608 | tf_op jit(solution)/shard_map/all_to_all | solution.py:300
  59.9 0.0 copy-start.1
  59.9 8.2 %collective-permute-start.3 = (bf16[8,32,2048]{2,1,0:T(8,128)(2,1)S(1)}, bf16[8,32,2048]{2,1,0:T(8,128)(2,1)S(1)}, u32[]{:S(2)}, u32[]{:S(2)}) collective-permute-start(bf16[8,32,2048]{2,1,0:T(8,128)(2,1)S(1)} %all-to-all-done.1.refs_5_), channel_id=1, source_target_pairs={{0,32},{32,0},{1,33},{33,1},{2,34},{34,2},{3,35},{35,3},{4,36},{36... | collective-permute-start | bytes 3145736 | tf_op jit(solution)/shard_map/ppermute | solution.py:292
  68.1 2.1 collective-permute-start.4
  70.1 3.3 %collective-permute-start.5 = (bf16[1,128,2048]{2,1,0:T(8,128)(2,1)}, bf16[1,128,2048]{2,1,0:T(8,128)(2,1)S(1)}, u32[]{:S(2)}, u32[]{:S(2)}) collective-permute-start(bf16[1,128,2048]{2,1,0:T(8,128)(2,1)} %get-tuple-element.22), channel_id=1, source_target_pairs={{0,17},{1,16},{16,1},{17,0},{2,19},{3,18},{18,3},{19,2},{4,21},{5,... | collective-permute-start | bytes 1572872 | tf_op jit(solution)/shard_map/ppermute | solution.py:296
  73.5 10.2 %collective-permute-done.4.refs_3_.refs_4_ = bf16[1,128,2048]{2,1,0:T(8,128)(2,1)S(1)} collective-permute-done((bf16[1,128,2048]{2,1,0:T(8,128)(2,1)}, bf16[1,128,2048]{2,1,0:T(8,128)(2,1)S(1)}, u32[]{:S(2)}, u32[]{:S(2)}) %collective-permute-start.4) | collective-permute-done | bytes 524320 | tf_op jit(solution)/shard_map/ppermute | solution.py:292
  83.7 0.0 copy-start.6
  83.7 11.4 %collective-permute-done.5.refs_4_.refs_5_ = bf16[1,128,2048]{2,1,0:T(8,128)(2,1)S(1)} collective-permute-done((bf16[1,128,2048]{2,1,0:T(8,128)(2,1)}, bf16[1,128,2048]{2,1,0:T(8,128)(2,1)S(1)}, u32[]{:S(2)}, u32[]{:S(2)}) %collective-permute-start.5) | collective-permute-done | bytes 524320 | tf_op jit(solution)/shard_map/ppermute | solution.py:296
  95.0 0.0 collective-permute-done.refs_2_.refs_3_.refs_4_
  95.1 0.0 copy-start
  95.1 0.0 collective-permute-done.3.refs_6_
  95.1 0.8 copy-done.7
  95.8 0.0 copy-start.4
  95.8 0.0 copy-done.5
  95.8 0.0 copy-done.1
  95.8 0.0 copy-done.6
  95.9 0.4 copy-done
  96.2 0.6 copy-done.4
  96.8 6.8 %shard_map.79 = bf16[4,160,512]{2,1,0:T(8,128)(2,1)} custom-call(s32[6]{0:T(128)} %stack.27.idx.refs_0_, bf16[2,128,2048]{2,1,0:T(8,128)(2,1)} %get-tuple-element.17.refs_1_.refs_2_.refs_3_, bf16[2,128,2048]{2,1,0:T(8,128)(2,1)} %copy-done, bf16[1,128,2048]{2,1,0:T(8,128)(2,1)} %copy-done.6, bf16[1,128,2048]{2,1,0:T(8,128)(2,1)} %copy-done.7, ...), custom_call_target="tpu_custom_call" | custom-call | tf_op jit(solution)/shard_map/pallas_call | solution.py:254
  103.7 0.0 copy-start.11
  103.7 0.0 copy-start.10
  103.7 13.1 %all_to_all.56.refs_0_ = bf16[4,160,512]{2,1,0:T(8,128)(2,1)} all-to-all(bf16[4,160,512]{2,1,0:T(8,128)(2,1)} %shard_map.79), channel_id=1, replica_groups=mesh['x'=4,'yh'=2,'c'=2,'yl'=2,'zh'=8,'zl'=2] {'yl','zl'}, dimensions={0} | all-to-all | bytes 1310720 | tf_op jit(solution)/shard_map/all_to_all | solution.py:300
  116.7 2.7 shard_map.80
  119.4 8.5 %all_to_all.57.refs_1_ = bf16[4,48,512]{2,1,0:T(8,128)(2,1)} all-to-all(bf16[4,48,512]{2,1,0:T(8,128)(2,1)} %shard_map.80), channel_id=1, replica_groups=mesh['x'=4,'yh'=2,'c'=2,'yl'=2,'zh'=8,'zl'=2] {'yl','zl'}, dimensions={0} | all-to-all | bytes 393216 | tf_op jit(solution)/shard_map/all_to_all | solution.py:300
  127.9 3.4 %shard_map.81 = bf16[8,72,256]{2,1,0:T(8,128)(2,1)} custom-call(s32[6]{0:T(128)} %stack.27.idx.refs_0_, bf16[4,48,512]{2,1,0:T(8,128)(2,1)} %all_to_all.57.refs_1_, bf16[2,128,2048]{2,1,0:T(8,128)(2,1)} %get-tuple-element.17.refs_1_.refs_2_.refs_3_, bf16[2,128,2048]{2,1,0:T(8,128)(2,1)} %copy-done, bf16[1,128,2048]{2,1,0:T(8,128)(2,1)} %copy-done.6, ...), custom_call_target="tpu_custom_call" | custom-call | tf_op jit(solution)/shard_map/pallas_call | solution.py:234
  131.3 6.1 %all-to-all-start.4 = ((bf16[8,72,256]{2,1,0:T(8,128)(2,1)}), bf16[8,72,256]{2,1,0:T(8,128)(2,1)S(1)}, u32[]{:S(2)}, u32[]{:S(2)}) async-start(bf16[8,72,256]{2,1,0:T(8,128)(2,1)} %shard_map.81), calls=%async_computation.4 | async-start | bytes 589824 | tf_op jit(solution)/shard_map/all_to_all | solution.py:300
  137.4 1.3 dynamic-slice_bitcast_fusion.refs_2_
  138.7 15.2 %all-to-all-done.4.refs_0_ = bf16[8,72,256]{2,1,0:T(8,128)(2,1)S(1)} async-done(((bf16[8,72,256]{2,1,0:T(8,128)(2,1)}), bf16[8,72,256]{2,1,0:T(8,128)(2,1)S(1)}, u32[]{:S(2)}, u32[]{:S(2)}) %all-to-all-start.4) | async-done | bytes 294944 | tf_op jit(solution)/shard_map/all_to_all | solution.py:300
  153.9 0.7 copy-done.8
  154.7 1.8 shard_map.82
  156.5 7.5 %all-to-all-start.5 = ((bf16[8,72,256]{2,1,0:T(8,128)(2,1)}), bf16[8,72,256]{2,1,0:T(8,128)(2,1)S(1)}, u32[]{:S(2)}, u32[]{:S(2)}) async-start(bf16[8,72,256]{2,1,0:T(8,128)(2,1)} %get-tuple-element.23), calls=%async_computation.5 | async-start | bytes 589824 | tf_op jit(solution)/shard_map/all_to_all | solution.py:300
  164.0 0.0 copy-done.11
  164.0 1.9 collective-permute-start.1
  165.9 0.0 copy-done.10
  165.9 3.3 %collective-permute-start.2 = (bf16[1,128,2048]{2,1,0:T(8,128)(2,1)S(1)}, bf16[1,128,2048]{2,1,0:T(8,128)(2,1)S(1)}, u32[]{:S(2)}, u32[]{:S(2)}) collective-permute-start(bf16[1,128,2048]{2,1,0:T(8,128)(2,1)S(1)} %copy-done.10), channel_id=1, source_target_pairs={{0,17},{1,16},{16,1},{17,0},{2,19},{3,18},{18,3},{19,2},{4,21},{5,... | collective-permute-start | bytes 1572872 | tf_op jit(solution)/shard_map/ppermute | solution.py:296
  169.2 19.1 %collective-permute-done.1.refs_3_.refs_5_.refs_4_ = bf16[1,128,2048]{2,1,0:T(8,128)(2,1)S(1)} collective-permute-done((bf16[1,128,2048]{2,1,0:T(8,128)(2,1)S(1)}, bf16[1,128,2048]{2,1,0:T(8,128)(2,1)S(1)}, u32[]{:S(2)}, u32[]{:S(2)}) %collective-permute-start.1) | collective-permute-done | bytes 524320 | tf_op jit(solution)/shard_map/ppermute | solution.py:292
  188.2 0.0 copy-start.2
  188.2 10.9 %collective-permute-done.2.refs_4_.refs_6_.refs_5_ = bf16[1,128,2048]{2,1,0:T(8,128)(2,1)S(1)} collective-permute-done((bf16[1,128,2048]{2,1,0:T(8,128)(2,1)S(1)}, bf16[1,128,2048]{2,1,0:T(8,128)(2,1)S(1)}, u32[]{:S(2)}, u32[]{:S(2)}) %collective-permute-start.2) | collective-permute-done | bytes 524320 | tf_op jit(solution)/shard_map/ppermute | solution.py:296
  199.1 0.0 copy-done.2
  199.1 0.0 copy-start.3
  199.1 0.8 copy-done.3
  199.9 6.1 %shard_map.78.refs_1_ = bf16[4,192,512]{2,1,0:T(8,128)(2,1)} custom-call(s32[6]{0:T(128)} %stack.27.idx.refs_0_, bf16[2,128,2048]{2,1,0:T(8,128)(2,1)} %get-tuple-element.17.refs_1_.refs_2_.refs_3_, bf16[2,128,2048]{2,1,0:T(8,128)(2,1)} %copy-done, bf16[1,128,2048]{2,1,0:T(8,128)(2,1)} %copy-done.2, bf16[1,128,2048]{2,1,0:T(8,128)(2,1)} %copy-done.3, ...), custom_call_target="tpu_custom_call" | custom-call | tf_op jit(solution)/shard_map/pallas_call | solution.py:254
  206.0 0.0 all-to-all-done.5.refs_2_
  206.0 0.0 copy-start.9
  206.0 0.7 copy-done.9
  206.7 3.7 %shard_map.83 = bf16[4,192,512]{2,1,0:T(8,128)(2,1)} custom-call(s32[6]{0:T(128)} %stack.27.idx.refs_0_, bf16[4,192,512]{2,1,0:T(8,128)(2,1)} %shard_map.78.refs_1_, bf16[8,72,256]{2,1,0:T(8,128)(2,1)} %copy-done.9, bf16[2,128,2048]{2,1,0:T(8,128)(2,1)} %get-tuple-element.17.refs_1_.refs_2_.refs_3_, ...), custom_call_target="tpu_custom_call", output_to_operand_aliasing={{}: (1, {})} | custom-call | tf_op jit(solution)/shard_map/pallas_call | solution.py:275
  210.5 13.1 %all_to_all.58.refs_0_ = bf16[4,192,512]{2,1,0:T(8,128)(2,1)} all-to-all(bf16[4,192,512]{2,1,0:T(8,128)(2,1)} %shard_map.83), channel_id=1, replica_groups=mesh['x'=4,'yh'=2,'c'=2,'yl'=2,'zh'=8,'zl'=2] {'yl','zl'}, dimensions={0} | all-to-all | bytes 1572864 | tf_op jit(solution)/shard_map/all_to_all | solution.py:300
  223.6 2.7 shard_map.84
  226.3 8.5 %all_to_all.59.refs_1_ = bf16[4,48,512]{2,1,0:T(8,128)(2,1)} all-to-all(bf16[4,48,512]{2,1,0:T(8,128)(2,1)} %get-tuple-element.24), channel_id=1, replica_groups=mesh['x'=4,'yh'=2,'c'=2,'yl'=2,'zh'=8,'zl'=2] {'yl','zl'}, dimensions={0} | all-to-all | bytes 393216 | tf_op jit(solution)/shard_map/all_to_all | solution.py:300
  234.8 3.5 %shard_map.85 = bf16[8,96,256]{2,1,0:T(8,128)(2,1)} custom-call(s32[6]{0:T(128)} %stack.27.idx.refs_0_, bf16[4,48,512]{2,1,0:T(8,128)(2,1)} %all_to_all.59.refs_1_, bf16[2,128,2048]{2,1,0:T(8,128)(2,1)} %get-tuple-element.17.refs_1_.refs_2_.refs_3_, bf16[2,128,2048]{2,1,0:T(8,128)(2,1)} %copy-done, bf16[1,128,2048]{2,1,0:T(8,128)(2,1)} %copy-done.2, ...), custom_call_target="tpu_custom_call" | custom-call | tf_op jit(solution)/shard_map/pallas_call | solution.py:234
  238.2 33.1 %all_to_all.60.refs_1_ = bf16[8,96,256]{2,1,0:T(8,128)(2,1)} all-to-all(bf16[8,96,256]{2,1,0:T(8,128)(2,1)} %shard_map.85), channel_id=1, replica_groups=mesh['x'=4,'yh'=2,'c'=2,'yl'=2,'zh'=8,'zl'=2] {'zh'}, dimensions={0} | all-to-all | bytes 786432 | tf_op jit(solution)/shard_map/all_to_all | solution.py:300
  271.4 1.8 shard_map.86
  273.2 7.9 %all_to_all.61.quarters = f32[4,16,512]{2,1,0:T(8,128)} all-to-all(f32[4,16,512]{2,1,0:T(8,128)} %get-tuple-element.28), channel_id=1, replica_groups=mesh['x'=4,'yh'=2,'c'=2,'yl'=2,'zh'=8,'zl'=2] {'yl','zl'}, dimensions={0} | all-to-all | bytes 262144 | tf_op jit(solution)/shard_map/all_to_all | solution.py:300
  281.1 2.4 shard_map.87
  283.4 26.3 %all_to_all.62.parts = bf16[16,32,256]{2,1,0:T(8,128)(2,1)} all-to-all(bf16[16,32,256]{2,1,0:T(8,128)(2,1)} %bitcast.36), channel_id=1, replica_groups=mesh['x'=4,'yh'=2,'c'=2,'yl'=2,'zh'=8,'zl'=2] {'x','yh','c'}, dimensions={0} | all-to-all | bytes 524288 | tf_op jit(solution)/shard_map/all_to_all | solution.py:300
  309.7 1.6 shard_map.88
  (4 shorter events, 0.0 us)
Async XLA Ops:
  40.7 55.1 %copy-start.5 = (bf16[8,96,256]{2,1,0:T(8,128)(2,1)}, bf16[8,96,256]{2,1,0:T(8,128)(2,1)S(1)}, u32[]{:S(2)}) copy-start(bf16[8,96,256]{2,1,0:T(8,128)(2,1)S(1)} %all_to_all.55.refs_8_) | copy-start | bytes 1179652
  41.8 18.1 %all-to-all-start.1 = ((bf16[8,32,2048]{2,1,0:T(8,128)(2,1)}), bf16[8,32,2048]{2,1,0:T(8,128)(2,1)S(1)}, u32[]{:S(2)}, u32[]{:S(2)}) async-start(bf16[8,32,2048]{2,1,0:T(8,128)(2,1)} %broadcast_in_dim.9), calls=%async_computation.1 | async-start | bytes 2097152 | tf_op jit(solution)/shard_map/all_to_all | solution.py:300
  53.9 41.2 %collective-permute-start = (bf16[2,128,2048]{2,1,0:T(8,128)(2,1)}, bf16[2,128,2048]{2,1,0:T(8,128)(2,1)S(1)}, u32[]{:S(2)}, u32[]{:S(2)}) collective-permute-start(bf16[2,128,2048]{2,1,0:T(8,128)(2,1)} %get-tuple-element.18), channel_id=1, source_target_pairs={{0,16},{16,0},{1,17},{17,1},{2,18},{18,2},{3,19},{19,3},{4,20},{20... | collective-permute-start | bytes 3145736 | tf_op jit(solution)/shard_map/ppermute | solution.py:292
  59.9 35.9 %copy-start.1 = (bf16[8,32,2048]{2,1,0:T(8,128)(2,1)}, bf16[8,32,2048]{2,1,0:T(8,128)(2,1)S(1)}, u32[]{:S(2)}) copy-start(bf16[8,32,2048]{2,1,0:T(8,128)(2,1)S(1)} %all-to-all-done.1.refs_5_) | copy-start | bytes 3145732
  59.9 35.1 %collective-permute-start.3 = (bf16[8,32,2048]{2,1,0:T(8,128)(2,1)S(1)}, bf16[8,32,2048]{2,1,0:T(8,128)(2,1)S(1)}, u32[]{:S(2)}, u32[]{:S(2)}) collective-permute-start(bf16[8,32,2048]{2,1,0:T(8,128)(2,1)S(1)} %all-to-all-done.1.refs_5_), channel_id=1, source_target_pairs={{0,32},{32,0},{1,33},{33,1},{2,34},{34,2},{3,35},{35,3},{4,36},{36... | collective-permute-start | bytes 3145736 | tf_op jit(solution)/shard_map/ppermute | solution.py:292
  68.1 15.6 %collective-permute-start.4 = (bf16[1,128,2048]{2,1,0:T(8,128)(2,1)}, bf16[1,128,2048]{2,1,0:T(8,128)(2,1)S(1)}, u32[]{:S(2)}, u32[]{:S(2)}) collective-permute-start(bf16[1,128,2048]{2,1,0:T(8,128)(2,1)} %get-tuple-element.21), channel_id=1, source_target_pairs={{0,1},{1,0},{2,3},{3,2},{4,5},{5,4},{6,7},{7,6},{8,9},{9,8},{10,11... | collective-permute-start | bytes 1572872 | tf_op jit(solution)/shard_map/ppermute | solution.py:292
  70.1 24.9 %collective-permute-start.5 = (bf16[1,128,2048]{2,1,0:T(8,128)(2,1)}, bf16[1,128,2048]{2,1,0:T(8,128)(2,1)S(1)}, u32[]{:S(2)}, u32[]{:S(2)}) collective-permute-start(bf16[1,128,2048]{2,1,0:T(8,128)(2,1)} %get-tuple-element.22), channel_id=1, source_target_pairs={{0,17},{1,16},{16,1},{17,0},{2,19},{3,18},{18,3},{19,2},{4,21},{5,... | collective-permute-start | bytes 1572872 | tf_op jit(solution)/shard_map/ppermute | solution.py:296
  83.7 12.2 %copy-start.6 = (bf16[1,128,2048]{2,1,0:T(8,128)(2,1)}, bf16[1,128,2048]{2,1,0:T(8,128)(2,1)S(1)}, u32[]{:S(2)}) copy-start(bf16[1,128,2048]{2,1,0:T(8,128)(2,1)S(1)} %collective-permute-done.4.refs_3_.refs_4_) | copy-start | bytes 1572868
  95.0 0.8 copy-start.7
  95.1 1.2 copy-start
  95.8 1.0 copy-start.4
  103.7 60.3 %copy-start.11 = (bf16[1,128,2048]{2,1,0:T(8,128)(2,1)S(1)}, bf16[1,128,2048]{2,1,0:T(8,128)(2,1)}, u32[]{:S(2)}) copy-start(bf16[1,128,2048]{2,1,0:T(8,128)(2,1)} %get-tuple-element.19) | copy-start | bytes 1572868
  103.7 62.2 %copy-start.10 = (bf16[1,128,2048]{2,1,0:T(8,128)(2,1)S(1)}, bf16[1,128,2048]{2,1,0:T(8,128)(2,1)}, u32[]{:S(2)}) copy-start(bf16[1,128,2048]{2,1,0:T(8,128)(2,1)} %get-tuple-element.20) | copy-start | bytes 1572868
  131.3 22.6 %all-to-all-start.4 = ((bf16[8,72,256]{2,1,0:T(8,128)(2,1)}), bf16[8,72,256]{2,1,0:T(8,128)(2,1)S(1)}, u32[]{:S(2)}, u32[]{:S(2)}) async-start(bf16[8,72,256]{2,1,0:T(8,128)(2,1)} %shard_map.81), calls=%async_computation.4 | async-start | bytes 589824 | tf_op jit(solution)/shard_map/all_to_all | solution.py:300
  153.9 0.7 copy-start.8
  156.5 49.6 %all-to-all-start.5 = ((bf16[8,72,256]{2,1,0:T(8,128)(2,1)}), bf16[8,72,256]{2,1,0:T(8,128)(2,1)S(1)}, u32[]{:S(2)}, u32[]{:S(2)}) async-start(bf16[8,72,256]{2,1,0:T(8,128)(2,1)} %get-tuple-element.23), calls=%async_computation.5 | async-start | bytes 589824 | tf_op jit(solution)/shard_map/all_to_all | solution.py:300
  164.0 24.3 %collective-permute-start.1 = (bf16[1,128,2048]{2,1,0:T(8,128)(2,1)S(1)}, bf16[1,128,2048]{2,1,0:T(8,128)(2,1)S(1)}, u32[]{:S(2)}, u32[]{:S(2)}) collective-permute-start(bf16[1,128,2048]{2,1,0:T(8,128)(2,1)S(1)} %copy-done.11), channel_id=1, source_target_pairs={{0,1},{1,0},{2,3},{3,2},{4,5},{5,4},{6,7},{7,6},{8,9},{9,8},{10,11... | collective-permute-start | bytes 1572872 | tf_op jit(solution)/shard_map/ppermute | solution.py:292
  165.9 33.2 %collective-permute-start.2 = (bf16[1,128,2048]{2,1,0:T(8,128)(2,1)S(1)}, bf16[1,128,2048]{2,1,0:T(8,128)(2,1)S(1)}, u32[]{:S(2)}, u32[]{:S(2)}) collective-permute-start(bf16[1,128,2048]{2,1,0:T(8,128)(2,1)S(1)} %copy-done.10), channel_id=1, source_target_pairs={{0,17},{1,16},{16,1},{17,0},{2,19},{3,18},{18,3},{19,2},{4,21},{5,... | collective-permute-start | bytes 1572872 | tf_op jit(solution)/shard_map/ppermute | solution.py:296
  188.2 10.9 %copy-start.2 = (bf16[1,128,2048]{2,1,0:T(8,128)(2,1)}, bf16[1,128,2048]{2,1,0:T(8,128)(2,1)S(1)}, u32[]{:S(2)}) copy-start(bf16[1,128,2048]{2,1,0:T(8,128)(2,1)S(1)} %collective-permute-done.1.refs_3_.refs_5_.refs_4_) | copy-start | bytes 1572868
  199.1 0.8 copy-start.3
  206.0 0.7 copy-start.9

commit v7 on v6

--- a/solution.py
+++ b/solution.py
@@ -45,15 +45,13 @@
         out[z, 32:] = a_ref[...].astype(bf16)
 
 
-def pack_kernel(idx, x_ref, own, to_y, to_z0, to_z1, to_both0, to_both1):
+def pack_kernel(idx, x_ref, *outs):
     yl, zl = idx[3], idx[5]
     n = 256
-    for k, outs in enumerate(((own,), (to_y,), (to_z0, to_z1), (to_both0, to_both1))):
+    for k, out in enumerate(outs):
         start = lax.rem(yl + k % 2, 2) * (2 * NZ * n) + lax.rem(zl + k // 2, 2) * n
-        for step in range(2):
-            out = outs[0].at[step] if len(outs) == 1 else outs[step].at[0]
-            for z in range(NZ):
-                out[:, z * n : (z + 1) * n] = x_ref[step, :, pl.ds(pl.multiple_of(start + z * 2 * n, n), n)]
+        for z in range(NZ):
+            out[0, :, z * n : (z + 1) * n] = x_ref[0, :, pl.ds(pl.multiple_of(start + z * 2 * n, n), n)]
 
 
 def wide(value):
@@ -214,20 +212,22 @@
 
 def pack(idx, tokens):
     steps, rows, width = tokens.shape
-    both = shaped((steps, rows, width // 4), bf16)
-    single = shaped((1, rows, width // 4), bf16)
+    quarter = width // 4
     return pl.pallas_call(
         pack_kernel,
-        out_shape=[both, both] + [single] * 4,
-        in_specs=[smem()] + vmem(1),
+        out_shape=[shaped((steps, rows, quarter), bf16)] * 4,
+        grid_spec=pltpu.PrefetchScalarGridSpec(
+            num_scalar_prefetch=1,
+            grid=(steps,),
+            in_specs=[pl.BlockSpec((1, rows, width), lambda i, s: (i, 0, 0))],
+            out_specs=[pl.BlockSpec((1, rows, quarter), lambda i, s: (i, 0, 0))] * 4,
+        ),
         compiler_params=VMEM,
     )(idx, tokens)
 
 
 def token_specs(step, xs):
-    return [
-        pl.BlockSpec((1, *x.shape[1:]), lambda i, s, at=step if x.shape[0] > 1 else 0: (at, 0, 0)) for x in xs
-    ]
+    return [pl.BlockSpec((1, *x.shape[1:]), lambda i, s: (step, 0, 0)) for x in xs]
 
 
 def with_tokens(kernel, step, shape, idx, args, xs):
@@ -312,9 +312,8 @@
     z = lax.axis_index("zh")
     block = lax.dynamic_slice(up_start, (16 * group + 8 * (z // 4), 128 * (z % 4)), (8, 128))
 
-    own, to_y, *rest = pack(idx, tokens)
-    by_y = swap(to_y, "yl")
-    xs = [(own, by_y, swap(rest[j], "zl"), swap_both(rest[2 + j])) for j in range(2)]
+    own, to_y, to_z, to_both = pack(idx, tokens)
+    xs = (own, swap(to_y, "yl"), swap(to_z, "zl"), swap_both(to_both))
     whole = exchange(call(start_kernel, shaped((NZ, 96, 256), bf16), base.T, a_start), "zh")
     cols = whole[:, :32].transpose(1, 0, 2).reshape(32, width // 4)
     near = exchange(jnp.broadcast_to(cols, (8, *cols.shape)), ("x", "yh"))
@@ -329,14 +328,14 @@
             down_kernel(step == 1, *refs)
 
         shape = shaped((NZ, 96 if step else 72, 256), bf16)
-        return exchange(with_tokens(body, step, shape, idx, (shared,), xs[step]), "zh")
-
-    keys = keys_of(0, scale, idx, shaped((4, rows + 32, 512), bf16), xs[0], targets[0], pieces, whole)
+        return exchange(with_tokens(body, step, shape, idx, (shared,), xs), "zh")
+
+    keys = keys_of(0, scale, idx, shaped((4, rows + 32, 512), bf16), xs, targets[0], pieces, whole)
     parts = exchange(keys, Q)
     mine = call(lambda *refs: first_error_kernel(total_rows, *refs), error_shape, parts, up_start)
     parts = gradients(0, mine)
 
-    keys = keys_of(1, scale, idx, shaped((4, rows + 64, 512), bf16), xs[1], targets[0], pieces)
+    keys = keys_of(1, scale, idx, shaped((4, rows + 64, 512), bf16), xs, targets[0], pieces)
     a_next, copies = call(
         lambda *refs: update_kernel(scale, *refs),
         (shaped((64, 256), f32), shaped((NZ, 72, 256), bf16)),
@@ -345,7 +344,7 @@
         block,
     )
     whole = exchange(copies, "zh")
-    low = exchange(low_of(scale, idx, keys, whole, xs[1]), Q)
+    low = exchange(low_of(scale, idx, keys, whole, xs), Q)
     mine, up_next = call(
         lambda *refs: second_error_kernel(total_rows, *refs), (error_shape, shaped((64, 512), f32)), low
     )

time: 313 us -> 295 us (0.942)
  waiting for transfers between devices: 70.4 us -> 56.7 us
  starting transfers between devices: 41.3 us -> 34.3 us
  blocking collectives: 149 us -> 154 us
    ppermute x4 -> x3, waiting for transfers between devices: 29.2 us -> 18.6 us  [swap(): return lax.ppermute(value, axis, [(0, 1), (1, 0)])]
    ppermute x2 -> x1, waiting for transfers between devices: 22.3 us -> 12.9 us  [swap_both(): return lax.ppermute(value, Q, [(k, 3 - k) for k in range(4)])]
    all_to_all x3, waiting for transfers between devices: 18.9 us -> 25.2 us  [exchange(): return lax.all_to_all(parts, axis, 0, 0, tiled=True)]
    all_to_all x8, blocking collectives: 149 us -> 154 us  [exchange(): return lax.all_to_all(parts, axis, 0, 0, tiled=True)]
    ppermute x2 -> x1, starting transfers between devices: 6.61 us -> 4.01 us  [swap_both(): return lax.ppermute(value, Q, [(k, 3 - k) for k in range(4)])]
    ppermute x4 -> x3, starting transfers between devices: 14.4 us -> 11.8 us  [swap(): return lax.ppermute(value, axis, [(0, 1), (1, 0)])]
  transfers between devices with their start and end apart: 9 -> 7, of which waited for: 6 -> 4; matrix products, arithmetic and copies ran while one was open for 1% -> 1% of each run, Pallas kernels for 3% -> 4%
where the time goes in v7:
time: 295 us; the launch traced here: 294 us
  blocking collectives  154 us (52%)
  waiting for transfers between devices  56.7 us (19%)
  Pallas kernels  42.7 us (14%)
  starting transfers between devices  34.3 us (12%)
  local copies, waits for them, and re-layouts  5.53 us (2%)
    all_to_all x8, blocking collectives, exchange(): return lax.all_to_all(parts, axis, 0, 0, tiled=True)  154 us
    all_to_all x3, waiting for transfers between devices, exchange(): return lax.all_to_all(parts, axis, 0, 0, tiled=True)  25.2 us
    ppermute x3, waiting for transfers between devices, swap(): return lax.ppermute(value, axis, [(0, 1), (1, 0)])  18.6 us
    all_to_all x3, starting transfers between devices, exchange(): return lax.all_to_all(parts, axis, 0, 0, tiled=True)  18.5 us
    pallas_call x2, Pallas kernels, keys_of(): pl.pallas_call(body, out_shape=shape, grid_spec=pltpu.PrefetchScalarGridS...  12.9 us
    ppermute x1, waiting for transfers between devices, swap_both(): return lax.ppermute(value, Q, [(k, 3 - k) for k in range(4)])  12.9 us
    pallas_call x6, Pallas kernels, call(): pl.pallas_call(kernel, out_shape=shapes, in_specs=vmem(len(args)), compil...  12.8 us
    ppermute x3, starting transfers between devices, swap(): return lax.ppermute(value, axis, [(0, 1), (1, 0)])  11.8 us
  transfers between devices with their start and end apart: 7, of which 4 were waited for; matrix products, arithmetic and copies ran while one was open for 1% of the time, Pallas kernels for 4%

profile of v7, /device:TPU:1, one launch (start us, length us, event | category | flops | bytes accessed | tf_op | source)
XLA Modules:
  0.0 293.9 jit_solution(3258926363048573899)
XLA Ops:
  0.6 1.6 shard_map.77
  2.3 38.4 %all_to_all.55.refs_8_ = bf16[8,96,256]{2,1,0:T(8,128)(2,1)S(1)} all-to-all(bf16[8,96,256]{2,1,0:T(8,128)(2,1)} %shard_map.77), channel_id=1, replica_groups=mesh['x'=4,'yh'=2,'c'=2,'yl'=2,'zh'=8,'zl'=2] {'zh'}, dimensions={0} | all-to-all | bytes 786432 | tf_op jit(solution)/shard_map/all_to_all | solution.py:300
  40.7 0.0 copy-start.3
  40.8 1.1 broadcast_in_dim.9
  41.9 6.7 %all-to-all-start.1 = ((bf16[8,32,2048]{2,1,0:T(8,128)(2,1)}), bf16[8,32,2048]{2,1,0:T(8,128)(2,1)}, u32[]{:S(2)}, u32[]{:S(2)}) async-start(bf16[8,32,2048]{2,1,0:T(8,128)(2,1)} %broadcast_in_dim.9), calls=%async_computation.1 | async-start | bytes 2097152 | tf_op jit(solution)/shard_map/all_to_all | solution.py:300
  48.5 0.7 stack.27.idx.refs_0_
  49.2 4.5 %shard_map.76 = (bf16[2,128,2048]{2,1,0:T(8,128)(2,1)}, bf16[2,128,2048]{2,1,0:T(8,128)(2,1)}, bf16[2,128,2048]{2,1,0:T(8,128)(2,1)}, bf16[2,128,2048]{2,1,0:T(8,128)(2,1)}) custom-call(s32[6]{0:T(128)} %stack.27.idx.refs_0_, bf16[2,128,8192]{2,1,0:T(8,128)(2,1)} %bitcast.27), custom_call_target="tpu_custom_call" | custom-call | tf_op jit(solution)/shard_map/pallas_call | solution.py:216
  53.7 2.3 collective-permute-start
  56.0 2.1 collective-permute-start.1
  58.1 4.0 %collective-permute-start.2 = (bf16[2,128,2048]{2,1,0:T(8,128)(2,1)}, bf16[2,128,2048]{2,1,0:T(8,128)(2,1)S(1)}, u32[]{:S(2)}, u32[]{:S(2)}) collective-permute-start(bf16[2,128,2048]{2,1,0:T(8,128)(2,1)} %get-tuple-element.18), channel_id=1, source_target_pairs={{0,17},{1,16},{16,1},{17,0},{2,19},{3,18},{18,3},{19,2},{4,21},{5,... | collective-permute-start | bytes 3145736 | tf_op jit(solution)/shard_map/ppermute | solution.py:296
  62.1 0.0 all-to-all-done.1.refs_5_
  62.1 7.5 %collective-permute-start.3 = (bf16[8,32,2048]{2,1,0:T(8,128)(2,1)}, bf16[8,32,2048]{2,1,0:T(8,128)(2,1)}, u32[]{:S(2)}, u32[]{:S(2)}) collective-permute-start(bf16[8,32,2048]{2,1,0:T(8,128)(2,1)} %all-to-all-done.1.refs_5_), channel_id=1, source_target_pairs={{0,32},{32,0},{1,33},{33,1},{2,34},{34,2},{3,35},{35,3},{4,36},{36... | collective-permute-start | bytes 3145736 | tf_op jit(solution)/shard_map/ppermute | solution.py:292
  69.6 18.6 %collective-permute-done.refs_2_.refs_3_.refs_4_ = bf16[2,128,2048]{2,1,0:T(8,128)(2,1)S(1)} collective-permute-done((bf16[2,128,2048]{2,1,0:T(8,128)(2,1)}, bf16[2,128,2048]{2,1,0:T(8,128)(2,1)S(1)}, u32[]{:S(2)}, u32[]{:S(2)}) %collective-permute-start) | collective-permute-done | bytes 1048608 | tf_op jit(solution)/shard_map/ppermute | solution.py:292
  88.2 0.0 copy-start
  88.2 0.0 collective-permute-done.1.refs_3_.refs_4_.refs_5_
  88.2 0.0 copy-start.1
  88.2 12.9 %collective-permute-done.2.refs_4_.refs_5_.refs_6_ = bf16[2,128,2048]{2,1,0:T(8,128)(2,1)S(1)} collective-permute-done((bf16[2,128,2048]{2,1,0:T(8,128)(2,1)}, bf16[2,128,2048]{2,1,0:T(8,128)(2,1)S(1)}, u32[]{:S(2)}, u32[]{:S(2)}) %collective-permute-start.2) | collective-permute-done | bytes 1048608 | tf_op jit(solution)/shard_map/ppermute | solution.py:296
  101.1 0.0 copy-start.2
  101.1 0.0 collective-permute-done.3.refs_6_
  101.1 0.0 copy-done.3
  101.1 0.0 copy-done
  101.1 0.0 copy-done.1
  101.1 1.0 copy-done.2
  102.1 6.9 %shard_map.79 = bf16[4,160,512]{2,1,0:T(8,128)(2,1)} custom-call(s32[6]{0:T(128)} %stack.27.idx.refs_0_, bf16[2,128,2048]{2,1,0:T(8,128)(2,1)} %get-tuple-element.15.refs_1_.refs_2_.refs_3_, bf16[2,128,2048]{2,1,0:T(8,128)(2,1)} %copy-done, bf16[2,128,2048]{2,1,0:T(8,128)(2,1)} %copy-done.1, bf16[2,128,2048]{2,1,0:T(8,128)(2,1)} %copy-done.2, ...), custom_call_target="tpu_custom_call" | custom-call | tf_op jit(solution)/shard_map/pallas_call | solution.py:254
  108.9 16.6 %all_to_all.56.refs_0_ = bf16[4,160,512]{2,1,0:T(8,128)(2,1)} all-to-all(bf16[4,160,512]{2,1,0:T(8,128)(2,1)} %shard_map.79), channel_id=1, replica_groups=mesh['x'=4,'yh'=2,'c'=2,'yl'=2,'zh'=8,'zl'=2] {'yl','zl'}, dimensions={0} | all-to-all | bytes 1310720 | tf_op jit(solution)/shard_map/all_to_all | solution.py:300
  125.5 2.7 shard_map.80
  128.2 8.5 %all_to_all.57.refs_1_ = bf16[4,48,512]{2,1,0:T(8,128)(2,1)} all-to-all(bf16[4,48,512]{2,1,0:T(8,128)(2,1)} %shard_map.80), channel_id=1, replica_groups=mesh['x'=4,'yh'=2,'c'=2,'yl'=2,'zh'=8,'zl'=2] {'yl','zl'}, dimensions={0} | all-to-all | bytes 393216 | tf_op jit(solution)/shard_map/all_to_all | solution.py:300
  136.7 3.5 %shard_map.81 = bf16[8,72,256]{2,1,0:T(8,128)(2,1)} custom-call(s32[6]{0:T(128)} %stack.27.idx.refs_0_, bf16[4,48,512]{2,1,0:T(8,128)(2,1)} %all_to_all.57.refs_1_, bf16[2,128,2048]{2,1,0:T(8,128)(2,1)} %get-tuple-element.15.refs_1_.refs_2_.refs_3_, bf16[2,128,2048]{2,1,0:T(8,128)(2,1)} %copy-done, bf16[2,128,2048]{2,1,0:T(8,128)(2,1)} %copy-done.1, ...), custom_call_target="tpu_custom_call" | custom-call | tf_op jit(solution)/shard_map/pallas_call | solution.py:234
  140.1 5.9 %all-to-all-start.4 = ((bf16[8,72,256]{2,1,0:T(8,128)(2,1)}), bf16[8,72,256]{2,1,0:T(8,128)(2,1)S(1)}, u32[]{:S(2)}, u32[]{:S(2)}) async-start(bf16[8,72,256]{2,1,0:T(8,128)(2,1)} %shard_map.81), calls=%async_computation.4 | async-start | bytes 589824 | tf_op jit(solution)/shard_map/all_to_all | solution.py:300
  146.0 1.3 dynamic-slice_bitcast_fusion.refs_2_
  147.3 15.6 %all-to-all-done.4.refs_0_ = bf16[8,72,256]{2,1,0:T(8,128)(2,1)S(1)} async-done(((bf16[8,72,256]{2,1,0:T(8,128)(2,1)}), bf16[8,72,256]{2,1,0:T(8,128)(2,1)S(1)}, u32[]{:S(2)}, u32[]{:S(2)}) %all-to-all-start.4) | async-done | bytes 294944 | tf_op jit(solution)/shard_map/all_to_all | solution.py:300
  162.9 0.0 copy-start.5
  162.9 0.7 copy-done.5
  163.7 1.8 shard_map.82
  165.5 5.9 %all-to-all-start.5 = ((bf16[8,72,256]{2,1,0:T(8,128)(2,1)}), bf16[8,72,256]{2,1,0:T(8,128)(2,1)S(1)}, u32[]{:S(2)}, u32[]{:S(2)}) async-start(bf16[8,72,256]{2,1,0:T(8,128)(2,1)} %get-tuple-element.19), calls=%async_computation.5 | async-start | bytes 589824 | tf_op jit(solution)/shard_map/all_to_all | solution.py:300
  171.4 6.1 %shard_map.78.refs_1_ = bf16[4,192,512]{2,1,0:T(8,128)(2,1)} custom-call(s32[6]{0:T(128)} %stack.27.idx.refs_0_, bf16[2,128,2048]{2,1,0:T(8,128)(2,1)} %get-tuple-element.15.refs_1_.refs_2_.refs_3_, bf16[2,128,2048]{2,1,0:T(8,128)(2,1)} %copy-done, bf16[2,128,2048]{2,1,0:T(8,128)(2,1)} %copy-done.1, bf16[2,128,2048]{2,1,0:T(8,128)(2,1)} %copy-done.2, ...), custom_call_target="tpu_custom_call" | custom-call | tf_op jit(solution)/shard_map/pallas_call | solution.py:254
  177.5 9.6 %all-to-all-done.5.refs_2_ = bf16[8,72,256]{2,1,0:T(8,128)(2,1)S(1)} async-done(((bf16[8,72,256]{2,1,0:T(8,128)(2,1)}), bf16[8,72,256]{2,1,0:T(8,128)(2,1)S(1)}, u32[]{:S(2)}, u32[]{:S(2)}) %all-to-all-start.5) | async-done | bytes 294944 | tf_op jit(solution)/shard_map/all_to_all | solution.py:300
  187.1 0.0 copy-start.4
  187.1 0.7 copy-done.4
  187.8 3.8 %shard_map.83 = bf16[4,192,512]{2,1,0:T(8,128)(2,1)} custom-call(s32[6]{0:T(128)} %stack.27.idx.refs_0_, bf16[4,192,512]{2,1,0:T(8,128)(2,1)} %shard_map.78.refs_1_, bf16[8,72,256]{2,1,0:T(8,128)(2,1)} %copy-done.4, bf16[2,128,2048]{2,1,0:T(8,128)(2,1)} %get-tuple-element.15.refs_1_.refs_2_.refs_3_, ...), custom_call_target="tpu_custom_call", output_to_operand_aliasing={{}: (1, {})} | custom-call | tf_op jit(solution)/shard_map/pallas_call | solution.py:275
  191.6 13.1 %all_to_all.58.refs_0_ = bf16[4,192,512]{2,1,0:T(8,128)(2,1)} all-to-all(bf16[4,192,512]{2,1,0:T(8,128)(2,1)} %shard_map.83), channel_id=1, replica_groups=mesh['x'=4,'yh'=2,'c'=2,'yl'=2,'zh'=8,'zl'=2] {'yl','zl'}, dimensions={0} | all-to-all | bytes 1572864 | tf_op jit(solution)/shard_map/all_to_all | solution.py:300
  204.6 2.7 shard_map.84
  207.3 8.5 %all_to_all.59.refs_1_ = bf16[4,48,512]{2,1,0:T(8,128)(2,1)} all-to-all(bf16[4,48,512]{2,1,0:T(8,128)(2,1)} %get-tuple-element.20), channel_id=1, replica_groups=mesh['x'=4,'yh'=2,'c'=2,'yl'=2,'zh'=8,'zl'=2] {'yl','zl'}, dimensions={0} | all-to-all | bytes 393216 | tf_op jit(solution)/shard_map/all_to_all | solution.py:300
  215.8 3.5 %shard_map.85 = bf16[8,96,256]{2,1,0:T(8,128)(2,1)} custom-call(s32[6]{0:T(128)} %stack.27.idx.refs_0_, bf16[4,48,512]{2,1,0:T(8,128)(2,1)} %all_to_all.59.refs_1_, bf16[2,128,2048]{2,1,0:T(8,128)(2,1)} %get-tuple-element.15.refs_1_.refs_2_.refs_3_, bf16[2,128,2048]{2,1,0:T(8,128)(2,1)} %copy-done, bf16[2,128,2048]{2,1,0:T(8,128)(2,1)} %copy-done.1, ...), custom_call_target="tpu_custom_call" | custom-call | tf_op jit(solution)/shard_map/pallas_call | solution.py:234
  219.2 29.0 %all_to_all.60.refs_1_ = bf16[8,96,256]{2,1,0:T(8,128)(2,1)} all-to-all(bf16[8,96,256]{2,1,0:T(8,128)(2,1)} %shard_map.85), channel_id=1, replica_groups=mesh['x'=4,'yh'=2,'c'=2,'yl'=2,'zh'=8,'zl'=2] {'zh'}, dimensions={0} | all-to-all | bytes 786432 | tf_op jit(solution)/shard_map/all_to_all | solution.py:300
  248.2 1.8 shard_map.86
  250.0 8.7 %all_to_all.61.quarters = f32[4,16,512]{2,1,0:T(8,128)} all-to-all(f32[4,16,512]{2,1,0:T(8,128)} %get-tuple-element.24), channel_id=1, replica_groups=mesh['x'=4,'yh'=2,'c'=2,'yl'=2,'zh'=8,'zl'=2] {'yl','zl'}, dimensions={0} | all-to-all | bytes 262144 | tf_op jit(solution)/shard_map/all_to_all | solution.py:300
  258.7 2.4 shard_map.87
  261.1 31.3 %all_to_all.62.parts = bf16[16,32,256]{2,1,0:T(8,128)(2,1)} all-to-all(bf16[16,32,256]{2,1,0:T(8,128)(2,1)} %bitcast.36), channel_id=1, replica_groups=mesh['x'=4,'yh'=2,'c'=2,'yl'=2,'zh'=8,'zl'=2] {'x','yh','c'}, dimensions={0} | all-to-all | bytes 524288 | tf_op jit(solution)/shard_map/all_to_all | solution.py:300
  292.3 1.6 shard_map.88
  (2 shorter events, 0.0 us)
Async XLA Ops:
  40.7 60.4 %copy-start.3 = (bf16[8,96,256]{2,1,0:T(8,128)(2,1)}, bf16[8,96,256]{2,1,0:T(8,128)(2,1)S(1)}, u32[]{:S(2)}) copy-start(bf16[8,96,256]{2,1,0:T(8,128)(2,1)S(1)} %all_to_all.55.refs_8_) | copy-start | bytes 1179652
  41.9 20.2 %all-to-all-start.1 = ((bf16[8,32,2048]{2,1,0:T(8,128)(2,1)}), bf16[8,32,2048]{2,1,0:T(8,128)(2,1)}, u32[]{:S(2)}, u32[]{:S(2)}) async-start(bf16[8,32,2048]{2,1,0:T(8,128)(2,1)} %broadcast_in_dim.9), calls=%async_computation.1 | async-start | bytes 2097152 | tf_op jit(solution)/shard_map/all_to_all | solution.py:300
  53.7 34.5 %collective-permute-start = (bf16[2,128,2048]{2,1,0:T(8,128)(2,1)}, bf16[2,128,2048]{2,1,0:T(8,128)(2,1)S(1)}, u32[]{:S(2)}, u32[]{:S(2)}) collective-permute-start(bf16[2,128,2048]{2,1,0:T(8,128)(2,1)} %get-tuple-element.16), channel_id=1, source_target_pairs={{0,16},{16,0},{1,17},{17,1},{2,18},{18,2},{3,19},{19,3},{4,20},{20... | collective-permute-start | bytes 3145736 | tf_op jit(solution)/shard_map/ppermute | solution.py:292
  56.0 32.2 %collective-permute-start.1 = (bf16[2,128,2048]{2,1,0:T(8,128)(2,1)}, bf16[2,128,2048]{2,1,0:T(8,128)(2,1)S(1)}, u32[]{:S(2)}, u32[]{:S(2)}) collective-permute-start(bf16[2,128,2048]{2,1,0:T(8,128)(2,1)} %get-tuple-element.17), channel_id=1, source_target_pairs={{0,1},{1,0},{2,3},{3,2},{4,5},{5,4},{6,7},{7,6},{8,9},{9,8},{10,11... | collective-permute-start | bytes 3145736 | tf_op jit(solution)/shard_map/ppermute | solution.py:292
  58.1 43.0 %collective-permute-start.2 = (bf16[2,128,2048]{2,1,0:T(8,128)(2,1)}, bf16[2,128,2048]{2,1,0:T(8,128)(2,1)S(1)}, u32[]{:S(2)}, u32[]{:S(2)}) collective-permute-start(bf16[2,128,2048]{2,1,0:T(8,128)(2,1)} %get-tuple-element.18), channel_id=1, source_target_pairs={{0,17},{1,16},{16,1},{17,0},{2,19},{3,18},{18,3},{19,2},{4,21},{5,... | collective-permute-start | bytes 3145736 | tf_op jit(solution)/shard_map/ppermute | solution.py:296
  62.1 39.0 %collective-permute-start.3 = (bf16[8,32,2048]{2,1,0:T(8,128)(2,1)}, bf16[8,32,2048]{2,1,0:T(8,128)(2,1)}, u32[]{:S(2)}, u32[]{:S(2)}) collective-permute-start(bf16[8,32,2048]{2,1,0:T(8,128)(2,1)} %all-to-all-done.1.refs_5_), channel_id=1, source_target_pairs={{0,32},{32,0},{1,33},{33,1},{2,34},{34,2},{3,35},{35,3},{4,36},{36... | collective-permute-start | bytes 3145736 | tf_op jit(solution)/shard_map/ppermute | solution.py:292
  88.2 12.9 %copy-start = (bf16[2,128,2048]{2,1,0:T(8,128)(2,1)}, bf16[2,128,2048]{2,1,0:T(8,128)(2,1)S(1)}, u32[]{:S(2)}) copy-start(bf16[2,128,2048]{2,1,0:T(8,128)(2,1)S(1)} %collective-permute-done.refs_2_.refs_3_.refs_4_) | copy-start | bytes 3145732
  88.2 12.9 %copy-start.1 = (bf16[2,128,2048]{2,1,0:T(8,128)(2,1)}, bf16[2,128,2048]{2,1,0:T(8,128)(2,1)S(1)}, u32[]{:S(2)}) copy-start(bf16[2,128,2048]{2,1,0:T(8,128)(2,1)S(1)} %collective-permute-done.1.refs_3_.refs_4_.refs_5_) | copy-start | bytes 3145732
  101.1 1.0 copy-start.2
  140.1 22.8 %all-to-all-start.4 = ((bf16[8,72,256]{2,1,0:T(8,128)(2,1)}), bf16[8,72,256]{2,1,0:T(8,128)(2,1)S(1)}, u32[]{:S(2)}, u32[]{:S(2)}) async-start(bf16[8,72,256]{2,1,0:T(8,128)(2,1)} %shard_map.81), calls=%async_computation.4 | async-start | bytes 589824 | tf_op jit(solution)/shard_map/all_to_all | solution.py:300
  162.9 0.7 copy-start.5
  165.5 21.6 %all-to-all-start.5 = ((bf16[8,72,256]{2,1,0:T(8,128)(2,1)}), bf16[8,72,256]{2,1,0:T(8,128)(2,1)S(1)}, u32[]{:S(2)}, u32[]{:S(2)}) async-start(bf16[8,72,256]{2,1,0:T(8,128)(2,1)} %get-tuple-element.19), calls=%async_computation.5 | async-start | bytes 589824 | tf_op jit(solution)/shard_map/all_to_all | solution.py:300
  187.1 0.7 copy-start.4

commit v8 on v7

--- a/solution.py
+++ b/solution.py
@@ -68,24 +68,26 @@
 
 
 def keys_kernel(step, scale, idx, *rest):
-    x_refs, pieces, y_ref, out, bs = rest[:4], rest[4:6], rest[6], rest[-2], rest[-1]
+    x_refs, pieces, y_ref, out, bs = rest[:4], rest[4:12], rest[12], rest[-2], rest[-1]
     rows, quarter = x_refs[0].shape[1:]
+    px, pyh, pc = idx[0], idx[1], idx[2]
     places = [group_at(idx, k) for k in range(4)]
     tokens = jnp.concatenate([ref[0] for ref in x_refs], axis=0)
     if step == 0:
-        whole = rest[7]
+        whole = rest[13]
         a_half = jnp.concatenate([whole[z, 32:] for z in range(NZ)], axis=1)
         low = dot(a_half, tokens, 1, 1) * scale
         for k in range(4):
             hi, lo = split(low[:, k * rows : (k + 1) * rows])
             out[places[k], rows : rows + 16] = wide(hi)
             out[places[k], rows + 16 :] = wide(lo)
-    for x in range(4):
+    for dx in range(4):
         for dc in range(2):
-            for y in range(2):
-                bs[x, 2 * y + lax.rem(idx[2] + dc, 2)] = pieces[dc][2 * x + y]
-        at = slice(x * 128, x * 128 + 128)
-        part = dot(tokens, bs[x].reshape(128, quarter), 1, 1) * scale
+            for dy in range(2):
+                w = lax.rem(pyh + dy, 2) * 2 + lax.rem(pc + dc, 2)
+                bs[dx, w] = pieces[4 * dc + dx][dy]
+        at = pl.ds(pl.multiple_of(lax.rem(px + 4 - dx, 4) * 128, 128), 128)
+        part = dot(tokens, bs[dx].reshape(128, quarter), 1, 1) * scale
         for k in range(4):
             value = part[k * rows : (k + 1) * rows]
             if k == 0:
@@ -296,6 +298,10 @@
     return lax.ppermute(value, Q, [(k, 3 - k) for k in range(4)])
 
 
+def shift(value, axis, by, count):
+    return lax.ppermute(value, axis, [(i, (i + by) % count) for i in range(count)])
+
+
 def exchange(parts, axis):
     return lax.all_to_all(parts, axis, 0, 0, tiled=True)
 
@@ -316,8 +322,9 @@
     xs = (own, swap(to_y, "yl"), swap(to_z, "zl"), swap_both(to_both))
     whole = exchange(call(start_kernel, shaped((NZ, 96, 256), bf16), base.T, a_start), "zh")
     cols = whole[:, :32].transpose(1, 0, 2).reshape(32, width // 4)
-    near = exchange(jnp.broadcast_to(cols, (8, *cols.shape)), ("x", "yh"))
-    pieces = (near, swap(near, "c"))
+    pair = jnp.stack([cols, swap(cols, "yh")])
+    near = [pair] + [shift(pair, "x", d, 4) for d in (1, 2, 3)]
+    pieces = near + [swap(piece, "c") for piece in near]
 
     error_shape = shaped((4, 48, 512), bf16)
 

time: 295 us -> 270 us (0.915)
  blocking collectives: 154 us -> 102 us
  starting transfers between devices: 34.3 us -> 72.2 us
  waiting for transfers between devices: 56.7 us -> 41.1 us
    all_to_all x8 -> x7, blocking collectives: 154 us -> 102 us  [exchange(): return lax.all_to_all(parts, axis, 0, 0, tiled=True)]
    all_to_all x3, starting transfers between devices: 18.5 us -> 33.5 us  [exchange(): return lax.all_to_all(parts, axis, 0, 0, tiled=True)]
    ppermute x3 -> x7, starting transfers between devices: 11.8 us -> 26.3 us  [swap(): return lax.ppermute(value, axis, [(0, 1), (1, 0)])]
    ppermute x3 -> x7, waiting for transfers between devices: 18.6 us -> 5.76 us  [swap(): return lax.ppermute(value, axis, [(0, 1), (1, 0)])]
    ppermute x1, waiting for transfers between devices: 12.9 us -> 1.67 us  [swap_both(): return lax.ppermute(value, Q, [(k, 3 - k) for k in range(4)])]
    ppermute x0 -> x3, starting transfers between devices: none -> 9.93 us  [shift(): lax.ppermute(value, axis, [(i, (i + by) % count) for i in range(count)])]
    all_to_all x3, waiting for transfers between devices: 25.2 us -> 33.7 us  [exchange(): return lax.all_to_all(parts, axis, 0, 0, tiled=True)]
  transfers between devices with their start and end apart: 7 -> 14, of which waited for: 4 -> 5; matrix products, arithmetic and copies ran while one was open for 1% -> 2% of each run, Pallas kernels for 4% -> 4%
where the time goes in v8:
time: 270 us; the launch traced here: 268 us
  blocking collectives  102 us (38%)
  starting transfers between devices  72.2 us (27%)
  Pallas kernels  42.9 us (16%)
  waiting for transfers between devices  41.1 us (15%)
  local copies, waits for them, and re-layouts  7.98 us (3%)
    all_to_all x7, blocking collectives, exchange(): return lax.all_to_all(parts, axis, 0, 0, tiled=True)  102 us
    all_to_all x3, waiting for transfers between devices, exchange(): return lax.all_to_all(parts, axis, 0, 0, tiled=True)  33.7 us
    all_to_all x3, starting transfers between devices, exchange(): return lax.all_to_all(parts, axis, 0, 0, tiled=True)  33.5 us
    ppermute x7, starting transfers between devices, swap(): return lax.ppermute(value, axis, [(0, 1), (1, 0)])  26.3 us
    pallas_call x2, Pallas kernels, keys_of(): pl.pallas_call(body, out_shape=shape, grid_spec=pltpu.PrefetchScalarGridS...  13.1 us
    pallas_call x6, Pallas kernels, call(): pl.pallas_call(kernel, out_shape=shapes, in_specs=vmem(len(args)), compil...  12.8 us
    ppermute x3, starting transfers between devices, shift(): lax.ppermute(value, axis, [(i, (i + by) % count) for i in range(count)])  9.93 us
    pallas_call x2, Pallas kernels, with_tokens(): pl.pallas_call(kernel, out_shape=shape, grid_spec=pltpu.PrefetchScalarGri...  6.95 us
  transfers between devices with their start and end apart: 14, of which 5 were waited for; matrix products, arithmetic and copies ran while one was open for 2% of the time, Pallas kernels for 4%

profile of v8, /device:TPU:1, one launch (start us, length us, event | category | flops | bytes accessed | tf_op | source)
XLA Modules:
  0.0 267.8 jit_solution(232731718701299341)
XLA Ops:
  0.6 1.7 shard_map.77
  2.3 15.6 %all-to-all-start = ((bf16[8,96,256]{2,1,0:T(8,128)(2,1)}), bf16[8,96,256]{2,1,0:T(8,128)(2,1)S(1)}, u32[]{:S(2)}, u32[]{:S(2)}) async-start(bf16[8,96,256]{2,1,0:T(8,128)(2,1)} %shard_map.77), calls=%async_computation | async-start | bytes 786432 | tf_op jit(solution)/shard_map/all_to_all | solution.py:306
  17.9 0.7 stack.33.idx.refs_0_
  18.6 4.6 %shard_map.76 = (bf16[2,128,2048]{2,1,0:T(8,128)(2,1)}, bf16[2,128,2048]{2,1,0:T(8,128)(2,1)}, bf16[2,128,2048]{2,1,0:T(8,128)(2,1)}, bf16[2,128,2048]{2,1,0:T(8,128)(2,1)}) custom-call(s32[6]{0:T(128)} %stack.33.idx.refs_0_, bf16[2,128,8192]{2,1,0:T(8,128)(2,1)} %bitcast.29), custom_call_target="tpu_custom_call" | custom-call | tf_op jit(solution)/shard_map/pallas_call | solution.py:218
  23.2 3.2 %collective-permute-start = (bf16[2,128,2048]{2,1,0:T(8,128)(2,1)}, bf16[2,128,2048]{2,1,0:T(8,128)(2,1)S(1)}, u32[]{:S(2)}, u32[]{:S(2)}) collective-permute-start(bf16[2,128,2048]{2,1,0:T(8,128)(2,1)} %get-tuple-element.16), channel_id=1, source_target_pairs={{0,16},{16,0},{1,17},{17,1},{2,18},{18,2},{3,19},{19,3},{4,20},{20... | collective-permute-start | bytes 3145736 | tf_op jit(solution)/shard_map/ppermute | solution.py:294
  26.4 2.6 collective-permute-start.1
  29.0 2.5 collective-permute-start.2
  31.6 8.8 %all-to-all-done.refs_14_ = bf16[8,96,256]{2,1,0:T(8,128)(2,1)S(1)} async-done(((bf16[8,96,256]{2,1,0:T(8,128)(2,1)}), bf16[8,96,256]{2,1,0:T(8,128)(2,1)S(1)}, u32[]{:S(2)}, u32[]{:S(2)}) %all-to-all-start) | async-done | bytes 393248 | tf_op jit(solution)/shard_map/all_to_all | solution.py:306
  40.4 0.8 copy.11
  41.1 4.8 %collective-permute-start.3 = (bf16[32,2048]{1,0:T(8,128)(2,1)}, bf16[32,2048]{1,0:T(8,128)(2,1)}, u32[]{:S(2)}, u32[]{:S(2)}) collective-permute-start(bf16[32,2048]{1,0:T(8,128)(2,1)} %bitcast.25), channel_id=1, source_target_pairs={{0,64},{64,0},{1,65},{65,1},{2,66},{66,2},{3,67},{67,3},{4,68},{68... | collective-permute-start | bytes 393224 | tf_op jit(solution)/shard_map/ppermute | solution.py:294
  46.0 0.7 copy.9
  46.7 1.6 stack_reshape.3
  48.4 5.7 %collective-permute-done.3 = bf16[32,2048]{1,0:T(8,128)(2,1)} collective-permute-done((bf16[32,2048]{1,0:T(8,128)(2,1)}, bf16[32,2048]{1,0:T(8,128)(2,1)}, u32[]{:S(2)}, u32[]{:S(2)}) %collective-permute-start.3) | collective-permute-done | bytes 131104 | tf_op jit(solution)/shard_map/ppermute | solution.py:294
  54.1 0.0 copy-done.4
  54.1 1.0 pad_maximum_fusion.refs_5_
  55.1 4.4 %collective-permute-start.6 = (bf16[2,32,2048]{2,1,0:T(8,128)(2,1)S(1)}, bf16[2,32,2048]{2,1,0:T(8,128)(2,1)S(1)}, u32[]{:S(2)}, u32[]{:S(2)}) collective-permute-start(bf16[2,32,2048]{2,1,0:T(8,128)(2,1)S(1)} %pad_maximum_fusion.refs_5_), channel_id=1, source_target_pairs={{0,384},{128,0},{256,128},{384,256},{1,385},{129,1},{257,129},{385... | collective-permute-start | bytes 786440 | tf_op jit(solution)/shard_map/ppermute | solution.py:302
  59.5 1.9 collective-permute-start.4
  61.4 0.0 collective-permute-done.refs_2_.refs_3_.refs_4_
  61.4 0.0 copy-start
  61.5 3.6 %collective-permute-start.5 = (bf16[2,32,2048]{2,1,0:T(8,128)(2,1)S(1)}, bf16[2,32,2048]{2,1,0:T(8,128)(2,1)S(1)}, u32[]{:S(2)}, u32[]{:S(2)}) collective-permute-start(bf16[2,32,2048]{2,1,0:T(8,128)(2,1)S(1)} %pad_maximum_fusion.refs_5_), channel_id=1, source_target_pairs={{0,256},{128,384},{256,0},{384,128},{1,257},{129,385},{257,1},{385... | collective-permute-start | bytes 786440 | tf_op jit(solution)/shard_map/ppermute | solution.py:302
  65.1 0.0 collective-permute-done.1.refs_3_.refs_4_.refs_5_
  65.1 4.9 %collective-permute-start.7 = (bf16[2,32,2048]{2,1,0:T(8,128)(2,1)S(1)}, bf16[2,32,2048]{2,1,0:T(8,128)(2,1)S(1)}, u32[]{:S(2)}, u32[]{:S(2)}) collective-permute-start(bf16[2,32,2048]{2,1,0:T(8,128)(2,1)S(1)} %pad_maximum_fusion.refs_5_), channel_id=1, source_target_pairs={{0,32},{32,0},{1,33},{33,1},{2,34},{34,2},{3,35},{35,3},{4,36},{36... | collective-permute-start | bytes 786440 | tf_op jit(solution)/shard_map/ppermute | solution.py:294
  70.0 0.0 collective-permute-done.6.refs_8_
  70.0 1.9 collective-permute-start.10
  71.9 0.0 collective-permute-done.4.refs_6_
  71.9 6.9 %collective-permute-start.8 = (bf16[2,32,2048]{2,1,0:T(8,128)(2,1)S(1)}, bf16[2,32,2048]{2,1,0:T(8,128)(2,1)S(1)}, u32[]{:S(2)}, u32[]{:S(2)}) collective-permute-start(bf16[2,32,2048]{2,1,0:T(8,128)(2,1)S(1)} %collective-permute-done.4.refs_6_), channel_id=1, source_target_pairs={{0,32},{32,0},{1,33},{33,1},{2,34},{34,2},{3,35},{35,3},{4,36},{36... | collective-permute-start | bytes 786440 | tf_op jit(solution)/shard_map/ppermute | solution.py:294
  78.9 0.0 collective-permute-done.5.refs_7_
  78.9 1.9 collective-permute-start.9
  80.8 1.7 collective-permute-done.2.refs_4_.refs_5_.refs_6_
  82.5 0.0 collective-permute-done.7.refs_9_
  82.5 0.0 collective-permute-done.10.refs_12_
  82.5 0.0 copy-start.11
  82.5 0.0 collective-permute-done.8.refs_10_
  82.5 0.0 collective-permute-done.9.refs_11_
  82.5 0.7 copy-done.10
  83.2 0.1 copy-done.11
  83.3 0.1 copy-done.12
  83.4 0.5 copy-done.13
  83.9 0.0 copy-done.1
  84.0 6.9 %shard_map.79 = bf16[4,160,512]{2,1,0:T(8,128)(2,1)} custom-call(s32[6]{0:T(128)} %stack.33.idx.refs_0_, bf16[2,128,2048]{2,1,0:T(8,128)(2,1)} %get-tuple-element.15.refs_1_.refs_2_.refs_3_, bf16[2,128,2048]{2,1,0:T(8,128)(2,1)} %copy-done, bf16[2,128,2048]{2,1,0:T(8,128)(2,1)} %copy-done.1, bf16[2,128,2048]{2,1,0:T(8,128)(2,1)} %copy-done.2, ...), custom_call_target="tpu_custom_call" | custom-call | tf_op jit(solution)/shard_map/pallas_call | solution.py:256
  90.9 12.9 %all_to_all.50.refs_0_ = bf16[4,160,512]{2,1,0:T(8,128)(2,1)} all-to-all(bf16[4,160,512]{2,1,0:T(8,128)(2,1)} %shard_map.79), channel_id=1, replica_groups=mesh['x'=4,'yh'=2,'c'=2,'yl'=2,'zh'=8,'zl'=2] {'yl','zl'}, dimensions={0} | all-to-all | bytes 1310720 | tf_op jit(solution)/shard_map/all_to_all | solution.py:306
  103.8 2.7 shard_map.80
  106.5 8.4 %all_to_all.51.refs_1_ = bf16[4,48,512]{2,1,0:T(8,128)(2,1)} all-to-all(bf16[4,48,512]{2,1,0:T(8,128)(2,1)} %shard_map.80), channel_id=1, replica_groups=mesh['x'=4,'yh'=2,'c'=2,'yl'=2,'zh'=8,'zl'=2] {'yl','zl'}, dimensions={0} | all-to-all | bytes 393216 | tf_op jit(solution)/shard_map/all_to_all | solution.py:306
  114.9 3.5 %shard_map.81 = bf16[8,72,256]{2,1,0:T(8,128)(2,1)} custom-call(s32[6]{0:T(128)} %stack.33.idx.refs_0_, bf16[4,48,512]{2,1,0:T(8,128)(2,1)} %all_to_all.51.refs_1_, bf16[2,128,2048]{2,1,0:T(8,128)(2,1)} %get-tuple-element.15.refs_1_.refs_2_.refs_3_, bf16[2,128,2048]{2,1,0:T(8,128)(2,1)} %copy-done, bf16[2,128,2048]{2,1,0:T(8,128)(2,1)} %copy-done.1, ...), custom_call_target="tpu_custom_call" | custom-call | tf_op jit(solution)/shard_map/pallas_call | solution.py:236
  118.4 10.1 %all-to-all-start.3 = ((bf16[8,72,256]{2,1,0:T(8,128)(2,1)}), bf16[8,72,256]{2,1,0:T(8,128)(2,1)S(1)}, u32[]{:S(2)}, u32[]{:S(2)}) async-start(bf16[8,72,256]{2,1,0:T(8,128)(2,1)} %shard_map.81), calls=%async_computation.3 | async-start | bytes 589824 | tf_op jit(solution)/shard_map/all_to_all | solution.py:306
  128.5 1.3 dynamic-slice_bitcast_fusion.refs_2_
  129.7 14.2 %all-to-all-done.3.refs_0_ = bf16[8,72,256]{2,1,0:T(8,128)(2,1)S(1)} async-done(((bf16[8,72,256]{2,1,0:T(8,128)(2,1)}), bf16[8,72,256]{2,1,0:T(8,128)(2,1)S(1)}, u32[]{:S(2)}, u32[]{:S(2)}) %all-to-all-start.3) | async-done | bytes 294944 | tf_op jit(solution)/shard_map/all_to_all | solution.py:306
  143.9 0.7 copy-done.6
  144.7 1.8 shard_map.82
  146.5 7.8 %all-to-all-start.4 = ((bf16[8,72,256]{2,1,0:T(8,128)(2,1)}), bf16[8,72,256]{2,1,0:T(8,128)(2,1)S(1)}, u32[]{:S(2)}, u32[]{:S(2)}) async-start(bf16[8,72,256]{2,1,0:T(8,128)(2,1)} %get-tuple-element.19), calls=%async_computation.4 | async-start | bytes 589824 | tf_op jit(solution)/shard_map/all_to_all | solution.py:306
  154.3 6.2 %shard_map.78.refs_1_ = bf16[4,192,512]{2,1,0:T(8,128)(2,1)} custom-call(s32[6]{0:T(128)} %stack.33.idx.refs_0_, bf16[2,128,2048]{2,1,0:T(8,128)(2,1)} %get-tuple-element.15.refs_1_.refs_2_.refs_3_, bf16[2,128,2048]{2,1,0:T(8,128)(2,1)} %copy-done, bf16[2,128,2048]{2,1,0:T(8,128)(2,1)} %copy-done.1, bf16[2,128,2048]{2,1,0:T(8,128)(2,1)} %copy-done.2, ...), custom_call_target="tpu_custom_call" | custom-call | tf_op jit(solution)/shard_map/pallas_call | solution.py:256
  160.4 10.7 %all-to-all-done.4.refs_2_ = bf16[8,72,256]{2,1,0:T(8,128)(2,1)S(1)} async-done(((bf16[8,72,256]{2,1,0:T(8,128)(2,1)}), bf16[8,72,256]{2,1,0:T(8,128)(2,1)S(1)}, u32[]{:S(2)}, u32[]{:S(2)}) %all-to-all-start.4) | async-done | bytes 294944 | tf_op jit(solution)/shard_map/all_to_all | solution.py:306
  171.1 0.7 copy-done.5
  171.8 3.8 %shard_map.83 = bf16[4,192,512]{2,1,0:T(8,128)(2,1)} custom-call(s32[6]{0:T(128)} %stack.33.idx.refs_0_, bf16[4,192,512]{2,1,0:T(8,128)(2,1)} %shard_map.78.refs_1_, bf16[8,72,256]{2,1,0:T(8,128)(2,1)} %copy-done.5, bf16[2,128,2048]{2,1,0:T(8,128)(2,1)} %get-tuple-element.15.refs_1_.refs_2_.refs_3_, ...), custom_call_target="tpu_custom_call", output_to_operand_aliasing={{}: (1, {})} | custom-call | tf_op jit(solution)/shard_map/pallas_call | solution.py:277
  175.6 11.7 %all_to_all.52.refs_0_ = bf16[4,192,512]{2,1,0:T(8,128)(2,1)} all-to-all(bf16[4,192,512]{2,1,0:T(8,128)(2,1)} %shard_map.83), channel_id=1, replica_groups=mesh['x'=4,'yh'=2,'c'=2,'yl'=2,'zh'=8,'zl'=2] {'yl','zl'}, dimensions={0} | all-to-all | bytes 1572864 | tf_op jit(solution)/shard_map/all_to_all | solution.py:306
  187.2 2.7 %shard_map.84 = (bf16[4,48,512]{2,1,0:T(8,128)(2,1)}, f32[64,512]{1,0:T(8,128)}) custom-call(bf16[4,192,512]{2,1,0:T(8,128)(2,1)} %all_to_all.52.refs_0_), custom_call_target="tpu_custom_call" | custom-call | tf_op jit(solution)/shard_map/pallas_call | solution.py:212
  189.9 8.5 %all_to_all.53.refs_1_ = bf16[4,48,512]{2,1,0:T(8,128)(2,1)} all-to-all(bf16[4,48,512]{2,1,0:T(8,128)(2,1)} %get-tuple-element.20), channel_id=1, replica_groups=mesh['x'=4,'yh'=2,'c'=2,'yl'=2,'zh'=8,'zl'=2] {'yl','zl'}, dimensions={0} | all-to-all | bytes 393216 | tf_op jit(solution)/shard_map/all_to_all | solution.py:306
  198.4 3.5 %shard_map.85 = bf16[8,96,256]{2,1,0:T(8,128)(2,1)} custom-call(s32[6]{0:T(128)} %stack.33.idx.refs_0_, bf16[4,48,512]{2,1,0:T(8,128)(2,1)} %all_to_all.53.refs_1_, bf16[2,128,2048]{2,1,0:T(8,128)(2,1)} %get-tuple-element.15.refs_1_.refs_2_.refs_3_, bf16[2,128,2048]{2,1,0:T(8,128)(2,1)} %copy-done, bf16[2,128,2048]{2,1,0:T(8,128)(2,1)} %copy-done.1, ...), custom_call_target="tpu_custom_call" | custom-call | tf_op jit(solution)/shard_map/pallas_call | solution.py:236
  201.9 27.6 %all_to_all.54.refs_1_ = bf16[8,96,256]{2,1,0:T(8,128)(2,1)} all-to-all(bf16[8,96,256]{2,1,0:T(8,128)(2,1)} %shard_map.85), channel_id=1, replica_groups=mesh['x'=4,'yh'=2,'c'=2,'yl'=2,'zh'=8,'zl'=2] {'zh'}, dimensions={0} | all-to-all | bytes 786432 | tf_op jit(solution)/shard_map/all_to_all | solution.py:306
  229.5 1.8 shard_map.86
  231.3 7.9 %all_to_all.55.quarters = f32[4,16,512]{2,1,0:T(8,128)} all-to-all(f32[4,16,512]{2,1,0:T(8,128)} %get-tuple-element.24), channel_id=1, replica_groups=mesh['x'=4,'yh'=2,'c'=2,'yl'=2,'zh'=8,'zl'=2] {'yl','zl'}, dimensions={0} | all-to-all | bytes 262144 | tf_op jit(solution)/shard_map/all_to_all | solution.py:306
  239.2 2.4 shard_map.87
  241.5 24.7 %all_to_all.56.parts = bf16[16,32,256]{2,1,0:T(8,128)(2,1)} all-to-all(bf16[16,32,256]{2,1,0:T(8,128)(2,1)} %bitcast.37), channel_id=1, replica_groups=mesh['x'=4,'yh'=2,'c'=2,'yl'=2,'zh'=8,'zl'=2] {'x','yh','c'}, dimensions={0} | all-to-all | bytes 524288 | tf_op jit(solution)/shard_map/all_to_all | solution.py:306
  266.2 1.6 shard_map.88
  (19 shorter events, 0.1 us)
Async XLA Ops:
  2.3 38.1 %all-to-all-start = ((bf16[8,96,256]{2,1,0:T(8,128)(2,1)}), bf16[8,96,256]{2,1,0:T(8,128)(2,1)S(1)}, u32[]{:S(2)}, u32[]{:S(2)}) async-start(bf16[8,96,256]{2,1,0:T(8,128)(2,1)} %shard_map.77), calls=%async_computation | async-start | bytes 786432 | tf_op jit(solution)/shard_map/all_to_all | solution.py:306
  23.2 38.3 %collective-permute-start = (bf16[2,128,2048]{2,1,0:T(8,128)(2,1)}, bf16[2,128,2048]{2,1,0:T(8,128)(2,1)S(1)}, u32[]{:S(2)}, u32[]{:S(2)}) collective-permute-start(bf16[2,128,2048]{2,1,0:T(8,128)(2,1)} %get-tuple-element.16), channel_id=1, source_target_pairs={{0,16},{16,0},{1,17},{17,1},{2,18},{18,2},{3,19},{19,3},{4,20},{20... | collective-permute-start | bytes 3145736 | tf_op jit(solution)/shard_map/ppermute | solution.py:294
  26.4 38.7 %collective-permute-start.1 = (bf16[2,128,2048]{2,1,0:T(8,128)(2,1)}, bf16[2,128,2048]{2,1,0:T(8,128)(2,1)S(1)}, u32[]{:S(2)}, u32[]{:S(2)}) collective-permute-start(bf16[2,128,2048]{2,1,0:T(8,128)(2,1)} %get-tuple-element.17), channel_id=1, source_target_pairs={{0,1},{1,0},{2,3},{3,2},{4,5},{5,4},{6,7},{7,6},{8,9},{9,8},{10,11... | collective-permute-start | bytes 3145736 | tf_op jit(solution)/shard_map/ppermute | solution.py:294
  29.0 53.4 %collective-permute-start.2 = (bf16[2,128,2048]{2,1,0:T(8,128)(2,1)}, bf16[2,128,2048]{2,1,0:T(8,128)(2,1)S(1)}, u32[]{:S(2)}, u32[]{:S(2)}) collective-permute-start(bf16[2,128,2048]{2,1,0:T(8,128)(2,1)} %get-tuple-element.18), channel_id=1, source_target_pairs={{0,17},{1,16},{16,1},{17,0},{2,19},{3,18},{18,3},{19,2},{4,21},{5,... | collective-permute-start | bytes 3145736 | tf_op jit(solution)/shard_map/ppermute | solution.py:298
  40.4 13.7 %copy-start.4 = (bf16[8,96,256]{2,1,0:T(8,128)(2,1)}, bf16[8,96,256]{2,1,0:T(8,128)(2,1)S(1)}, u32[]{:S(2)}) copy-start(bf16[8,96,256]{2,1,0:T(8,128)(2,1)S(1)} %all-to-all-done.refs_14_) | copy-start | bytes 1179652
  41.1 12.9 %collective-permute-start.3 = (bf16[32,2048]{1,0:T(8,128)(2,1)}, bf16[32,2048]{1,0:T(8,128)(2,1)}, u32[]{:S(2)}, u32[]{:S(2)}) collective-permute-start(bf16[32,2048]{1,0:T(8,128)(2,1)} %bitcast.25), channel_id=1, source_target_pairs={{0,64},{64,0},{1,65},{65,1},{2,66},{66,2},{3,67},{67,3},{4,68},{68... | collective-permute-start | bytes 393224 | tf_op jit(solution)/shard_map/ppermute | solution.py:294
  55.1 28.8 %copy-start.3 = (bf16[2,32,2048]{2,1,0:T(8,128)(2,1)}, bf16[2,32,2048]{2,1,0:T(8,128)(2,1)S(1)}, u32[]{:S(2)}) copy-start(bf16[2,32,2048]{2,1,0:T(8,128)(2,1)S(1)} %pad_maximum_fusion.refs_5_) | copy-start | bytes 786436
  55.1 14.9 %collective-permute-start.6 = (bf16[2,32,2048]{2,1,0:T(8,128)(2,1)S(1)}, bf16[2,32,2048]{2,1,0:T(8,128)(2,1)S(1)}, u32[]{:S(2)}, u32[]{:S(2)}) collective-permute-start(bf16[2,32,2048]{2,1,0:T(8,128)(2,1)S(1)} %pad_maximum_fusion.refs_5_), channel_id=1, source_target_pairs={{0,384},{128,0},{256,128},{384,256},{1,385},{129,1},{257,129},{385... | collective-permute-start | bytes 786440 | tf_op jit(solution)/shard_map/ppermute | solution.py:302
  59.5 12.4 %collective-permute-start.4 = (bf16[2,32,2048]{2,1,0:T(8,128)(2,1)S(1)}, bf16[2,32,2048]{2,1,0:T(8,128)(2,1)S(1)}, u32[]{:S(2)}, u32[]{:S(2)}) collective-permute-start(bf16[2,32,2048]{2,1,0:T(8,128)(2,1)S(1)} %pad_maximum_fusion.refs_5_), channel_id=1, source_target_pairs={{0,128},{128,256},{256,384},{384,0},{1,129},{129,257},{257,385},{3... | collective-permute-start | bytes 786440 | tf_op jit(solution)/shard_map/ppermute | solution.py:302
  61.4 22.5 %copy-start = (bf16[2,128,2048]{2,1,0:T(8,128)(2,1)}, bf16[2,128,2048]{2,1,0:T(8,128)(2,1)S(1)}, u32[]{:S(2)}) copy-start(bf16[2,128,2048]{2,1,0:T(8,128)(2,1)S(1)} %collective-permute-done.refs_2_.refs_3_.refs_4_) | copy-start | bytes 3145732
  61.5 17.4 %collective-permute-start.5 = (bf16[2,32,2048]{2,1,0:T(8,128)(2,1)S(1)}, bf16[2,32,2048]{2,1,0:T(8,128)(2,1)S(1)}, u32[]{:S(2)}, u32[]{:S(2)}) collective-permute-start(bf16[2,32,2048]{2,1,0:T(8,128)(2,1)S(1)} %pad_maximum_fusion.refs_5_), channel_id=1, source_target_pairs={{0,256},{128,384},{256,0},{384,128},{1,257},{129,385},{257,1},{385... | collective-permute-start | bytes 786440 | tf_op jit(solution)/shard_map/ppermute | solution.py:302
  65.1 18.8 %copy-start.1 = (bf16[2,128,2048]{2,1,0:T(8,128)(2,1)}, bf16[2,128,2048]{2,1,0:T(8,128)(2,1)S(1)}, u32[]{:S(2)}) copy-start(bf16[2,128,2048]{2,1,0:T(8,128)(2,1)S(1)} %collective-permute-done.1.refs_3_.refs_4_.refs_5_) | copy-start | bytes 3145732
  65.1 17.4 %collective-permute-start.7 = (bf16[2,32,2048]{2,1,0:T(8,128)(2,1)S(1)}, bf16[2,32,2048]{2,1,0:T(8,128)(2,1)S(1)}, u32[]{:S(2)}, u32[]{:S(2)}) collective-permute-start(bf16[2,32,2048]{2,1,0:T(8,128)(2,1)S(1)} %pad_maximum_fusion.refs_5_), channel_id=1, source_target_pairs={{0,32},{32,0},{1,33},{33,1},{2,34},{34,2},{3,35},{35,3},{4,36},{36... | collective-permute-start | bytes 786440 | tf_op jit(solution)/shard_map/ppermute | solution.py:294
  70.0 14.0 %copy-start.7 = (bf16[2,32,2048]{2,1,0:T(8,128)(2,1)}, bf16[2,32,2048]{2,1,0:T(8,128)(2,1)S(1)}, u32[]{:S(2)}) copy-start(bf16[2,32,2048]{2,1,0:T(8,128)(2,1)S(1)} %collective-permute-done.6.refs_8_) | copy-start | bytes 786436
  70.0 12.5 %collective-permute-start.10 = (bf16[2,32,2048]{2,1,0:T(8,128)(2,1)S(1)}, bf16[2,32,2048]{2,1,0:T(8,128)(2,1)S(1)}, u32[]{:S(2)}, u32[]{:S(2)}) collective-permute-start(bf16[2,32,2048]{2,1,0:T(8,128)(2,1)S(1)} %collective-permute-done.6.refs_8_), channel_id=1, source_target_pairs={{0,32},{32,0},{1,33},{33,1},{2,34},{34,2},{3,35},{35,3},{4,36},{36... | collective-permute-start | bytes 786440 | tf_op jit(solution)/shard_map/ppermute | solution.py:294
  71.9 12.0 %copy-start.8 = (bf16[2,32,2048]{2,1,0:T(8,128)(2,1)}, bf16[2,32,2048]{2,1,0:T(8,128)(2,1)S(1)}, u32[]{:S(2)}) copy-start(bf16[2,32,2048]{2,1,0:T(8,128)(2,1)S(1)} %collective-permute-done.4.refs_6_) | copy-start | bytes 786436
  71.9 10.6 %collective-permute-start.8 = (bf16[2,32,2048]{2,1,0:T(8,128)(2,1)S(1)}, bf16[2,32,2048]{2,1,0:T(8,128)(2,1)S(1)}, u32[]{:S(2)}, u32[]{:S(2)}) collective-permute-start(bf16[2,32,2048]{2,1,0:T(8,128)(2,1)S(1)} %collective-permute-done.4.refs_6_), channel_id=1, source_target_pairs={{0,32},{32,0},{1,33},{33,1},{2,34},{34,2},{3,35},{35,3},{4,36},{36... | collective-permute-start | bytes 786440 | tf_op jit(solution)/shard_map/ppermute | solution.py:294
  78.9 3.6 %copy-start.9 = (bf16[2,32,2048]{2,1,0:T(8,128)(2,1)}, bf16[2,32,2048]{2,1,0:T(8,128)(2,1)S(1)}, u32[]{:S(2)}) copy-start(bf16[2,32,2048]{2,1,0:T(8,128)(2,1)S(1)} %collective-permute-done.5.refs_7_) | copy-start | bytes 786436
  78.9 3.7 %collective-permute-start.9 = (bf16[2,32,2048]{2,1,0:T(8,128)(2,1)S(1)}, bf16[2,32,2048]{2,1,0:T(8,128)(2,1)S(1)}, u32[]{:S(2)}, u32[]{:S(2)}) collective-permute-start(bf16[2,32,2048]{2,1,0:T(8,128)(2,1)S(1)} %collective-permute-done.5.refs_7_), channel_id=1, source_target_pairs={{0,32},{32,0},{1,33},{33,1},{2,34},{34,2},{3,35},{35,3},{4,36},{36... | collective-permute-start | bytes 786440 | tf_op jit(solution)/shard_map/ppermute | solution.py:294
  82.5 1.5 copy-start.2
  82.5 0.7 copy-start.10
  82.5 0.8 copy-start.11
  82.5 0.9 copy-start.12
  83.2 0.7 copy-start.13
  118.4 25.6 %all-to-all-start.3 = ((bf16[8,72,256]{2,1,0:T(8,128)(2,1)}), bf16[8,72,256]{2,1,0:T(8,128)(2,1)S(1)}, u32[]{:S(2)}, u32[]{:S(2)}) async-start(bf16[8,72,256]{2,1,0:T(8,128)(2,1)} %shard_map.81), calls=%async_computation.3 | async-start | bytes 589824 | tf_op jit(solution)/shard_map/all_to_all | solution.py:306
  143.9 0.7 copy-start.6
  146.5 24.6 %all-to-all-start.4 = ((bf16[8,72,256]{2,1,0:T(8,128)(2,1)}), bf16[8,72,256]{2,1,0:T(8,128)(2,1)S(1)}, u32[]{:S(2)}, u32[]{:S(2)}) async-start(bf16[8,72,256]{2,1,0:T(8,128)(2,1)} %get-tuple-element.19), calls=%async_computation.4 | async-start | bytes 589824 | tf_op jit(solution)/shard_map/all_to_all | solution.py:306
  171.1 0.7 copy-start.5

commit v9 on v5

--- a/solution.py
+++ b/solution.py
@@ -18,12 +18,17 @@
 
 bf16 = jnp.bfloat16
 f32 = jnp.float32
-HIGH = lax.Precision.HIGHEST
 VMEM = pltpu.CompilerParams(vmem_limit_bytes=60 * 1024 * 1024)
 
 
-def dot(a, b, ca, cb, precision=None):
-    return lax.dot_general(a, b, (((ca,), (cb,)), ((), ())), precision=precision, preferred_element_type=f32)
+def dot(a, b, ca, cb):
+    return lax.dot_general(a, b, (((ca,), (cb,)), ((), ())), preferred_element_type=f32)
+
+
+def fine_dot(a, b, ca, cb):
+    a_hi, a_lo = split(a)
+    b_hi, b_lo = split(b)
+    return dot(a_hi, b_hi, ca, cb) + (dot(a_hi, b_lo, ca, cb) + dot(a_lo, b_hi, ca, cb))
 
 
 def split(value):
@@ -37,6 +42,12 @@
 
 def smem():
     return pl.BlockSpec(memory_space=pltpu.SMEM)
+
+
+def start_kernel(base, a_ref, cols, downs):
+    for z in range(NZ):
+        cols[z] = base[...].astype(bf16)
+        downs[z] = a_ref[...].astype(bf16)
 
 
 def pack_kernel(idx, x_ref, *outs):
@@ -116,9 +127,9 @@
 
 
 def error_of(total_rows, keys, low, up, out):
-    error = (keys + branch_scale * dot(low, up, 0, 0, HIGH)) / total_rows
-    back = wide((branch_scale * dot(up, error, 1, 1, HIGH)).astype(bf16))
-    hi, lo = split(branch_scale * dot(low, error, 1, 0, HIGH))
+    error = (keys + branch_scale * fine_dot(low, up, 0, 0)) / total_rows
+    back = wide((branch_scale * fine_dot(up, error, 1, 1)).astype(bf16))
+    hi, lo = split(branch_scale * fine_dot(low, error, 1, 0))
     for q in range(4):
         out[q, :16] = back
         out[q, 16:32] = hi[16 * q : 16 * q + 16]
@@ -191,7 +202,7 @@
     up = jnp.concatenate([quarters[q] for q in range(4)], axis=0)
     left = jnp.concatenate([up, -up_start[...]], axis=0)
     right = jnp.concatenate([a_ref[...], a_start[...]], axis=0)
-    out[...] = (branch_scale * dot(left, right, 0, 0, HIGH)).astype(bf16)
+    out[...] = (branch_scale * fine_dot(left, right, 0, 0)).astype(bf16)
     b_out[...] = up
 
 
@@ -300,10 +311,6 @@
     return lax.all_to_all(parts, axis, 0, 0, tiled=True)
 
 
-def gather_z(value):
-    return exchange(jnp.broadcast_to(value, (NZ, *value.shape)), "zh")
-
-
 def whole_step(inputs, targets, base, adapter_a, adapter_b):
     tokens = inputs[0]
     a_start = adapter_a[0]
@@ -318,11 +325,14 @@
 
     own, to_y, to_z, to_both = pack(idx, tokens)
     xs = (own, swap(to_y, "yl"), swap(to_z, "zl"), swap_both(to_both))
-    cols = gather_z(base.T.astype(bf16))
+    columns, downs = call(
+        start_kernel, (shaped((NZ, 32, 256), bf16), shaped((NZ, 64, 256), bf16)), base.T, a_start
+    )
+    cols = exchange(columns, "zh")
     cols = cols.transpose(1, 0, 2).reshape(cols.shape[1], width // 4)
     pair = jnp.stack([cols, swap(cols, "yh")])
     near = [pair] + [shift(pair, "x", d, 4) for d in (1, 2, 3)]
-    whole = gather_z(a_start.astype(bf16))
+    whole = exchange(downs, "zh")
     pieces = near + [swap(piece, "c") for piece in near]
 
     error_shape = shaped((4, 48, 512), bf16)

time: 274 us -> 276 us (level)
  waiting for transfers between devices: 39.1 us -> 50 us
  starting transfers between devices: 82.6 us -> 72.1 us
    all_to_all x4, starting transfers between devices: 41 us -> 30.6 us  [exchange(): return lax.all_to_all(parts, axis, 0, 0, tiled=True)]
    all_to_all x4, waiting for transfers between devices: 32.3 us -> 41.9 us  [exchange(): return lax.all_to_all(parts, axis, 0, 0, tiled=True)]
    pallas_call x5 -> x6, Pallas kernels: 11.1 us -> 12.1 us  [call(): pl.pallas_call(kernel, out_shape=shapes, in_specs=vmem(len(args)), compil...]
  transfers between devices with their start and end apart: 15 -> 15, of which waited for: 6 -> 7; matrix products, arithmetic and copies ran while one was open for 2% -> 1% of each run, Pallas kernels for 4% -> 4%
where the time goes in v9:
time: 276 us; the launch traced here: 274 us
  blocking collectives  102 us (37%)
  starting transfers between devices  72.1 us (26%)
  waiting for transfers between devices  50 us (18%)
  Pallas kernels  42.1 us (15%)
  local copies, waits for them, and re-layouts  5.4 us (2%)
    all_to_all x7, blocking collectives, exchange(): return lax.all_to_all(parts, axis, 0, 0, tiled=True)  102 us
    all_to_all x4, waiting for transfers between devices, exchange(): return lax.all_to_all(parts, axis, 0, 0, tiled=True)  41.9 us
    all_to_all x4, starting transfers between devices, exchange(): return lax.all_to_all(parts, axis, 0, 0, tiled=True)  30.6 us
    ppermute x7, starting transfers between devices, swap(): return lax.ppermute(value, axis, [(0, 1), (1, 0)])  28.7 us
    pallas_call x2, Pallas kernels, keys_of(): pl.pallas_call(body, out_shape=shape, grid_spec=pltpu.PrefetchScalarGridS...  13 us
    pallas_call x6, Pallas kernels, call(): pl.pallas_call(kernel, out_shape=shapes, in_specs=vmem(len(args)), compil...  12.1 us
    ppermute x3, starting transfers between devices, shift(): lax.ppermute(value, axis, [(i, (i + by) % count) for i in range(count)])  10.8 us
    pallas_call x2, Pallas kernels, with_tokens(): pl.pallas_call(kernel, out_shape=shape, grid_spec=pltpu.PrefetchScalarGri...  6.91 us
  transfers between devices with their start and end apart: 15, of which 7 were waited for; matrix products, arithmetic and copies ran while one was open for 1% of the time, Pallas kernels for 4%

profile of v9, /device:TPU:1, one launch (start us, length us, event | category | flops | bytes accessed | tf_op | source)
XLA Modules:
  0.0 273.8 jit_solution(5202618126072718698)
XLA Ops:
  0.6 1.6 shard_map.77
  2.3 15.6 %all-to-all-start = ((bf16[8,32,256]{2,1,0:T(8,128)(2,1)}), bf16[8,32,256]{2,1,0:T(8,128)(2,1)S(1)}, u32[]{:S(2)}, u32[]{:S(2)}) async-start(bf16[8,32,256]{2,1,0:T(8,128)(2,1)} %get-tuple-element.21), calls=%async_computation | async-start | bytes 262144 | tf_op jit(solution)/shard_map/all_to_all | solution.py:311
  17.9 0.6 stack.33.idx.refs_0_
  18.5 4.6 %shard_map.76 = (bf16[2,128,2048]{2,1,0:T(8,128)(2,1)}, bf16[2,128,2048]{2,1,0:T(8,128)(2,1)}, bf16[2,128,2048]{2,1,0:T(8,128)(2,1)}, bf16[2,128,2048]{2,1,0:T(8,128)(2,1)}) custom-call(s32[6]{0:T(128)} %stack.33.idx.refs_0_, bf16[2,128,8192]{2,1,0:T(8,128)(2,1)} %bitcast.27), custom_call_target="tpu_custom_call" | custom-call | tf_op jit(solution)/shard_map/pallas_call | solution.py:224
  23.1 3.2 %collective-permute-start = (bf16[2,128,2048]{2,1,0:T(8,128)(2,1)}, bf16[2,128,2048]{2,1,0:T(8,128)(2,1)S(1)}, u32[]{:S(2)}, u32[]{:S(2)}) collective-permute-start(bf16[2,128,2048]{2,1,0:T(8,128)(2,1)} %get-tuple-element.18), channel_id=1, source_target_pairs={{0,16},{16,0},{1,17},{17,1},{2,18},{18,2},{3,19},{19,3},{4,20},{20... | collective-permute-start | bytes 3145736 | tf_op jit(solution)/shard_map/ppermute | solution.py:299
  26.3 4.8 %all-to-all-done = bf16[8,32,256]{2,1,0:T(8,128)(2,1)S(1)} async-done(((bf16[8,32,256]{2,1,0:T(8,128)(2,1)}), bf16[8,32,256]{2,1,0:T(8,128)(2,1)S(1)}, u32[]{:S(2)}, u32[]{:S(2)}) %all-to-all-start) | async-done | bytes 131104 | tf_op jit(solution)/shard_map/all_to_all | solution.py:311
  31.1 0.7 copy.11
  31.7 4.8 %collective-permute-start.3 = (bf16[32,2048]{1,0:T(8,128)(2,1)}, bf16[32,2048]{1,0:T(8,128)(2,1)}, u32[]{:S(2)}, u32[]{:S(2)}) collective-permute-start(bf16[32,2048]{1,0:T(8,128)(2,1)} %bitcast.25), channel_id=1, source_target_pairs={{0,64},{64,0},{1,65},{65,1},{2,66},{66,2},{3,67},{67,3},{4,68},{68... | collective-permute-start | bytes 393224 | tf_op jit(solution)/shard_map/ppermute | solution.py:299
  36.5 3.4 %collective-permute-start.1 = (bf16[2,128,2048]{2,1,0:T(8,128)(2,1)}, bf16[2,128,2048]{2,1,0:T(8,128)(2,1)S(1)}, u32[]{:S(2)}, u32[]{:S(2)}) collective-permute-start(bf16[2,128,2048]{2,1,0:T(8,128)(2,1)} %get-tuple-element.19), channel_id=1, source_target_pairs={{0,1},{1,0},{2,3},{3,2},{4,5},{5,4},{6,7},{7,6},{8,9},{9,8},{10,11... | collective-permute-start | bytes 3145736 | tf_op jit(solution)/shard_map/ppermute | solution.py:299
  39.9 2.0 collective-permute-start.2
  42.0 5.8 %all-to-all-start.1 = ((bf16[8,64,256]{2,1,0:T(8,128)(2,1)}), bf16[8,64,256]{2,1,0:T(8,128)(2,1)}, u32[]{:S(2)}, u32[]{:S(2)}) async-start(bf16[8,64,256]{2,1,0:T(8,128)(2,1)} %get-tuple-element.22), calls=%async_computation.1 | async-start | bytes 524288 | tf_op jit(solution)/shard_map/all_to_all | solution.py:311
  47.8 0.1 copy.9
  47.9 0.1 stack_reshape.3
  47.9 6.0 %collective-permute-done.3 = bf16[32,2048]{1,0:T(8,128)(2,1)} collective-permute-done((bf16[32,2048]{1,0:T(8,128)(2,1)}, bf16[32,2048]{1,0:T(8,128)(2,1)}, u32[]{:S(2)}, u32[]{:S(2)}) %collective-permute-start.3) | collective-permute-done | bytes 131104 | tf_op jit(solution)/shard_map/ppermute | solution.py:299
  54.0 0.9 pad_maximum_fusion.refs_5_
  54.9 0.0 copy-start.3
  54.9 4.4 %collective-permute-start.6 = (bf16[2,32,2048]{2,1,0:T(8,128)(2,1)S(1)}, bf16[2,32,2048]{2,1,0:T(8,128)(2,1)}, u32[]{:S(2)}, u32[]{:S(2)}) collective-permute-start(bf16[2,32,2048]{2,1,0:T(8,128)(2,1)S(1)} %pad_maximum_fusion.refs_5_), channel_id=1, source_target_pairs={{0,384},{128,0},{256,128},{384,256},{1,385},{129,1},{257,129},{385... | collective-permute-start | bytes 786440 | tf_op jit(solution)/shard_map/ppermute | solution.py:307
  59.3 1.9 collective-permute-start.4
  61.2 1.6 collective-permute-done.6.refs_8_
  62.9 4.5 %collective-permute-start.5 = (bf16[2,32,2048]{2,1,0:T(8,128)(2,1)S(1)}, bf16[2,32,2048]{2,1,0:T(8,128)(2,1)}, u32[]{:S(2)}, u32[]{:S(2)}) collective-permute-start(bf16[2,32,2048]{2,1,0:T(8,128)(2,1)S(1)} %pad_maximum_fusion.refs_5_), channel_id=1, source_target_pairs={{0,256},{128,384},{256,0},{384,128},{1,257},{129,385},{257,1},{385... | collective-permute-start | bytes 786440 | tf_op jit(solution)/shard_map/ppermute | solution.py:307
  67.3 0.4 collective-permute-done.4.refs_6_
  67.8 11.0 %collective-permute-start.7 = (bf16[2,32,2048]{2,1,0:T(8,128)(2,1)S(1)}, bf16[2,32,2048]{2,1,0:T(8,128)(2,1)S(1)}, u32[]{:S(2)}, u32[]{:S(2)}) collective-permute-start(bf16[2,32,2048]{2,1,0:T(8,128)(2,1)S(1)} %pad_maximum_fusion.refs_5_), channel_id=1, source_target_pairs={{0,32},{32,0},{1,33},{33,1},{2,34},{34,2},{3,35},{35,3},{4,36},{36... | collective-permute-start | bytes 786440 | tf_op jit(solution)/shard_map/ppermute | solution.py:299
  78.8 0.0 collective-permute-done.5.refs_7_
  78.8 1.9 collective-permute-start.10
  80.7 0.0 collective-permute-done.7.refs_9_
  80.8 0.0 copy-start.6
  80.8 2.4 collective-permute-start.8
  83.2 0.0 collective-permute-done.refs_2_.refs_3_.refs_4_
  83.2 0.0 copy-done.6
  83.2 0.0 copy-start
  83.2 1.9 collective-permute-start.9
  85.1 11.7 %all-to-all-done.1.refs_14_ = bf16[8,64,256]{2,1,0:T(8,128)(2,1)} async-done(((bf16[8,64,256]{2,1,0:T(8,128)(2,1)}), bf16[8,64,256]{2,1,0:T(8,128)(2,1)}, u32[]{:S(2)}, u32[]{:S(2)}) %all-to-all-start.1) | async-done | bytes 262176 | tf_op jit(solution)/shard_map/all_to_all | solution.py:311
  96.8 0.0 collective-permute-done.1.refs_3_.refs_4_.refs_5_
  96.8 0.0 collective-permute-done.2.refs_4_.refs_5_.refs_6_
  96.9 0.0 collective-permute-done.10.refs_12_
  96.9 0.0 collective-permute-done.8.refs_10_
  96.9 0.0 collective-permute-done.9.refs_11_
  96.9 0.9 copy-done.1
  97.8 0.3 copy-done.2
  98.2 6.9 %shard_map.79 = bf16[4,160,512]{2,1,0:T(8,128)(2,1)} custom-call(s32[6]{0:T(128)} %stack.33.idx.refs_0_, bf16[2,128,2048]{2,1,0:T(8,128)(2,1)} %get-tuple-element.17.refs_1_.refs_2_.refs_3_, bf16[2,128,2048]{2,1,0:T(8,128)(2,1)} %copy-done, bf16[2,128,2048]{2,1,0:T(8,128)(2,1)} %copy-done.1, bf16[2,128,2048]{2,1,0:T(8,128)(2,1)} %copy-done.2, ...), custom_call_target="tpu_custom_call" | custom-call | tf_op jit(solution)/shard_map/pallas_call | solution.py:259
  105.0 10.9 %all_to_all.55.refs_0_ = bf16[4,160,512]{2,1,0:T(8,128)(2,1)} all-to-all(bf16[4,160,512]{2,1,0:T(8,128)(2,1)} %shard_map.79), channel_id=1, replica_groups=mesh['x'=4,'yh'=2,'c'=2,'yl'=2,'zh'=8,'zl'=2] {'yl','zl'}, dimensions={0} | all-to-all | bytes 1310720 | tf_op jit(solution)/shard_map/all_to_all | solution.py:311
  115.9 2.4 shard_map.80
  118.4 8.5 %all_to_all.56.refs_1_ = bf16[4,48,512]{2,1,0:T(8,128)(2,1)} all-to-all(bf16[4,48,512]{2,1,0:T(8,128)(2,1)} %shard_map.80), channel_id=1, replica_groups=mesh['x'=4,'yh'=2,'c'=2,'yl'=2,'zh'=8,'zl'=2] {'yl','zl'}, dimensions={0} | all-to-all | bytes 393216 | tf_op jit(solution)/shard_map/all_to_all | solution.py:311
  126.8 3.4 %shard_map.81 = bf16[8,72,256]{2,1,0:T(8,128)(2,1)} custom-call(s32[6]{0:T(128)} %stack.33.idx.refs_0_, bf16[4,48,512]{2,1,0:T(8,128)(2,1)} %all_to_all.56.refs_1_, bf16[2,128,2048]{2,1,0:T(8,128)(2,1)} %get-tuple-element.17.refs_1_.refs_2_.refs_3_, bf16[2,128,2048]{2,1,0:T(8,128)(2,1)} %copy-done, bf16[2,128,2048]{2,1,0:T(8,128)(2,1)} %copy-done.1, ...), custom_call_target="tpu_custom_call" | custom-call | tf_op jit(solution)/shard_map/pallas_call | solution.py:239
  130.2 5.7 %all-to-all-start.4 = ((bf16[8,72,256]{2,1,0:T(8,128)(2,1)}), bf16[8,72,256]{2,1,0:T(8,128)(2,1)S(1)}, u32[]{:S(2)}, u32[]{:S(2)}) async-start(bf16[8,72,256]{2,1,0:T(8,128)(2,1)} %shard_map.81), calls=%async_computation.4 | async-start | bytes 589824 | tf_op jit(solution)/shard_map/all_to_all | solution.py:311
  136.0 1.3 dynamic-slice_bitcast_fusion.refs_2_
  137.3 15.3 %all-to-all-done.4.refs_0_ = bf16[8,72,256]{2,1,0:T(8,128)(2,1)S(1)} async-done(((bf16[8,72,256]{2,1,0:T(8,128)(2,1)}), bf16[8,72,256]{2,1,0:T(8,128)(2,1)S(1)}, u32[]{:S(2)}, u32[]{:S(2)}) %all-to-all-start.4) | async-done | bytes 294944 | tf_op jit(solution)/shard_map/all_to_all | solution.py:311
  152.5 0.7 copy-done.5
  153.3 1.8 shard_map.82
  155.1 3.4 %all-to-all-start.5 = ((bf16[8,72,256]{2,1,0:T(8,128)(2,1)}), bf16[8,72,256]{2,1,0:T(8,128)(2,1)S(1)}, u32[]{:S(2)}, u32[]{:S(2)}) async-start(bf16[8,72,256]{2,1,0:T(8,128)(2,1)} %get-tuple-element.23), calls=%async_computation.5 | async-start | bytes 589824 | tf_op jit(solution)/shard_map/all_to_all | solution.py:311
  158.5 6.1 %shard_map.78.refs_1_ = bf16[4,192,512]{2,1,0:T(8,128)(2,1)} custom-call(s32[6]{0:T(128)} %stack.33.idx.refs_0_, bf16[2,128,2048]{2,1,0:T(8,128)(2,1)} %get-tuple-element.17.refs_1_.refs_2_.refs_3_, bf16[2,128,2048]{2,1,0:T(8,128)(2,1)} %copy-done, bf16[2,128,2048]{2,1,0:T(8,128)(2,1)} %copy-done.1, bf16[2,128,2048]{2,1,0:T(8,128)(2,1)} %copy-done.2, ...), custom_call_target="tpu_custom_call" | custom-call | tf_op jit(solution)/shard_map/pallas_call | solution.py:259
  164.6 10.1 %all-to-all-done.5.refs_2_ = bf16[8,72,256]{2,1,0:T(8,128)(2,1)S(1)} async-done(((bf16[8,72,256]{2,1,0:T(8,128)(2,1)}), bf16[8,72,256]{2,1,0:T(8,128)(2,1)S(1)}, u32[]{:S(2)}, u32[]{:S(2)}) %all-to-all-start.5) | async-done | bytes 294944 | tf_op jit(solution)/shard_map/all_to_all | solution.py:311
  174.7 0.7 copy-done.4
  175.5 3.8 %shard_map.83 = bf16[4,192,512]{2,1,0:T(8,128)(2,1)} custom-call(s32[6]{0:T(128)} %stack.33.idx.refs_0_, bf16[4,192,512]{2,1,0:T(8,128)(2,1)} %shard_map.78.refs_1_, bf16[8,72,256]{2,1,0:T(8,128)(2,1)} %copy-done.4, bf16[2,128,2048]{2,1,0:T(8,128)(2,1)} %get-tuple-element.17.refs_1_.refs_2_.refs_3_, ...), custom_call_target="tpu_custom_call", output_to_operand_aliasing={{}: (1, {})} | custom-call | tf_op jit(solution)/shard_map/pallas_call | solution.py:282
  179.2 11.7 %all_to_all.57.refs_0_ = bf16[4,192,512]{2,1,0:T(8,128)(2,1)} all-to-all(bf16[4,192,512]{2,1,0:T(8,128)(2,1)} %shard_map.83), channel_id=1, replica_groups=mesh['x'=4,'yh'=2,'c'=2,'yl'=2,'zh'=8,'zl'=2] {'yl','zl'}, dimensions={0} | all-to-all | bytes 1572864 | tf_op jit(solution)/shard_map/all_to_all | solution.py:311
  190.9 2.5 shard_map.84
  193.4 9.3 %all_to_all.58.refs_1_ = bf16[4,48,512]{2,1,0:T(8,128)(2,1)} all-to-all(bf16[4,48,512]{2,1,0:T(8,128)(2,1)} %get-tuple-element.24), channel_id=1, replica_groups=mesh['x'=4,'yh'=2,'c'=2,'yl'=2,'zh'=8,'zl'=2] {'yl','zl'}, dimensions={0} | all-to-all | bytes 393216 | tf_op jit(solution)/shard_map/all_to_all | solution.py:311
  202.7 3.5 %shard_map.85 = bf16[8,96,256]{2,1,0:T(8,128)(2,1)} custom-call(s32[6]{0:T(128)} %stack.33.idx.refs_0_, bf16[4,48,512]{2,1,0:T(8,128)(2,1)} %all_to_all.58.refs_1_, bf16[2,128,2048]{2,1,0:T(8,128)(2,1)} %get-tuple-element.17.refs_1_.refs_2_.refs_3_, bf16[2,128,2048]{2,1,0:T(8,128)(2,1)} %copy-done, bf16[2,128,2048]{2,1,0:T(8,128)(2,1)} %copy-done.1, ...), custom_call_target="tpu_custom_call" | custom-call | tf_op jit(solution)/shard_map/pallas_call | solution.py:239
  206.2 22.9 %all_to_all.59.refs_1_ = bf16[8,96,256]{2,1,0:T(8,128)(2,1)} all-to-all(bf16[8,96,256]{2,1,0:T(8,128)(2,1)} %shard_map.85), channel_id=1, replica_groups=mesh['x'=4,'yh'=2,'c'=2,'yl'=2,'zh'=8,'zl'=2] {'zh'}, dimensions={0} | all-to-all | bytes 786432 | tf_op jit(solution)/shard_map/all_to_all | solution.py:311
  229.1 1.8 shard_map.86
  230.9 8.3 %all_to_all.60.quarters = f32[4,16,512]{2,1,0:T(8,128)} all-to-all(f32[4,16,512]{2,1,0:T(8,128)} %get-tuple-element.28), channel_id=1, replica_groups=mesh['x'=4,'yh'=2,'c'=2,'yl'=2,'zh'=8,'zl'=2] {'yl','zl'}, dimensions={0} | all-to-all | bytes 262144 | tf_op jit(solution)/shard_map/all_to_all | solution.py:311
  239.2 2.1 shard_map.87
  241.3 30.8 %all_to_all.61.parts = bf16[16,32,256]{2,1,0:T(8,128)(2,1)} all-to-all(bf16[16,32,256]{2,1,0:T(8,128)(2,1)} %bitcast.37), channel_id=1, replica_groups=mesh['x'=4,'yh'=2,'c'=2,'yl'=2,'zh'=8,'zl'=2] {'x','yh','c'}, dimensions={0} | all-to-all | bytes 524288 | tf_op jit(solution)/shard_map/all_to_all | solution.py:311
  272.2 1.6 shard_map.88
  (6 shorter events, 0.0 us)
Async XLA Ops:
  2.3 28.8 %all-to-all-start = ((bf16[8,32,256]{2,1,0:T(8,128)(2,1)}), bf16[8,32,256]{2,1,0:T(8,128)(2,1)S(1)}, u32[]{:S(2)}, u32[]{:S(2)}) async-start(bf16[8,32,256]{2,1,0:T(8,128)(2,1)} %get-tuple-element.21), calls=%async_computation | async-start | bytes 262144 | tf_op jit(solution)/shard_map/all_to_all | solution.py:311
  23.1 60.1 %collective-permute-start = (bf16[2,128,2048]{2,1,0:T(8,128)(2,1)}, bf16[2,128,2048]{2,1,0:T(8,128)(2,1)S(1)}, u32[]{:S(2)}, u32[]{:S(2)}) collective-permute-start(bf16[2,128,2048]{2,1,0:T(8,128)(2,1)} %get-tuple-element.18), channel_id=1, source_target_pairs={{0,16},{16,0},{1,17},{17,1},{2,18},{18,2},{3,19},{19,3},{4,20},{20... | collective-permute-start | bytes 3145736 | tf_op jit(solution)/shard_map/ppermute | solution.py:299
  31.7 22.3 %collective-permute-start.3 = (bf16[32,2048]{1,0:T(8,128)(2,1)}, bf16[32,2048]{1,0:T(8,128)(2,1)}, u32[]{:S(2)}, u32[]{:S(2)}) collective-permute-start(bf16[32,2048]{1,0:T(8,128)(2,1)} %bitcast.25), channel_id=1, source_target_pairs={{0,64},{64,0},{1,65},{65,1},{2,66},{66,2},{3,67},{67,3},{4,68},{68... | collective-permute-start | bytes 393224 | tf_op jit(solution)/shard_map/ppermute | solution.py:299
  36.5 60.3 %collective-permute-start.1 = (bf16[2,128,2048]{2,1,0:T(8,128)(2,1)}, bf16[2,128,2048]{2,1,0:T(8,128)(2,1)S(1)}, u32[]{:S(2)}, u32[]{:S(2)}) collective-permute-start(bf16[2,128,2048]{2,1,0:T(8,128)(2,1)} %get-tuple-element.19), channel_id=1, source_target_pairs={{0,1},{1,0},{2,3},{3,2},{4,5},{5,4},{6,7},{7,6},{8,9},{9,8},{10,11... | collective-permute-start | bytes 3145736 | tf_op jit(solution)/shard_map/ppermute | solution.py:299
  39.9 56.9 %collective-permute-start.2 = (bf16[2,128,2048]{2,1,0:T(8,128)(2,1)}, bf16[2,128,2048]{2,1,0:T(8,128)(2,1)S(1)}, u32[]{:S(2)}, u32[]{:S(2)}) collective-permute-start(bf16[2,128,2048]{2,1,0:T(8,128)(2,1)} %get-tuple-element.20), channel_id=1, source_target_pairs={{0,17},{1,16},{16,1},{17,0},{2,19},{3,18},{18,3},{19,2},{4,21},{5,... | collective-permute-start | bytes 3145736 | tf_op jit(solution)/shard_map/ppermute | solution.py:303
  42.0 54.9 %all-to-all-start.1 = ((bf16[8,64,256]{2,1,0:T(8,128)(2,1)}), bf16[8,64,256]{2,1,0:T(8,128)(2,1)}, u32[]{:S(2)}, u32[]{:S(2)}) async-start(bf16[8,64,256]{2,1,0:T(8,128)(2,1)} %get-tuple-element.22), calls=%async_computation.1 | async-start | bytes 524288 | tf_op jit(solution)/shard_map/all_to_all | solution.py:311
  54.9 42.0 %copy-start.3 = (bf16[2,32,2048]{2,1,0:T(8,128)(2,1)}, bf16[2,32,2048]{2,1,0:T(8,128)(2,1)S(1)}, u32[]{:S(2)}) copy-start(bf16[2,32,2048]{2,1,0:T(8,128)(2,1)S(1)} %pad_maximum_fusion.refs_5_) | copy-start | bytes 786436
  54.9 7.9 %collective-permute-start.6 = (bf16[2,32,2048]{2,1,0:T(8,128)(2,1)S(1)}, bf16[2,32,2048]{2,1,0:T(8,128)(2,1)}, u32[]{:S(2)}, u32[]{:S(2)}) collective-permute-start(bf16[2,32,2048]{2,1,0:T(8,128)(2,1)S(1)} %pad_maximum_fusion.refs_5_), channel_id=1, source_target_pairs={{0,384},{128,0},{256,128},{384,256},{1,385},{129,1},{257,129},{385... | collective-permute-start | bytes 786440 | tf_op jit(solution)/shard_map/ppermute | solution.py:307
  59.3 8.4 %collective-permute-start.4 = (bf16[2,32,2048]{2,1,0:T(8,128)(2,1)S(1)}, bf16[2,32,2048]{2,1,0:T(8,128)(2,1)}, u32[]{:S(2)}, u32[]{:S(2)}) collective-permute-start(bf16[2,32,2048]{2,1,0:T(8,128)(2,1)S(1)} %pad_maximum_fusion.refs_5_), channel_id=1, source_target_pairs={{0,128},{128,256},{256,384},{384,0},{1,129},{129,257},{257,385},{3... | collective-permute-start | bytes 786440 | tf_op jit(solution)/shard_map/ppermute | solution.py:307
  62.9 16.0 %collective-permute-start.5 = (bf16[2,32,2048]{2,1,0:T(8,128)(2,1)S(1)}, bf16[2,32,2048]{2,1,0:T(8,128)(2,1)}, u32[]{:S(2)}, u32[]{:S(2)}) collective-permute-start(bf16[2,32,2048]{2,1,0:T(8,128)(2,1)S(1)} %pad_maximum_fusion.refs_5_), channel_id=1, source_target_pairs={{0,256},{128,384},{256,0},{384,128},{1,257},{129,385},{257,1},{385... | collective-permute-start | bytes 786440 | tf_op jit(solution)/shard_map/ppermute | solution.py:307
  67.8 13.0 %collective-permute-start.7 = (bf16[2,32,2048]{2,1,0:T(8,128)(2,1)S(1)}, bf16[2,32,2048]{2,1,0:T(8,128)(2,1)S(1)}, u32[]{:S(2)}, u32[]{:S(2)}) collective-permute-start(bf16[2,32,2048]{2,1,0:T(8,128)(2,1)S(1)} %pad_maximum_fusion.refs_5_), channel_id=1, source_target_pairs={{0,32},{32,0},{1,33},{33,1},{2,34},{34,2},{3,35},{35,3},{4,36},{36... | collective-permute-start | bytes 786440 | tf_op jit(solution)/shard_map/ppermute | solution.py:299
  78.8 18.0 %collective-permute-start.10 = (bf16[2,32,2048]{2,1,0:T(8,128)(2,1)}, bf16[2,32,2048]{2,1,0:T(8,128)(2,1)}, u32[]{:S(2)}, u32[]{:S(2)}) collective-permute-start(bf16[2,32,2048]{2,1,0:T(8,128)(2,1)} %collective-permute-done.6.refs_8_), channel_id=1, source_target_pairs={{0,32},{32,0},{1,33},{33,1},{2,34},{34,2},{3,35},{35,3},{4,36},{36... | collective-permute-start | bytes 786440 | tf_op jit(solution)/shard_map/ppermute | solution.py:299
  80.8 2.4 copy-start.6
  80.8 16.1 %collective-permute-start.8 = (bf16[2,32,2048]{2,1,0:T(8,128)(2,1)}, bf16[2,32,2048]{2,1,0:T(8,128)(2,1)}, u32[]{:S(2)}, u32[]{:S(2)}) collective-permute-start(bf16[2,32,2048]{2,1,0:T(8,128)(2,1)} %collective-permute-done.4.refs_6_), channel_id=1, source_target_pairs={{0,32},{32,0},{1,33},{33,1},{2,34},{34,2},{3,35},{35,3},{4,36},{36... | collective-permute-start | bytes 786440 | tf_op jit(solution)/shard_map/ppermute | solution.py:299
  83.2 13.7 %copy-start = (bf16[2,128,2048]{2,1,0:T(8,128)(2,1)}, bf16[2,128,2048]{2,1,0:T(8,128)(2,1)S(1)}, u32[]{:S(2)}) copy-start(bf16[2,128,2048]{2,1,0:T(8,128)(2,1)S(1)} %collective-permute-done.refs_2_.refs_3_.refs_4_) | copy-start | bytes 3145732
  83.2 13.7 %collective-permute-start.9 = (bf16[2,32,2048]{2,1,0:T(8,128)(2,1)}, bf16[2,32,2048]{2,1,0:T(8,128)(2,1)}, u32[]{:S(2)}, u32[]{:S(2)}) collective-permute-start(bf16[2,32,2048]{2,1,0:T(8,128)(2,1)} %collective-permute-done.5.refs_7_), channel_id=1, source_target_pairs={{0,32},{32,0},{1,33},{33,1},{2,34},{34,2},{3,35},{35,3},{4,36},{36... | collective-permute-start | bytes 786440 | tf_op jit(solution)/shard_map/ppermute | solution.py:299
  96.8 1.0 copy-start.1
  96.9 1.3 copy-start.2
  130.2 22.3 %all-to-all-start.4 = ((bf16[8,72,256]{2,1,0:T(8,128)(2,1)}), bf16[8,72,256]{2,1,0:T(8,128)(2,1)S(1)}, u32[]{:S(2)}, u32[]{:S(2)}) async-start(bf16[8,72,256]{2,1,0:T(8,128)(2,1)} %shard_map.81), calls=%async_computation.4 | async-start | bytes 589824 | tf_op jit(solution)/shard_map/all_to_all | solution.py:311
  152.5 0.7 copy-start.5
  155.1 19.7 %all-to-all-start.5 = ((bf16[8,72,256]{2,1,0:T(8,128)(2,1)}), bf16[8,72,256]{2,1,0:T(8,128)(2,1)S(1)}, u32[]{:S(2)}, u32[]{:S(2)}) async-start(bf16[8,72,256]{2,1,0:T(8,128)(2,1)} %get-tuple-element.23), calls=%async_computation.5 | async-start | bytes 589824 | tf_op jit(solution)/shard_map/all_to_all | solution.py:311
  174.7 0.7 copy-start.4
